TPU v7x, 256 devices: a whole 4x4x8 slice. The times are simulated.
256 devices in a mesh: wide: 16 (over y_hi, x, core), narrow: 16 (over z, y_lo).
Axes of the slice: x: 4, y: 4 (y_hi: 2, y_lo: 2; y = y_hi * 2 + y_lo), z: 8, core: 2. Of those that a mesh axis runs over, the one named last changes fastest.
Arguments:
- documents: bfloat16 [16384, 768], P('wide'), may hold values from -8 to 8
- label_weight: bfloat16 [32768, 768], P(('wide', 'narrow')), may hold values from -1 to 1
- sample_ids: int32 [32768], P(('wide', 'narrow')), may hold values from 0 to 2812280, as said below
- positive_cols: int32 [16384, 4], P('wide'), may hold values from 0 to 32767
- up_weight: bfloat16 [768, 3072], P(None, 'narrow'), may hold values from -0.21875 to 0.21875
- down_weight: bfloat16 [3072, 768], P('narrow'), may hold values from -0.109375 to 0.109375
Outputs:
- label_grad: float32 [32768, 768], P(('wide', 'narrow'))
- up_grad: float32 [768, 3072], P('wide', 'narrow')
- down_grad: float32 [3072, 768], P('narrow', 'wide')
Inputs may be any that keep to these rules, and one draw needn't show every extreme that they name: `sample_ids`: frequency ranks (0 is the most frequent of 2812281 labels), not falling along the sampled columns; frequent ranks repeat.
All inputs are finite; a program needn't handle non-finite values.
Results may differ from a plain program's by a relative error of at most 0.01.
Values may be sent and summed in bfloat16 or wider, within the bound.
No kernel may reach another device: no remote copies, remote signals or barrier semaphores. Data moves between devices by JAX's collectives and lax.ppermute only.
A program may use at most 64 MiB of HBM per device.

v0:
```python
from functools import partial

import jax
import jax.numpy as jnp
import numpy as np
from jax import lax
from jax.experimental import pallas as pl
from jax.experimental.pallas import tpu as pltpu
from jax.sharding import Mesh
from jax.sharding import PartitionSpec as P


CATALOG = 2812281
BF16, F32, I32 = jnp.bfloat16, jnp.float32, jnp.int32
D = 768
LAB = 128
EXTRA = 8
BLK = LAB + EXTRA
NB = 32
GRP = 4
TILE = GRP * LAB
STEPS = NB // GRP
DOCS = 512
REL = (0, -1, 1, 2)
NT = (((1,), (1,)), ((), ()))
TN = (((0,), (0,)), ((), ()))


def move(block, axes, size, distance):
    return lax.ppermute(block, axes, [(i, (i + distance) % size) for i in range(size)])


def add(a, b):
    return a.astype(F32) + b.astype(F32)


def total(parts):
    result = parts[0].astype(F32)
    for j in range(1, parts.shape[0]):
        result = result + parts[j].astype(F32)
    return result


def rounded(values):
    return lax.reduce_precision(values, 8, 7)


def log_expected(rank_ids, sampled):
    rank_float = rank_ids.astype(F32)
    return (
        jnp.log(F32(sampled))
        + jnp.log(jnp.log1p(1.0 / (rank_float + 1.0)))
        - jnp.log(jnp.log(F32(CATALOG) + 1.0))
    )


def fetch_labels(label_refs, rows, extras, sems):
    copies = []
    for g in range(STEPS):
        side, dx = g // 4, g % 4
        if dx < 3:
            sources = [(label_refs[side * 5 + dx], 0, GRP)]
        else:
            half = GRP // 2
            sources = [(label_refs[side * 5 + 3], 0, half), (label_refs[side * 5 + 4], half, half)]
        for n, (ref, at, size) in enumerate(sources):
            span = pl.ds(at, size)
            copies.append(
                (g, pltpu.make_async_copy(ref.at[:, pl.ds(0, LAB), :], rows.at[g, span], sems.at[g, 2 * n]))
            )
            if extras is not None:
                copies.append(
                    (
                        g,
                        pltpu.make_async_copy(
                            ref.at[:, pl.ds(LAB, EXTRA), pl.ds(0, LAB)],
                            extras.at[g, span],
                            sems.at[g, 2 * n + 1],
                        ),
                    )
                )
    return copies


def start_and_wait(copies):
    step = pl.program_id(0)

    @pl.when(step == 0)
    def _():
        for _, copy in copies:
            copy.start()

    for g in range(STEPS):

        @pl.when(step == g)
        def _():
            for at, copy in copies:
                if at == g:
                    copy.wait()


def first_kernel(*refs):
    label_refs = refs[:10]
    emb_ref, exp_ref, top_ref, stat_ref, rows, extras, sems, raw_a, raw_b, bias_a, bias_b, run_max, run_sum = refs[10:]
    step = pl.program_id(0)
    start_and_wait(fetch_labels(label_refs, rows, extras, sems))
    group = jnp.minimum(step, STEPS - 1)

    def body(raw_out, bias_out, raw_in, bias_in):
        lhs = rows[group].reshape(TILE, D)
        raw_out[...] = lax.dot_general(lhs, emb_ref[...], NT, preferred_element_type=F32)
        for j in range(GRP):
            pieces = extras[group, j].astype(F32)
            row = pieces[0:1] + pieces[1:2] + pieces[2:3]
            bias_out[j * LAB : (j + 1) * LAB, :] = jnp.broadcast_to(row, (LAB, LAB)).T
        for h in range(DOCS // LAB):
            cols = slice(h * LAB, (h + 1) * LAB)
            logits = raw_in[:, cols] - bias_in[...]
            old = run_max[:, cols]
            new = jnp.maximum(old, jnp.max(logits, axis=0, keepdims=True))
            exps = jnp.exp(logits - new)
            exp_ref[:, cols] = exps
            run_sum[:, cols] = run_sum[:, cols] * jnp.exp(old - new) + jnp.sum(exps, axis=0, keepdims=True)
            run_max[:, cols] = new

    @pl.when(lax.rem(step, 2) == 0)
    def _():
        body(raw_a, bias_a, raw_b, bias_b)

    @pl.when(lax.rem(step, 2) == 1)
    def _():
        body(raw_b, bias_b, raw_a, bias_a)

    @pl.when(step == 0)
    def _():
        run_max[...] = jnp.full_like(run_max, -jnp.inf)
        run_sum[...] = jnp.zeros_like(run_sum)

    top_ref[0] = run_max[...]

    @pl.when(step == STEPS)
    def _():
        for j in range(4):
            stat_ref[j : j + 1, :] = run_max[:, j * 128 : (j + 1) * 128]
            stat_ref[4 + j : 5 + j, :] = run_sum[:, j * 128 : (j + 1) * 128]


def second_kernel(base_ref, *refs):
    label_refs = refs[:10]
    exp_ref, top_ref, total_ref, pos_ref, grad_ref, out_ref, rows, sems, grad_a, grad_b, acc = refs[10:]
    step = pl.program_id(0)
    start_and_wait(fetch_labels(label_refs, rows, None, sems))
    group = jnp.minimum(step, STEPS - 1)
    before = jnp.maximum(step - 1, 0)

    def body(grad_out, grad_in):
        scale = jnp.exp(top_ref[0] - total_ref[...])
        pos = [pos_ref[k : k + 1, :] for k in range(4)]
        weights = []
        for k in range(4):
            same = [jnp.where(pos[k] == pos[n], F32(0.25), F32(0.0)) for n in range(4)]
            weights.append(same[0] + same[1] + same[2] + same[3])
        for j in range(GRP):
            span = slice(j * LAB, (j + 1) * LAB)
            base = base_ref[group * GRP + j]
            for h in range(DOCS // LAB):
                cols = slice(h * LAB, (h + 1) * LAB)
                ids = lax.broadcasted_iota(I32, (LAB, LAB), 0)
                hits = jnp.zeros((LAB, LAB), F32)
                for k in (3, 2, 1, 0):
                    hits = jnp.where(pos[k][:, cols] - base == ids, weights[k][:, cols], hits)
                grads = (exp_ref[span, cols] * scale[:, cols] - hits).astype(BF16)
                grad_ref[0, span, cols] = grads
                grad_out[span, cols] = grads
        acc[...] += lax.dot_general(
            grad_in[...], rows[before].reshape(TILE, D), TN, preferred_element_type=F32
        )

    @pl.when(lax.rem(step, 2) == 0)
    def _():
        body(grad_a, grad_b)

    @pl.when(lax.rem(step, 2) == 1)
    def _():
        body(grad_b, grad_a)

    @pl.when(step == 0)
    def _():
        acc[...] = jnp.zeros_like(acc)

    @pl.when(step == STEPS)
    def _():
        out_ref[...] = acc[...].astype(BF16)


def label_specs():
    return [pl.BlockSpec(memory_space=pl.ANY)] * 10


def behind(step, *_):
    return (jnp.maximum(step - 1, 0), 0)


def first_pass(labels, embedding):
    return pl.pallas_call(
        first_kernel,
        out_shape=(
            jax.ShapeDtypeStruct((NB * LAB, DOCS), F32),
            jax.ShapeDtypeStruct((STEPS, 1, DOCS), F32),
            jax.ShapeDtypeStruct((8, 128), F32),
        ),
        grid=(STEPS + 1,),
        in_specs=label_specs() + [pl.BlockSpec((DOCS, D), lambda s: (0, 0))],
        out_specs=(
            pl.BlockSpec((TILE, DOCS), behind),
            pl.BlockSpec((1, 1, DOCS), lambda s: (jnp.maximum(s - 1, 0), 0, 0)),
            pl.BlockSpec((8, 128), lambda s: (0, 0)),
        ),
        scratch_shapes=[
            pltpu.VMEM((STEPS, GRP, LAB, D), BF16),
            pltpu.VMEM((STEPS, GRP, EXTRA, LAB), BF16),
            pltpu.SemaphoreType.DMA((STEPS, 4)),
            pltpu.VMEM((TILE, DOCS), F32),
            pltpu.VMEM((TILE, DOCS), F32),
            pltpu.VMEM((TILE, LAB), F32),
            pltpu.VMEM((TILE, LAB), F32),
            pltpu.VMEM((1, DOCS), F32),
            pltpu.VMEM((1, DOCS), F32),
        ],
        compiler_params=pltpu.CompilerParams(
            dimension_semantics=("arbitrary",), vmem_limit_bytes=32 << 20
        ),
        cost_estimate=pl.CostEstimate(
            flops=2 * NB * LAB * DOCS * D, bytes_accessed=16 << 20, transcendentals=NB * LAB * DOCS
        ),
        name="first_pass",
    )(*labels, embedding)


def second_pass(bases, labels, exps, tops, log_total, positives):
    last = STEPS - 1
    return pl.pallas_call(
        second_kernel,
        out_shape=(
            jax.ShapeDtypeStruct((STEPS, TILE, DOCS), BF16),
            jax.ShapeDtypeStruct((DOCS, D), BF16),
        ),
        grid_spec=pltpu.PrefetchScalarGridSpec(
            num_scalar_prefetch=1,
            grid=(STEPS + 1,),
            in_specs=label_specs()
            + [
                pl.BlockSpec((TILE, DOCS), lambda s, b: (jnp.minimum(s, last), 0)),
                pl.BlockSpec((1, 1, DOCS), lambda s, b: (jnp.minimum(s, last), 0, 0)),
                pl.BlockSpec((1, DOCS), lambda s, b: (0, 0)),
                pl.BlockSpec((4, DOCS), lambda s, b: (0, 0)),
            ],
            out_specs=(
                pl.BlockSpec((1, TILE, DOCS), lambda s, b: (jnp.minimum(s, last), 0, 0)),
                pl.BlockSpec((DOCS, D), lambda s, b: (0, 0)),
            ),
            scratch_shapes=[
                pltpu.VMEM((STEPS, GRP, LAB, D), BF16),
                pltpu.SemaphoreType.DMA((STEPS, 4)),
                pltpu.VMEM((TILE, DOCS), BF16),
                pltpu.VMEM((TILE, DOCS), BF16),
                pltpu.VMEM((DOCS, D), F32),
            ],
        ),
        compiler_params=pltpu.CompilerParams(
            dimension_semantics=("arbitrary",), vmem_limit_bytes=32 << 20
        ),
        cost_estimate=pl.CostEstimate(
            flops=2 * NB * LAB * DOCS * D, bytes_accessed=20 << 20, transcendentals=0
        ),
        name="second_pass",
    )(bases, *labels, exps, tops, log_total, positives)


def spread(chunks):
    return lax.all_to_all(chunks, "z", 0, 0)


def everywhere(block):
    return spread(jnp.broadcast_to(block[None], (8,) + block.shape))


def step_of(documents, label_weight, sample_ids, positive_cols, up_weight, down_weight):
    yh, yl = lax.axis_index("yh"), lax.axis_index("yl")
    x, core, z = lax.axis_index("x"), lax.axis_index("core"), lax.axis_index("z")
    plane_y = ("yh", "yl")
    units = down_weight.shape[0]

    log_expect = log_expected(sample_ids, label_weight.shape[0] * 256)
    piece_a = rounded(log_expect)
    piece_b = rounded(log_expect - piece_a)
    piece_c = log_expect - piece_a - piece_b
    pieces = jnp.stack([piece_a, piece_b, piece_c]).astype(BF16)
    pieces = jnp.pad(pieces, ((0, EXTRA - 3), (0, D - LAB)))
    block = jnp.concatenate([label_weight, pieces], axis=0)
    y_low = move(block, plane_y, 4, 1)
    y_high = move(block, plane_y, 4, -1)
    y_far_a = move(y_low[:64], plane_y, 4, 1)
    y_far_b = move(y_high[64:], plane_y, 4, -1)
    column = jnp.concatenate([block, y_low, y_high, y_far_a, y_far_b], axis=0)
    x_low = move(column, "x", 4, 1)
    x_high = move(column, "x", 4, -1)
    c_column = move(column, "core", 2, 1)

    up_rows = up_weight.T
    mine = jnp.where(core == 0, up_rows, down_weight)
    got = move(mine, "yl", 2, 1)
    got_other = move(got, "core", 2, 1)
    up_far = jnp.where(core == 0, got, got_other)
    down_far = jnp.where(core == 0, got_other, got)
    up_all = jnp.concatenate([jnp.where(yl == 0, up_rows, up_far), jnp.where(yl == 0, up_far, up_rows)], axis=0)
    down_all = jnp.concatenate(
        [jnp.where(yl == 0, down_weight, down_far), jnp.where(yl == 0, down_far, down_weight)], axis=0
    )

    docs = lax.dynamic_slice_in_dim(documents, yl * DOCS, DOCS, 0)
    pre_act = lax.dot_general(docs, up_all, NT, preferred_element_type=F32)
    hidden = jax.nn.gelu(pre_act, approximate=False).astype(BF16)
    partial_out = jnp.dot(hidden, down_all, preferred_element_type=F32).astype(BF16)
    parts = spread(partial_out.reshape(8, DOCS // 8, D))
    parts, x_low, x_high = lax.optimization_barrier((parts, x_low, x_high))
    own_docs = lax.dynamic_slice_in_dim(docs, z * (DOCS // 8), DOCS // 8, 0)
    own_emb = (own_docs.astype(F32) + total(parts)).astype(BF16)
    x_far_a = move(x_low[: 2 * BLK], "x", 4, 1)
    x_far_b = move(x_high[2 * BLK :], "x", 4, -1)
    c_low = move(x_low, "core", 2, 1)
    c_high = move(x_high, "core", 2, 1)
    c_far_a = move(x_far_a, "core", 2, 1)
    c_far_b = move(x_far_b, "core", 2, 1)
    embedding = everywhere(own_emb).reshape(DOCS, D)
    near = [column, x_low, x_high, x_far_a, x_far_b]
    far = [c_column, c_low, c_high, c_far_a, c_far_b]
    labels = [part.reshape(-1, BLK, D) for part in near + far]

    which = jnp.arange(NB, dtype=I32)
    rel = jnp.array(REL, I32)
    b_core = core ^ (which >> 4)
    b_x = (x + rel[(which >> 2) & 3]) % 4
    b_y = (yh * 2 + yl + rel[which & 3]) % 4
    bases = (((((b_y >> 1) * 4 + b_x) * 2 + b_core) * 16) + z * 2 + (b_y & 1)) * LAB

    exps, tops, stats = first_pass(labels, embedding)
    all_stats = everywhere(stats)
    maxes, sums = all_stats[:, :4], all_stats[:, 4:]
    row_top = jnp.max(maxes, axis=0)
    row_total = jnp.sum(sums * jnp.exp(maxes - row_top[None]), axis=0)
    log_total = (row_top + jnp.log(row_total)).reshape(1, DOCS)
    positives = lax.dynamic_slice_in_dim(positive_cols, yl * DOCS, DOCS, 0).T
    grads, embed_part = second_pass(bases, labels, exps, tops, log_total, positives)

    back = spread(embed_part.reshape(8, DOCS // 8, D))
    own_grad = total(back).astype(BF16)
    embed_grad = everywhere(own_grad).reshape(DOCS, D)

    sums = [None] * 4
    for g in (3, 2, 1, 0):
        far_term = jnp.dot(grads[4 + g], embedding, preferred_element_type=F32).astype(BF16)
        far_term = move(far_term, "core", 2, 1)
        near_term = jnp.dot(grads[g], embedding, preferred_element_type=F32)
        sums[g] = (near_term + far_term.astype(F32)).astype(BF16)
    half = TILE // 2
    low_a = move(sums[3][:half], "x", 4, 1)
    high_b = move(sums[3][half:], "x", 4, -1)
    up_hi = move(sums[2][half:], "x", 4, 1)
    down_lo = move(sums[1][:half], "x", 4, -1)
    up_lo = add(sums[2][:half], low_a).astype(BF16)
    down_hi = add(sums[1][half:], high_b).astype(BF16)
    up_lo = move(up_lo, "x", 4, 1)
    down_hi = move(down_hi, "x", 4, -1)

    act_grad = lax.dot_general(embed_grad, down_all, NT, preferred_element_type=F32)
    _, gelu_pull = jax.vjp(partial(jax.nn.gelu, approximate=False), pre_act)
    pre_grad = gelu_pull(act_grad)[0].astype(BF16)
    pieces = []
    for j in range(2):
        cols = slice(j * units, (j + 1) * units)
        up_term = lax.dot_general(docs, pre_grad[:, cols], TN, preferred_element_type=F32)
        down_term = lax.dot_general(embed_grad, hidden[:, cols], TN, preferred_element_type=F32)
        pieces.append(jnp.concatenate([up_term, down_term], axis=1).astype(BF16))
    rows = D // 16
    terms = jnp.stack(pieces).reshape(2, 8, 2, rows, 2 * units)
    keep = jnp.where(core == 0, terms[:, :, 0], terms[:, :, 1])
    give = jnp.where(core == 0, terms[:, :, 1], terms[:, :, 0])
    give, up_lo, up_hi, down_lo, down_hi = lax.optimization_barrier((give, up_lo, up_hi, down_lo, down_hi))
    given = move(give, "core", 2, 1)
    both = add(keep, given).astype(BF16)
    both = jnp.swapaxes(both, 0, 1).reshape(16, rows, 2 * units)
    mlp = total(lax.all_to_all(both, ("yh", "x", "yl"), 0, 0))

    lo = (add(sums[0][:half], up_lo) + down_lo.astype(F32)).astype(BF16)
    hi = (add(sums[0][half:], up_hi) + down_hi.astype(F32)).astype(BF16)
    y_sums = [lo[:LAB], lo[LAB:], hi[:LAB], hi[LAB:]]
    half = LAB // 2
    low_a = move(y_sums[3][:half], plane_y, 4, 1)
    high_b = move(y_sums[3][half:], plane_y, 4, -1)
    up = jnp.concatenate([add(y_sums[2][:half], low_a), y_sums[2][half:].astype(F32)], axis=0).astype(BF16)
    down = jnp.concatenate([y_sums[1][:half].astype(F32), add(y_sums[1][half:], high_b)], axis=0).astype(BF16)
    up = move(up, plane_y, 4, 1)
    down = move(down, plane_y, 4, -1)
    label_grad = add(y_sums[0], up) + down.astype(F32)
    return (label_grad, mlp[:, :units], mlp[:, units:].T)


def solution(mesh):
    cut = Mesh(np.asarray(mesh.devices).reshape(2, 4, 2, 8, 2), ("yh", "x", "core", "z", "yl"))
    wide, narrow = ("yh", "x", "core"), ("z", "yl")
    in_specs = (
        P(wide, None),
        P(wide + narrow, None),
        P(wide + narrow),
        P(wide, None),
        P(None, narrow),
        P(narrow, None),
    )
    out_specs = (P(wide + narrow, None), P(wide, narrow), P(narrow, wide))
    return jax.shard_map(step_of, mesh=cut, in_specs=in_specs, out_specs=out_specs, check_vma=False)
```

profile of v0, /device:TPU:2, one launch (start us, length us, event | category | flops | bytes accessed | tf_op | source)
XLA Modules:
  0.0 222.7 jit_solution(15334626928252145749)
XLA Ops:
  4.1 6.6 %collective-permute-done.4 = bf16[192,768]{1,0:T(8,128)(2,1)S(1)} collective-permute-done((bf16[192,768]{1,0:T(8,128)(2,1)S(1)}, bf16[192,768]{1,0:T(8,128)(2,1)S(1)}, u32[]{:S(2)}, u32[]{:S(2)}) %collective-permute-start.4) | collective-permute-done | bytes 294944 | tf_op jit(solution)/shard_map/ppermute | solution.py:30
  13.2 3.0 %collective-permute-start.1 = (bf16[136,768]{1,0:T(8,128)(2,1)}, bf16[136,768]{1,0:T(8,128)(2,1)S(1)}, u32[]{:S(2)}, u32[]{:S(2)}) collective-permute-start(bf16[136,768]{1,0:T(8,128)(2,1)} %pad_maximum_fusion.5), channel_id=1, source_target_pairs={{0,129},{1,0},{128,1},{129,128},{2,131},{3,2},{130,3},{131,130},{4... | collective-permute-start | bytes 626696 | tf_op jit(solution)/shard_map/ppermute | solution.py:30
  17.4 3.1 %multiply_convert_fusion = (bf16[512,384]{0,1:T(8,128)(2,1)S(1)}, f32[512,384]{0,1:T(8,128)}, f32[512,384]{0,1:T(8,128)}) fusion(bf16[192,768]{1,0:T(8,128)(2,1)S(1)} %get-tuple-element.41, bf16[192,768]{1,0:T(8,128)(2,1)S(1)} %get-tuple-element.42, bf16[1024,768]{1,0:T(8,128)(2,1)S(1)} %copy-done.5, s32[]{:T(128)S(6)} %select_n.96), kind=kOutput, calls=%fused_computation.26 | convolution fusion | flops 315949056 | bytes 3342340 | tf_op jit(solution)/shard_map/dot_general | solution.py:322
  22.0 8.5 %all-to-all-start = ((bf16[8,64,768]{2,1,0:T(8,128)(2,1)}), bf16[8,64,768]{2,1,0:T(8,128)(2,1)S(1)}, u32[]{:S(2)}, u32[]{:S(2)}) async-start(bf16[8,64,768]{2,1,0:T(8,128)(2,1)} %bitcast.7), calls=%async_computation | async-start | bytes 1572864 | tf_op jit(solution)/shard_map/all_to_all | solution.py:281
  30.5 3.3 %collective-permute-start.3 = (bf16[72,768]{1,0:T(8,128)(2,1)S(1)}, bf16[72,768]{1,0:T(8,128)(2,1)S(1)}, u32[]{:S(2)}, u32[]{:S(2)}) collective-permute-start(bf16[72,768]{1,0:T(8,128)(2,1)S(1)} %slice.298), channel_id=1, source_target_pairs={{0,129},{1,0},{128,1},{129,128},{2,131},{3,2},{130,3},{131,130},{4... | collective-permute-start | bytes 331784 | tf_op jit(solution)/shard_map/ppermute | solution.py:30
  35.7 4.8 %collective-permute-done.2 = bf16[64,768]{1,0:T(8,128)(2,1)S(1)} collective-permute-done((bf16[64,768]{1,0:T(8,128)(2,1)S(1)}, bf16[64,768]{1,0:T(8,128)(2,1)S(1)}, u32[]{:S(2)}, u32[]{:S(2)}) %collective-permute-start.2) | collective-permute-done | bytes 98336 | tf_op jit(solution)/shard_map/ppermute | solution.py:30
  42.7 17.0 %collective-permute-done.7 = bf16[544,768]{1,0:T(8,128)(2,1)S(1)} collective-permute-done((bf16[544,768]{1,0:T(8,128)(2,1)S(1)}, bf16[544,768]{1,0:T(8,128)(2,1)S(1)}, u32[]{:S(2)}, u32[]{:S(2)}) %collective-permute-start.7) | collective-permute-done | bytes 835616 | tf_op jit(solution)/shard_map/ppermute | solution.py:30
  63.0 6.9 %all-to-all-start.1 = ((bf16[8,64,768]{2,1,0:T(8,128)(2,1)}), bf16[8,64,768]{2,1,0:T(8,128)(2,1)}, u32[]{:S(2)}, u32[]{:S(2)}) async-start(bf16[8,64,768]{2,1,0:T(8,128)(2,1)} %broadcast_in_dim.8), calls=%async_computation.1 | async-start | bytes 1572864 | tf_op jit(solution)/shard_map/all_to_all | solution.py:281
  69.9 3.0 %collective-permute-start.9 = (bf16[272,768]{1,0:T(8,128)(2,1)S(1)}, bf16[272,768]{1,0:T(8,128)(2,1)}, u32[]{:S(2)}, u32[]{:S(2)}) collective-permute-start(bf16[272,768]{1,0:T(8,128)(2,1)S(1)} %slice.221), channel_id=1, source_target_pairs={{0,96},{32,0},{64,32},{96,64},{1,97},{33,1},{65,33},{97,65},{2,98}... | collective-permute-start | bytes 1253384 | tf_op jit(solution)/shard_map/ppermute | solution.py:30
  73.7 8.8 %collective-permute-done.9 = bf16[272,768]{1,0:T(8,128)(2,1)} collective-permute-done((bf16[272,768]{1,0:T(8,128)(2,1)S(1)}, bf16[272,768]{1,0:T(8,128)(2,1)}, u32[]{:S(2)}, u32[]{:S(2)}) %collective-permute-start.9) | collective-permute-done | bytes 417824 | tf_op jit(solution)/shard_map/ppermute | solution.py:30
  87.1 3.7 %all-to-all-done.1 = bf16[8,64,768]{2,1,0:T(8,128)(2,1)} async-done(((bf16[8,64,768]{2,1,0:T(8,128)(2,1)}), bf16[8,64,768]{2,1,0:T(8,128)(2,1)}, u32[]{:S(2)}, u32[]{:S(2)}) %all-to-all-start.1) | async-done | bytes 786464 | tf_op jit(solution)/shard_map/all_to_all | solution.py:281
  90.7 9.5 %first_pass.1 = (f32[4096,512]{1,0:T(8,128)S(1)}, f32[8,1,512]{2,1,0:T(1,128)S(1)}, f32[8,128]{1,0:T(8,128)S(1)}) custom-call(bf16[4,136,768]{2,1,0:T(8,128)(2,1)S(1)} %bitcast.151, bf16[4,136,768]{2,1,0:T(8,128)(2,1)S(1)} %bitcast.149, bf16[4,136,768]{2,1,0:T(8,128)(2,1)S(1)} %bitcast.147, bf16[2,136,768]{2,1,0:T(8,128)(2,1)} %bitcast.10.refs_3_, ...), custom_call_target="tpu_custom_call" | custom-call | flops 3221225472 | bytes 16777216 | tf_op jit(solution)/shard_map/first_pass/pallas_call | solution.py:205
  100.3 3.3 %copy-done.1 = f32[4096,512]{1,0:T(8,128)} copy-done((f32[4096,512]{1,0:T(8,128)}, f32[4096,512]{1,0:T(8,128)S(1)}, u32[]{:S(2)}) %copy-start.1) | copy-done | bytes 8388632
  104.2 3.6 %all-to-all-start.2 = ((f32[8,8,128]{2,1,0:T(8,128)}), f32[8,8,128]{2,1,0:T(8,128)S(1)}, u32[]{:S(2)}, u32[]{:S(2)}) async-start(f32[8,8,128]{2,1,0:T(8,128)} %broadcast_in_dim.9), calls=%async_computation.2 | async-start | bytes 65536 | tf_op jit(solution)/shard_map/all_to_all | solution.py:281
  107.8 8.0 %all-to-all-done.2 = f32[8,8,128]{2,1,0:T(8,128)S(1)} async-done(((f32[8,8,128]{2,1,0:T(8,128)}), f32[8,8,128]{2,1,0:T(8,128)S(1)}, u32[]{:S(2)}, u32[]{:S(2)}) %all-to-all-start.2) | async-done | bytes 32800 | tf_op jit(solution)/shard_map/all_to_all | solution.py:281
  115.9 3.4 %copy-done.2 = f32[4096,512]{1,0:T(8,128)S(1)} copy-done((f32[4096,512]{1,0:T(8,128)S(1)}, f32[4096,512]{1,0:T(8,128)}, u32[]{:S(2)}) %copy-start.2) | copy-done | bytes 8388632
  119.2 11.1 %second_pass.1 = (bf16[8,512,512]{2,1,0:T(8,128)(2,1)S(1)}, bf16[512,768]{1,0:T(8,128)(2,1)S(1)}) custom-call(s32[32]{0:T(128)S(1)} %add_multiply_fusion.base_ref, bf16[4,136,768]{2,1,0:T(8,128)(2,1)S(1)} %bitcast.152, bf16[4,136,768]{2,1,0:T(8,128)(2,1)S(1)} %bitcast.150, bf16[4,136,768]{2,1,0:T(8,128)(2,1)S(1)} %bitcast.148, ...), custom_call_target="tpu_custom_call" | custom-call | flops 3221225472 | bytes 20971520 | tf_op jit(solution)/shard_map/second_pass/pallas_call | solution.py:242
  133.3 3.5 %all-to-all-start.3 = ((bf16[8,64,768]{2,1,0:T(8,128)(2,1)}), bf16[8,64,768]{2,1,0:T(8,128)(2,1)S(1)}, u32[]{:S(2)}, u32[]{:S(2)}) async-start(bf16[8,64,768]{2,1,0:T(8,128)(2,1)} %bitcast.155), calls=%async_computation.3 | async-start | bytes 1572864 | tf_op jit(solution)/shard_map/all_to_all | solution.py:281
  151.1 8.0 %all-to-all-done.3 = bf16[8,64,768]{2,1,0:T(8,128)(2,1)S(1)} async-done(((bf16[8,64,768]{2,1,0:T(8,128)(2,1)}), bf16[8,64,768]{2,1,0:T(8,128)(2,1)S(1)}, u32[]{:S(2)}, u32[]{:S(2)}) %all-to-all-start.3) | async-done | bytes 786464 | tf_op jit(solution)/shard_map/all_to_all | solution.py:281
  160.1 3.5 %all-to-all-start.4 = ((bf16[8,64,768]{2,1,0:T(8,128)(2,1)}), bf16[8,64,768]{2,1,0:T(8,128)(2,1)S(1)}, u32[]{:S(2)}, u32[]{:S(2)}) async-start(bf16[8,64,768]{2,1,0:T(8,128)(2,1)} %broadcast_in_dim.11), calls=%async_computation.4 | async-start | bytes 1572864 | tf_op jit(solution)/shard_map/all_to_all | solution.py:281
  174.3 3.0 %collective-permute-done.18 = bf16[256,768]{1,0:T(8,128)(2,1)S(1)} collective-permute-done((bf16[256,768]{1,0:T(8,128)(2,1)S(1)}, bf16[256,768]{1,0:T(8,128)(2,1)S(1)}, u32[]{:S(2)}, u32[]{:S(2)}) %collective-permute-start.18) | collective-permute-done | bytes 393248 | tf_op jit(solution)/shard_map/ppermute | solution.py:30
  181.0 6.2 %all-to-all-done.4 = bf16[8,64,768]{2,1,0:T(8,128)(2,1)S(1)} async-done(((bf16[8,64,768]{2,1,0:T(8,128)(2,1)}), bf16[8,64,768]{2,1,0:T(8,128)(2,1)S(1)}, u32[]{:S(2)}, u32[]{:S(2)}) %all-to-all-start.4) | async-done | bytes 786464 | tf_op jit(solution)/shard_map/all_to_all | solution.py:281
  203.3 4.1 %all-to-all-start.5 = ((bf16[16,48,384]{2,1,0:T(8,128)(2,1)}), bf16[16,48,384]{2,1,0:T(8,128)(2,1)S(1)}, u32[]{:S(2)}, u32[]{:S(2)}) async-start(bf16[16,48,384]{2,1,0:T(8,128)(2,1)} %bitcast.48), calls=%async_computation.5 | async-start | bytes 1179648 | tf_op jit(solution)/shard_map/all_to_all | solution.py:393
  209.0 12.1 %collective-permute-done.26 = bf16[128,768]{1,0:T(8,128)(2,1)S(1)} collective-permute-done((bf16[128,768]{1,0:T(8,128)(2,1)S(1)}, bf16[128,768]{1,0:T(8,128)(2,1)S(1)}, u32[]{:S(2)}, u32[]{:S(2)}) %collective-permute-start.26) | collective-permute-done | bytes 196640 | tf_op jit(solution)/shard_map/ppermute | solution.py:30
  (140 shorter events, 73.4 us)
Async XLA Ops:
  13.2 17.3 %collective-permute-start.1 = (bf16[136,768]{1,0:T(8,128)(2,1)}, bf16[136,768]{1,0:T(8,128)(2,1)S(1)}, u32[]{:S(2)}, u32[]{:S(2)}) collective-permute-start(bf16[136,768]{1,0:T(8,128)(2,1)} %pad_maximum_fusion.5), channel_id=1, source_target_pairs={{0,129},{1,0},{128,1},{129,128},{2,131},{3,2},{130,3},{131,130},{4... | collective-permute-start | bytes 626696 | tf_op jit(solution)/shard_map/ppermute | solution.py:30
  16.3 17.6 %collective-permute-start = (bf16[136,768]{1,0:T(8,128)(2,1)}, bf16[136,768]{1,0:T(8,128)(2,1)}, u32[]{:S(2)}, u32[]{:S(2)}) collective-permute-start(bf16[136,768]{1,0:T(8,128)(2,1)} %pad_maximum_fusion.5), channel_id=1, source_target_pairs={{0,1},{1,128},{128,129},{129,0},{2,3},{3,130},{130,131},{131,2},{4... | collective-permute-start | bytes 626696 | tf_op jit(solution)/shard_map/ppermute | solution.py:30
  22.0 38.9 %all-to-all-start = ((bf16[8,64,768]{2,1,0:T(8,128)(2,1)}), bf16[8,64,768]{2,1,0:T(8,128)(2,1)S(1)}, u32[]{:S(2)}, u32[]{:S(2)}) async-start(bf16[8,64,768]{2,1,0:T(8,128)(2,1)} %bitcast.7), calls=%async_computation | async-start | bytes 1572864 | tf_op jit(solution)/shard_map/all_to_all | solution.py:281
  40.6 19.1 %collective-permute-start.7 = (bf16[544,768]{1,0:T(8,128)(2,1)S(1)}, bf16[544,768]{1,0:T(8,128)(2,1)S(1)}, u32[]{:S(2)}, u32[]{:S(2)}) collective-permute-start(bf16[544,768]{1,0:T(8,128)(2,1)S(1)} %constant_dynamic-update-slice_fusion), channel_id=1, source_target_pairs={{0,96},{32,0},{64,32},{96,64},{1,97},{33,1},{65,33},{97,65},{2,98}... | collective-permute-start | bytes 2506760 | tf_op jit(solution)/shard_map/ppermute | solution.py:30
  41.2 19.8 %collective-permute-start.6 = (bf16[544,768]{1,0:T(8,128)(2,1)S(1)}, bf16[544,768]{1,0:T(8,128)(2,1)S(1)}, u32[]{:S(2)}, u32[]{:S(2)}) collective-permute-start(bf16[544,768]{1,0:T(8,128)(2,1)S(1)} %constant_dynamic-update-slice_fusion), channel_id=1, source_target_pairs={{0,32},{32,64},{64,96},{96,0},{1,33},{33,65},{65,97},{97,1},{2,34}... | collective-permute-start | bytes 2506760 | tf_op jit(solution)/shard_map/ppermute | solution.py:30
  63.0 27.7 %all-to-all-start.1 = ((bf16[8,64,768]{2,1,0:T(8,128)(2,1)}), bf16[8,64,768]{2,1,0:T(8,128)(2,1)}, u32[]{:S(2)}, u32[]{:S(2)}) async-start(bf16[8,64,768]{2,1,0:T(8,128)(2,1)} %broadcast_in_dim.8), calls=%async_computation.1 | async-start | bytes 1572864 | tf_op jit(solution)/shard_map/all_to_all | solution.py:281
  69.9 15.1 %collective-permute-start.10 = (bf16[544,768]{1,0:T(8,128)(2,1)S(1)}, bf16[544,768]{1,0:T(8,128)(2,1)S(1)}, u32[]{:S(2)}, u32[]{:S(2)}) collective-permute-start(bf16[544,768]{1,0:T(8,128)(2,1)S(1)} %constant_dynamic-update-slice_fusion), channel_id=1, source_target_pairs={{0,16},{16,0},{1,17},{17,1},{2,18},{18,2},{3,19},{19,3},{4,20},{20... | collective-permute-start | bytes 2506760 | tf_op jit(solution)/shard_map/ppermute | solution.py:30
  69.9 12.6 %collective-permute-start.9 = (bf16[272,768]{1,0:T(8,128)(2,1)S(1)}, bf16[272,768]{1,0:T(8,128)(2,1)}, u32[]{:S(2)}, u32[]{:S(2)}) collective-permute-start(bf16[272,768]{1,0:T(8,128)(2,1)S(1)} %slice.221), channel_id=1, source_target_pairs={{0,96},{32,0},{64,32},{96,64},{1,97},{33,1},{65,33},{97,65},{2,98}... | collective-permute-start | bytes 1253384 | tf_op jit(solution)/shard_map/ppermute | solution.py:30
  73.0 11.9 %collective-permute-start.8 = (bf16[272,768]{1,0:T(8,128)(2,1)S(1)}, bf16[272,768]{1,0:T(8,128)(2,1)}, u32[]{:S(2)}, u32[]{:S(2)}) collective-permute-start(bf16[272,768]{1,0:T(8,128)(2,1)S(1)} %slice.220), channel_id=1, source_target_pairs={{0,32},{32,64},{64,96},{96,0},{1,33},{33,65},{65,97},{97,1},{2,34}... | collective-permute-start | bytes 1253384 | tf_op jit(solution)/shard_map/ppermute | solution.py:30
  73.1 14.0 %collective-permute-start.11 = (bf16[544,768]{1,0:T(8,128)(2,1)S(1)}, bf16[544,768]{1,0:T(8,128)(2,1)}, u32[]{:S(2)}, u32[]{:S(2)}) collective-permute-start(bf16[544,768]{1,0:T(8,128)(2,1)S(1)} %collective-permute-done.6), channel_id=1, source_target_pairs={{0,16},{16,0},{1,17},{17,1},{2,18},{18,2},{3,19},{19,3},{4,20},{20... | collective-permute-start | bytes 2506760 | tf_op jit(solution)/shard_map/ppermute | solution.py:30
  73.4 13.7 %collective-permute-start.12 = (bf16[544,768]{1,0:T(8,128)(2,1)S(1)}, bf16[544,768]{1,0:T(8,128)(2,1)}, u32[]{:S(2)}, u32[]{:S(2)}) collective-permute-start(bf16[544,768]{1,0:T(8,128)(2,1)S(1)} %collective-permute-done.7), channel_id=1, source_target_pairs={{0,16},{16,0},{1,17},{17,1},{2,18},{18,2},{3,19},{19,3},{4,20},{20... | collective-permute-start | bytes 2506760 | tf_op jit(solution)/shard_map/ppermute | solution.py:30
  104.2 11.6 %all-to-all-start.2 = ((f32[8,8,128]{2,1,0:T(8,128)}), f32[8,8,128]{2,1,0:T(8,128)S(1)}, u32[]{:S(2)}, u32[]{:S(2)}) async-start(f32[8,8,128]{2,1,0:T(8,128)} %broadcast_in_dim.9), calls=%async_computation.2 | async-start | bytes 65536 | tf_op jit(solution)/shard_map/all_to_all | solution.py:281
  133.3 25.8 %all-to-all-start.3 = ((bf16[8,64,768]{2,1,0:T(8,128)(2,1)}), bf16[8,64,768]{2,1,0:T(8,128)(2,1)S(1)}, u32[]{:S(2)}, u32[]{:S(2)}) async-start(bf16[8,64,768]{2,1,0:T(8,128)(2,1)} %bitcast.155), calls=%async_computation.3 | async-start | bytes 1572864 | tf_op jit(solution)/shard_map/all_to_all | solution.py:281
  141.6 30.8 %collective-permute-start.15 = (bf16[512,768]{1,0:T(8,128)(2,1)}, bf16[512,768]{1,0:T(8,128)(2,1)S(1)}, u32[]{:S(2)}, u32[]{:S(2)}) collective-permute-start(bf16[512,768]{1,0:T(8,128)(2,1)} %convolution_convert_fusion.3), channel_id=1, source_target_pairs={{0,16},{16,0},{1,17},{17,1},{2,18},{18,2},{3,19},{19,3},{4,20},{20... | collective-permute-start | bytes 2359304 | tf_op jit(solution)/shard_map/ppermute | solution.py:30
  144.9 18.8 %collective-permute-start.17 = (bf16[512,768]{1,0:T(8,128)(2,1)}, bf16[512,768]{1,0:T(8,128)(2,1)}, u32[]{:S(2)}, u32[]{:S(2)}) collective-permute-start(bf16[512,768]{1,0:T(8,128)(2,1)} %convolution_convert_fusion.1), channel_id=1, source_target_pairs={{0,16},{16,0},{1,17},{17,1},{2,18},{18,2},{3,19},{19,3},{4,20},{20... | collective-permute-start | bytes 2359304 | tf_op jit(solution)/shard_map/ppermute | solution.py:30
  147.6 20.3 %collective-permute-start.21 = (bf16[512,768]{1,0:T(8,128)(2,1)}, bf16[512,768]{1,0:T(8,128)(2,1)}, u32[]{:S(2)}, u32[]{:S(2)}) collective-permute-start(bf16[512,768]{1,0:T(8,128)(2,1)} %convolution_convert_fusion), channel_id=1, source_target_pairs={{0,16},{16,0},{1,17},{17,1},{2,18},{18,2},{3,19},{19,3},{4,20},{20... | collective-permute-start | bytes 2359304 | tf_op jit(solution)/shard_map/ppermute | solution.py:30
  150.8 43.1 %collective-permute-start.20 = (bf16[256,768]{1,0:T(8,128)(2,1)}, bf16[256,768]{1,0:T(8,128)(2,1)S(1)}, u32[]{:S(2)}, u32[]{:S(2)}) collective-permute-start(bf16[256,768]{1,0:T(8,128)(2,1)} %slice.318), channel_id=1, source_target_pairs={{0,32},{32,64},{64,96},{96,0},{1,33},{33,65},{65,97},{97,1},{2,34}... | collective-permute-start | bytes 1179656 | tf_op jit(solution)/shard_map/ppermute | solution.py:30
  160.1 27.0 %all-to-all-start.4 = ((bf16[8,64,768]{2,1,0:T(8,128)(2,1)}), bf16[8,64,768]{2,1,0:T(8,128)(2,1)S(1)}, u32[]{:S(2)}, u32[]{:S(2)}) async-start(bf16[8,64,768]{2,1,0:T(8,128)(2,1)} %broadcast_in_dim.11), calls=%async_computation.4 | async-start | bytes 1572864 | tf_op jit(solution)/shard_map/all_to_all | solution.py:281
  165.9 13.7 %collective-permute-start.23 = (bf16[256,768]{1,0:T(8,128)(2,1)S(1)}, bf16[256,768]{1,0:T(8,128)(2,1)S(1)}, u32[]{:S(2)}, u32[]{:S(2)}) collective-permute-start(bf16[256,768]{1,0:T(8,128)(2,1)S(1)} %get-tuple-element.39), channel_id=1, source_target_pairs={{0,96},{32,0},{64,32},{96,64},{1,97},{33,1},{65,33},{97,65},{2,98}... | collective-permute-start | bytes 1179656 | tf_op jit(solution)/shard_map/ppermute | solution.py:30
  170.9 23.0 %collective-permute-start.22 = (bf16[256,768]{1,0:T(8,128)(2,1)}, bf16[256,768]{1,0:T(8,128)(2,1)}, u32[]{:S(2)}, u32[]{:S(2)}) collective-permute-start(bf16[256,768]{1,0:T(8,128)(2,1)} %slice.319), channel_id=1, source_target_pairs={{0,96},{32,0},{64,32},{96,64},{1,97},{33,1},{65,33},{97,65},{2,98}... | collective-permute-start | bytes 1179656 | tf_op jit(solution)/shard_map/ppermute | solution.py:30
  178.2 15.7 %collective-permute-start.19 = (bf16[256,768]{1,0:T(8,128)(2,1)}, bf16[256,768]{1,0:T(8,128)(2,1)}, u32[]{:S(2)}, u32[]{:S(2)}) collective-permute-start(bf16[256,768]{1,0:T(8,128)(2,1)} %add_convert_fusion.7), channel_id=1, source_target_pairs={{0,32},{32,64},{64,96},{96,0},{1,33},{33,65},{65,97},{97,1},{2,34}... | collective-permute-start | bytes 1179656 | tf_op jit(solution)/shard_map/ppermute | solution.py:30
  180.4 13.5 %collective-permute-start.24 = (bf16[256,768]{1,0:T(8,128)(2,1)}, bf16[256,768]{1,0:T(8,128)(2,1)}, u32[]{:S(2)}, u32[]{:S(2)}) collective-permute-start(bf16[256,768]{1,0:T(8,128)(2,1)} %add_convert_fusion.6), channel_id=1, source_target_pairs={{0,96},{32,0},{64,32},{96,64},{1,97},{33,1},{65,33},{97,65},{2,98}... | collective-permute-start | bytes 1179656 | tf_op jit(solution)/shard_map/ppermute | solution.py:30
  203.3 18.6 %all-to-all-start.5 = ((bf16[16,48,384]{2,1,0:T(8,128)(2,1)}), bf16[16,48,384]{2,1,0:T(8,128)(2,1)S(1)}, u32[]{:S(2)}, u32[]{:S(2)}) async-start(bf16[16,48,384]{2,1,0:T(8,128)(2,1)} %bitcast.48), calls=%async_computation.5 | async-start | bytes 1179648 | tf_op jit(solution)/shard_map/all_to_all | solution.py:393
  207.5 13.6 %collective-permute-start.26 = (bf16[128,768]{1,0:T(8,128)(2,1)S(1)}, bf16[128,768]{1,0:T(8,128)(2,1)S(1)}, u32[]{:S(2)}, u32[]{:S(2)}) collective-permute-start(bf16[128,768]{1,0:T(8,128)(2,1)S(1)} %pad_maximum_fusion.6), channel_id=1, source_target_pairs={{0,1},{1,128},{128,129},{129,0},{2,3},{3,130},{130,131},{131,2},{4... | collective-permute-start | bytes 589832 | tf_op jit(solution)/shard_map/ppermute | solution.py:30
  (26 other events, 255.0 us)
where the time goes:
time: 224 us; the launch traced here: 223 us
  waiting for transfers between devices  86.9 us (39%)
  starting transfers between devices  56.3 us (25%)
  matrix products  28.2 us (13%)
  Pallas kernels  20.7 us (9%)
  local copies, waits for them, and re-layouts  18.9 us (8%)
  other arithmetic  10.6 us (5%)
    ppermute x30, waiting for transfers between devices, move(): lax.ppermute(block, axes, [(i, (i + distance) % size) for i in range(size)])  61.1 us
    ppermute x30, starting transfers between devices, move(): lax.ppermute(block, axes, [(i, (i + distance) % size) for i in range(size)])  26.1 us
    all_to_all x5, starting transfers between devices, spread(): return lax.all_to_all(chunks, 'z', 0, 0)  26.1 us
    all_to_all x5, waiting for transfers between devices, spread(): return lax.all_to_all(chunks, 'z', 0, 0)  25.8 us
    unnamed x32, local copies, waits for them, and re-layouts  11.5 us
    pallas_call x1, Pallas kernels, second_pass(): pl.pallas_call(second_kernel, out_shape=(jax.ShapeDtypeStruct((STEPS, TIL...  11.1 us
    dot_general x4, matrix products, step_of(): jnp.dot(grads[4 + g], embedding, preferred_element_type=F32).astype(BF16)  10.2 us
    pallas_call x1, Pallas kernels, first_pass(): pl.pallas_call(first_kernel, out_shape=(jax.ShapeDtypeStruct((NB * LAB, D...  9.54 us
  transfers between devices with their start and end apart: 36, of which 16 were waited for; matrix products, arithmetic and copies ran while one was open for 19% of the time, Pallas kernels for 0%

commit v1 on v0

--- a/solution.py
+++ b/solution.py
@@ -101,35 +101,65 @@
 
 def first_kernel(*refs):
     label_refs = refs[:10]
-    emb_ref, exp_ref, top_ref, stat_ref, rows, extras, sems, raw_a, raw_b, bias_a, bias_b, run_max, run_sum = refs[10:]
+    (emb_hbm, exp_hbm, top_ref, stat_ref, rows, extras, sems, emb, emb_sem) = refs[10:19]
+    (raw_a, raw_b, bias_a, bias_b, exp_a, exp_b, exp_sem, run_max, run_sum) = refs[19:]
     step = pl.program_id(0)
+    fetch_emb = pltpu.make_async_copy(emb_hbm, emb, emb_sem)
+
+    @pl.when(step == 0)
+    def _():
+        fetch_emb.start()
+
     start_and_wait(fetch_labels(label_refs, rows, extras, sems))
+
+    @pl.when(step == 0)
+    def _():
+        fetch_emb.wait()
+
     group = jnp.minimum(step, STEPS - 1)
 
-    def body(raw_out, bias_out, raw_in, bias_in):
-        lhs = rows[group].reshape(TILE, D)
-        raw_out[...] = lax.dot_general(lhs, emb_ref[...], NT, preferred_element_type=F32)
+    def put(exp_out, slot, which):
+        return pltpu.make_async_copy(exp_out, exp_hbm.at[which], exp_sem.at[slot])
+
+    def body(slot, raw_out, bias_out, raw_in, bias_in, exp_out):
+        @pl.when(step >= 3)
+        def _():
+            put(exp_out, slot, step - 3).wait()
+
         for j in range(GRP):
             pieces = extras[group, j].astype(F32)
             row = pieces[0:1] + pieces[1:2] + pieces[2:3]
             bias_out[j * LAB : (j + 1) * LAB, :] = jnp.broadcast_to(row, (LAB, LAB)).T
-        for h in range(DOCS // LAB):
-            cols = slice(h * LAB, (h + 1) * LAB)
-            logits = raw_in[:, cols] - bias_in[...]
-            old = run_max[:, cols]
-            new = jnp.maximum(old, jnp.max(logits, axis=0, keepdims=True))
-            exps = jnp.exp(logits - new)
-            exp_ref[:, cols] = exps
-            run_sum[:, cols] = run_sum[:, cols] * jnp.exp(old - new) + jnp.sum(exps, axis=0, keepdims=True)
-            run_max[:, cols] = new
+        lhs = rows[group].reshape(TILE, D)
+        for half in range(2):
+            wide = slice(half * 256, (half + 1) * 256)
+            raw_out[:, wide] = lax.dot_general(lhs, emb[wide, :], NT, preferred_element_type=F32)
+            for h in range(2):
+                cols = slice(half * 256 + h * LAB, half * 256 + (h + 1) * LAB)
+                logits = raw_in[:, cols] - bias_in[...]
+                old = run_max[:, cols]
+                new = jnp.maximum(old, jnp.max(logits, axis=0, keepdims=True))
+                exps = jnp.exp(logits - new)
+                exp_out[:, cols] = exps
+                run_sum[:, cols] = run_sum[:, cols] * jnp.exp(old - new) + jnp.sum(exps, axis=0, keepdims=True)
+                run_max[:, cols] = new
+
+        @pl.when(step >= 1)
+        def _():
+            put(exp_out, slot, step - 1).start()
+
+        @pl.when(step == STEPS)
+        def _():
+            put(exp_b if slot == 0 else exp_a, 1 - slot, step - 2).wait()
+            put(exp_out, slot, step - 1).wait()
 
     @pl.when(lax.rem(step, 2) == 0)
     def _():
-        body(raw_a, bias_a, raw_b, bias_b)
+        body(0, raw_a, bias_a, raw_b, bias_b, exp_a)
 
     @pl.when(lax.rem(step, 2) == 1)
     def _():
-        body(raw_b, bias_b, raw_a, bias_a)
+        body(1, raw_b, bias_b, raw_a, bias_a, exp_b)
 
     @pl.when(step == 0)
     def _():
@@ -145,44 +175,67 @@
             stat_ref[4 + j : 5 + j, :] = run_sum[:, j * 128 : (j + 1) * 128]
 
 
-def second_kernel(base_ref, *refs):
+def hits_kernel(base_ref, pos_ref, hits_ref):
+    step = pl.program_id(0)
+    pos = [pos_ref[k : k + 1, :] for k in range(4)]
+    weights = []
+    for k in range(4):
+        same = [jnp.where(pos[k] == pos[n], F32(0.25), F32(0.0)) for n in range(4)]
+        weights.append(same[0] + same[1] + same[2] + same[3])
+    for h in range(DOCS // LAB):
+        cols = slice(h * LAB, (h + 1) * LAB)
+        ids = lax.broadcasted_iota(I32, (LAB, LAB), 0)
+
+        def block(j, carry):
+            base = base_ref[step * GRP + j]
+            hits = jnp.zeros((LAB, LAB), F32)
+            for k in (3, 2, 1, 0):
+                hits = jnp.where(pos[k][:, cols] - base == ids, weights[k][:, cols], hits)
+            hits_ref[0, pl.ds(pl.multiple_of(j * LAB, LAB), LAB), cols] = hits.astype(BF16)
+            return carry
+
+        lax.fori_loop(0, GRP, block, 0)
+
+
+def second_kernel(*refs):
     label_refs = refs[:10]
-    exp_ref, top_ref, total_ref, pos_ref, grad_ref, out_ref, rows, sems, grad_a, grad_b, acc = refs[10:]
+    exp_ref, top_ref, total_ref, hits_ref, grad_hbm, out_ref = refs[10:16]
+    rows, sems, grad_a, grad_b, grad_sem, acc = refs[16:]
     step = pl.program_id(0)
     start_and_wait(fetch_labels(label_refs, rows, None, sems))
-    group = jnp.minimum(step, STEPS - 1)
     before = jnp.maximum(step - 1, 0)
 
-    def body(grad_out, grad_in):
+    def put(grad, slot, which):
+        return pltpu.make_async_copy(grad, grad_hbm.at[which], grad_sem.at[slot])
+
+    def body(slot, grad_out, grad_in):
+        @pl.when(step >= 2)
+        def _():
+            put(grad_out, slot, step - 2).wait()
+
         scale = jnp.exp(top_ref[0] - total_ref[...])
-        pos = [pos_ref[k : k + 1, :] for k in range(4)]
-        weights = []
-        for k in range(4):
-            same = [jnp.where(pos[k] == pos[n], F32(0.25), F32(0.0)) for n in range(4)]
-            weights.append(same[0] + same[1] + same[2] + same[3])
         for j in range(GRP):
             span = slice(j * LAB, (j + 1) * LAB)
-            base = base_ref[group * GRP + j]
-            for h in range(DOCS // LAB):
-                cols = slice(h * LAB, (h + 1) * LAB)
-                ids = lax.broadcasted_iota(I32, (LAB, LAB), 0)
-                hits = jnp.zeros((LAB, LAB), F32)
-                for k in (3, 2, 1, 0):
-                    hits = jnp.where(pos[k][:, cols] - base == ids, weights[k][:, cols], hits)
-                grads = (exp_ref[span, cols] * scale[:, cols] - hits).astype(BF16)
-                grad_ref[0, span, cols] = grads
-                grad_out[span, cols] = grads
+            grad_out[span, :] = (exp_ref[0, span, :] * scale - hits_ref[0, span, :].astype(F32)).astype(BF16)
         acc[...] += lax.dot_general(
             grad_in[...], rows[before].reshape(TILE, D), TN, preferred_element_type=F32
         )
 
+        @pl.when(step < STEPS)
+        def _():
+            put(grad_out, slot, step).start()
+
+        @pl.when(step == STEPS)
+        def _():
+            put(grad_in, 1 - slot, step - 1).wait()
+
     @pl.when(lax.rem(step, 2) == 0)
     def _():
-        body(grad_a, grad_b)
+        body(0, grad_a, grad_b)
 
     @pl.when(lax.rem(step, 2) == 1)
     def _():
-        body(grad_b, grad_a)
+        body(1, grad_b, grad_a)
 
     @pl.when(step == 0)
     def _():
@@ -195,24 +248,20 @@
 
 def label_specs():
     return [pl.BlockSpec(memory_space=pl.ANY)] * 10
-
-
-def behind(step, *_):
-    return (jnp.maximum(step - 1, 0), 0)
 
 
 def first_pass(labels, embedding):
     return pl.pallas_call(
         first_kernel,
         out_shape=(
-            jax.ShapeDtypeStruct((NB * LAB, DOCS), F32),
+            pltpu.HBM((STEPS, TILE, DOCS), F32),
             jax.ShapeDtypeStruct((STEPS, 1, DOCS), F32),
             jax.ShapeDtypeStruct((8, 128), F32),
         ),
         grid=(STEPS + 1,),
-        in_specs=label_specs() + [pl.BlockSpec((DOCS, D), lambda s: (0, 0))],
+        in_specs=label_specs() + [pl.BlockSpec(memory_space=pl.ANY)],
         out_specs=(
-            pl.BlockSpec((TILE, DOCS), behind),
+            pl.BlockSpec(memory_space=pl.ANY),
             pl.BlockSpec((1, 1, DOCS), lambda s: (jnp.maximum(s - 1, 0), 0, 0)),
             pl.BlockSpec((8, 128), lambda s: (0, 0)),
         ),
@@ -220,10 +269,15 @@
             pltpu.VMEM((STEPS, GRP, LAB, D), BF16),
             pltpu.VMEM((STEPS, GRP, EXTRA, LAB), BF16),
             pltpu.SemaphoreType.DMA((STEPS, 4)),
+            pltpu.VMEM((DOCS, D), BF16),
+            pltpu.SemaphoreType.DMA,
             pltpu.VMEM((TILE, DOCS), F32),
             pltpu.VMEM((TILE, DOCS), F32),
             pltpu.VMEM((TILE, LAB), F32),
             pltpu.VMEM((TILE, LAB), F32),
+            pltpu.VMEM((TILE, DOCS), F32),
+            pltpu.VMEM((TILE, DOCS), F32),
+            pltpu.SemaphoreType.DMA((2,)),
             pltpu.VMEM((1, DOCS), F32),
             pltpu.VMEM((1, DOCS), F32),
         ],
@@ -237,36 +291,52 @@
     )(*labels, embedding)
 
 
-def second_pass(bases, labels, exps, tops, log_total, positives):
+def positive_hits(bases, positives):
+    return pl.pallas_call(
+        hits_kernel,
+        out_shape=pltpu.HBM((STEPS, TILE, DOCS), BF16),
+        grid_spec=pltpu.PrefetchScalarGridSpec(
+            num_scalar_prefetch=1,
+            grid=(STEPS,),
+            in_specs=[pl.BlockSpec((4, DOCS), lambda s, b: (0, 0))],
+            out_specs=pl.BlockSpec((1, TILE, DOCS), lambda s, b: (s, 0, 0)),
+        ),
+        compiler_params=pltpu.CompilerParams(dimension_semantics=("arbitrary",)),
+        cost_estimate=pl.CostEstimate(
+            flops=16 * NB * LAB * DOCS, bytes_accessed=4 << 20, transcendentals=0
+        ),
+        name="positive_hits",
+    )(bases, positives)
+
+
+def second_pass(labels, exps, tops, log_total, hits):
     last = STEPS - 1
     return pl.pallas_call(
         second_kernel,
         out_shape=(
-            jax.ShapeDtypeStruct((STEPS, TILE, DOCS), BF16),
-            jax.ShapeDtypeStruct((DOCS, D), BF16),
-        ),
-        grid_spec=pltpu.PrefetchScalarGridSpec(
-            num_scalar_prefetch=1,
-            grid=(STEPS + 1,),
-            in_specs=label_specs()
-            + [
-                pl.BlockSpec((TILE, DOCS), lambda s, b: (jnp.minimum(s, last), 0)),
-                pl.BlockSpec((1, 1, DOCS), lambda s, b: (jnp.minimum(s, last), 0, 0)),
-                pl.BlockSpec((1, DOCS), lambda s, b: (0, 0)),
-                pl.BlockSpec((4, DOCS), lambda s, b: (0, 0)),
-            ],
-            out_specs=(
-                pl.BlockSpec((1, TILE, DOCS), lambda s, b: (jnp.minimum(s, last), 0, 0)),
-                pl.BlockSpec((DOCS, D), lambda s, b: (0, 0)),
-            ),
-            scratch_shapes=[
-                pltpu.VMEM((STEPS, GRP, LAB, D), BF16),
-                pltpu.SemaphoreType.DMA((STEPS, 4)),
-                pltpu.VMEM((TILE, DOCS), BF16),
-                pltpu.VMEM((TILE, DOCS), BF16),
-                pltpu.VMEM((DOCS, D), F32),
-            ],
-        ),
+            pltpu.HBM((STEPS, TILE, DOCS), BF16),
+            pltpu.HBM((DOCS, D), BF16),
+        ),
+        grid=(STEPS + 1,),
+        in_specs=label_specs()
+        + [
+            pl.BlockSpec((1, TILE, DOCS), lambda s: (jnp.minimum(s, last), 0, 0)),
+            pl.BlockSpec((1, 1, DOCS), lambda s: (jnp.minimum(s, last), 0, 0)),
+            pl.BlockSpec((1, DOCS), lambda s: (0, 0)),
+            pl.BlockSpec((1, TILE, DOCS), lambda s: (jnp.minimum(s, last), 0, 0)),
+        ],
+        out_specs=(
+            pl.BlockSpec(memory_space=pl.ANY),
+            pl.BlockSpec((DOCS, D), lambda s: (0, 0)),
+        ),
+        scratch_shapes=[
+            pltpu.VMEM((STEPS, GRP, LAB, D), BF16),
+            pltpu.SemaphoreType.DMA((STEPS, 4)),
+            pltpu.VMEM((TILE, DOCS), BF16),
+            pltpu.VMEM((TILE, DOCS), BF16),
+            pltpu.SemaphoreType.DMA((2,)),
+            pltpu.VMEM((DOCS, D), F32),
+        ],
         compiler_params=pltpu.CompilerParams(
             dimension_semantics=("arbitrary",), vmem_limit_bytes=32 << 20
         ),
@@ -274,7 +344,7 @@
             flops=2 * NB * LAB * DOCS * D, bytes_accessed=20 << 20, transcendentals=0
         ),
         name="second_pass",
-    )(bases, *labels, exps, tops, log_total, positives)
+    )(*labels, exps, tops, log_total, hits)
 
 
 def spread(chunks):
@@ -351,18 +421,21 @@
     row_total = jnp.sum(sums * jnp.exp(maxes - row_top[None]), axis=0)
     log_total = (row_top + jnp.log(row_total)).reshape(1, DOCS)
     positives = lax.dynamic_slice_in_dim(positive_cols, yl * DOCS, DOCS, 0).T
-    grads, embed_part = second_pass(bases, labels, exps, tops, log_total, positives)
+    hits = positive_hits(bases, positives)
+    grads, embed_part = second_pass(labels, exps, tops, log_total, hits)
 
     back = spread(embed_part.reshape(8, DOCS // 8, D))
     own_grad = total(back).astype(BF16)
     embed_grad = everywhere(own_grad).reshape(DOCS, D)
 
-    sums = [None] * 4
-    for g in (3, 2, 1, 0):
-        far_term = jnp.dot(grads[4 + g], embedding, preferred_element_type=F32).astype(BF16)
-        far_term = move(far_term, "core", 2, 1)
-        near_term = jnp.dot(grads[g], embedding, preferred_element_type=F32)
-        sums[g] = (near_term + far_term.astype(F32)).astype(BF16)
+    far_all = jnp.dot(grads[4:].reshape(-1, DOCS), embedding, preferred_element_type=F32).astype(BF16)
+    far_all = move(far_all, "core", 2, 1)
+    far_all = far_all.reshape(4, TILE, D)
+    near_term = jnp.dot(grads[3], embedding, preferred_element_type=F32)
+    last_sum = (near_term + far_all[3].astype(F32)).astype(BF16)
+    near_term = jnp.dot(grads[:3].reshape(-1, DOCS), embedding, preferred_element_type=F32)
+    rest = (near_term + far_all[:3].reshape(-1, D).astype(F32)).astype(BF16).reshape(3, TILE, D)
+    sums = [rest[0], rest[1], rest[2], last_sum]
     half = TILE // 2
     low_a = move(sums[3][:half], "x", 4, 1)
     high_b = move(sums[3][half:], "x", 4, -1)

time: 224 us -> 252 us (1.12)
  waiting for transfers between devices: 86.9 us -> 117 us
  matrix products: 28.2 us -> 19.2 us
  Pallas kernels: 20.7 us -> 26.1 us
  starting transfers between devices: 56.3 us -> 59.4 us
    all_to_all x5, waiting for transfers between devices: 25.8 us -> 41.5 us  [spread(): return lax.all_to_all(chunks, 'z', 0, 0)]
    ppermute x30 -> x27, waiting for transfers between devices: 61.1 us -> 75.5 us  [move(): lax.ppermute(block, axes, [(i, (i + distance) % size) for i in range(size)])]
    dot_general x8 -> x3, matrix products: 18.1 us -> 10.1 us  [the longest x1 4.69 us: step_of(): jnp.dot(grads[4:].reshape(-1, DOCS), embedding, preferred_element_type=F32)]
    pallas_call x2 -> x3, Pallas kernels: 20.7 us -> 26.1 us  [the longest x1 10.4 us: first_pass(): pl.pallas_call(first_kernel, out_shape=(pltpu.HBM((STEPS, TILE, DOCS), F3...]
    slice x1 -> x2, local copies, waits for them, and re-layouts: 0.77 us -> 4.47 us  [the longest x1 2.74 us: step_of(): grads[:3].reshape(-1, DOCS)]
    all_to_all x5, starting transfers between devices: 26.1 us -> 29.1 us  [spread(): return lax.all_to_all(chunks, 'z', 0, 0)]
    unnamed x32 -> x34, local copies, waits for them, and re-layouts: 11.5 us -> 8.85 us
    ppermute x30 -> x27, starting transfers between devices: 26.1 us -> 25.1 us  [move(): lax.ppermute(block, axes, [(i, (i + distance) % size) for i in range(size)])]
  transfers between devices with their start and end apart: 36 -> 33, of which waited for: 16 -> 20; matrix products, arithmetic and copies ran while one was open for 19% -> 13% of each run, Pallas kernels for 0% -> 3%
where the time goes in v1:
time: 252 us; the launch traced here: 251 us
  waiting for transfers between devices  117 us (46%)
  starting transfers between devices  59.4 us (24%)
  Pallas kernels  26.1 us (10%)
  local copies, waits for them, and re-layouts  19.9 us (8%)
  matrix products  19.2 us (8%)
  other arithmetic  8.42 us (3%)
    ppermute x27, waiting for transfers between devices, move(): lax.ppermute(block, axes, [(i, (i + distance) % size) for i in range(size)])  75.5 us
    all_to_all x5, waiting for transfers between devices, spread(): return lax.all_to_all(chunks, 'z', 0, 0)  41.5 us
    all_to_all x5, starting transfers between devices, spread(): return lax.all_to_all(chunks, 'z', 0, 0)  29.1 us
    ppermute x27, starting transfers between devices, move(): lax.ppermute(block, axes, [(i, (i + distance) % size) for i in range(size)])  25.1 us
    pallas_call x1, Pallas kernels, first_pass(): pl.pallas_call(first_kernel, out_shape=(pltpu.HBM((STEPS, TILE, DOCS), F3...  10.4 us
    pallas_call x1, Pallas kernels, second_pass(): pl.pallas_call(second_kernel, out_shape=(pltpu.HBM((STEPS, TILE, DOCS), B...  8.87 us
    unnamed x34, local copies, waits for them, and re-layouts  8.85 us
    pallas_call x1, Pallas kernels, positive_hits(): pl.pallas_call(hits_kernel, out_shape=pltpu.HBM((STEPS, TILE, DOCS), BF16...  6.83 us
  transfers between devices with their start and end apart: 33, of which 20 were waited for; matrix products, arithmetic and copies ran while one was open for 13% of the time, Pallas kernels for 3%

profile of v1, /device:TPU:2, one launch (start us, length us, event | category | flops | bytes accessed | tf_op | source)
XLA Modules:
  0.0 251.1 jit_solution(8125506633954955707)
XLA Ops:
  4.1 6.6 %collective-permute-done.4 = bf16[192,768]{1,0:T(8,128)(2,1)S(1)} collective-permute-done((bf16[192,768]{1,0:T(8,128)(2,1)S(1)}, bf16[192,768]{1,0:T(8,128)(2,1)S(1)}, u32[]{:S(2)}, u32[]{:S(2)}) %collective-permute-start.4) | collective-permute-done | bytes 294944 | tf_op jit(solution)/shard_map/ppermute | solution.py:30
  22.0 8.5 %all-to-all-start = ((bf16[8,64,768]{2,1,0:T(8,128)(2,1)}), bf16[8,64,768]{2,1,0:T(8,128)(2,1)S(1)}, u32[]{:S(2)}, u32[]{:S(2)}) async-start(bf16[8,64,768]{2,1,0:T(8,128)(2,1)} %bitcast.5), calls=%async_computation | async-start | bytes 1572864 | tf_op jit(solution)/shard_map/all_to_all | solution.py:351
  30.5 3.3 %collective-permute-start.3 = (bf16[72,768]{1,0:T(8,128)(2,1)S(1)}, bf16[72,768]{1,0:T(8,128)(2,1)S(1)}, u32[]{:S(2)}, u32[]{:S(2)}) collective-permute-start(bf16[72,768]{1,0:T(8,128)(2,1)S(1)} %slice.303), channel_id=1, source_target_pairs={{0,129},{1,0},{128,1},{129,128},{2,131},{3,2},{130,3},{131,130},{4... | collective-permute-start | bytes 331784 | tf_op jit(solution)/shard_map/ppermute | solution.py:30
  35.7 4.8 %collective-permute-done.2 = bf16[64,768]{1,0:T(8,128)(2,1)S(1)} collective-permute-done((bf16[64,768]{1,0:T(8,128)(2,1)S(1)}, bf16[64,768]{1,0:T(8,128)(2,1)S(1)}, u32[]{:S(2)}, u32[]{:S(2)}) %collective-permute-start.2) | collective-permute-done | bytes 98336 | tf_op jit(solution)/shard_map/ppermute | solution.py:30
  42.7 17.0 %collective-permute-done.7 = bf16[544,768]{1,0:T(8,128)(2,1)S(1)} collective-permute-done((bf16[544,768]{1,0:T(8,128)(2,1)S(1)}, bf16[544,768]{1,0:T(8,128)(2,1)S(1)}, u32[]{:S(2)}, u32[]{:S(2)}) %collective-permute-start.7) | collective-permute-done | bytes 835616 | tf_op jit(solution)/shard_map/ppermute | solution.py:30
  63.0 6.9 %all-to-all-start.1 = ((bf16[8,64,768]{2,1,0:T(8,128)(2,1)}), bf16[8,64,768]{2,1,0:T(8,128)(2,1)}, u32[]{:S(2)}, u32[]{:S(2)}) async-start(bf16[8,64,768]{2,1,0:T(8,128)(2,1)} %broadcast_in_dim.8), calls=%async_computation.1 | async-start | bytes 1572864 | tf_op jit(solution)/shard_map/all_to_all | solution.py:351
  73.7 8.8 %collective-permute-done.9 = bf16[272,768]{1,0:T(8,128)(2,1)} collective-permute-done((bf16[272,768]{1,0:T(8,128)(2,1)S(1)}, bf16[272,768]{1,0:T(8,128)(2,1)}, u32[]{:S(2)}, u32[]{:S(2)}) %collective-permute-start.9) | collective-permute-done | bytes 417824 | tf_op jit(solution)/shard_map/ppermute | solution.py:30
  87.1 3.7 %all-to-all-done.1 = bf16[8,64,768]{2,1,0:T(8,128)(2,1)} async-done(((bf16[8,64,768]{2,1,0:T(8,128)(2,1)}), bf16[8,64,768]{2,1,0:T(8,128)(2,1)}, u32[]{:S(2)}, u32[]{:S(2)}) %all-to-all-start.1) | async-done | bytes 786464 | tf_op jit(solution)/shard_map/all_to_all | solution.py:351
  90.7 10.4 %first_pass.1 = (f32[8,512,512]{2,1,0:T(8,128)}, f32[8,1,512]{2,1,0:T(1,128)S(1)}, f32[8,128]{1,0:T(8,128)S(1)}) custom-call(bf16[4,136,768]{2,1,0:T(8,128)(2,1)S(1)} %bitcast.123, bf16[4,136,768]{2,1,0:T(8,128)(2,1)S(1)} %bitcast.121, bf16[4,136,768]{2,1,0:T(8,128)(2,1)S(1)} %bitcast.119, bf16[2,136,768]{2,1,0:T(8,128)(2,1)} %bitcast.8.refs_3_, ...), custom_call_target="tpu_custom_call" | custom-call | flops 3221225472 | bytes 16777216 | tf_op jit(solution)/shard_map/first_pass/pallas_call | solution.py:254
  101.7 3.6 %all-to-all-start.2 = ((f32[8,8,128]{2,1,0:T(8,128)}), f32[8,8,128]{2,1,0:T(8,128)S(1)}, u32[]{:S(2)}, u32[]{:S(2)}) async-start(f32[8,8,128]{2,1,0:T(8,128)} %broadcast_in_dim.9), calls=%async_computation.2 | async-start | bytes 65536 | tf_op jit(solution)/shard_map/all_to_all | solution.py:351
  105.8 6.8 %positive_hits.1.refs_13_ = bf16[8,512,512]{2,1,0:T(8,128)(2,1)} custom-call(s32[32]{0:T(128)} %add_multiply_fusion.base_ref, s32[4,512]{1,0:T(4,128)} %dynamic-slice_bitcast_fusion.pos_ref), custom_call_target="tpu_custom_call" | custom-call | flops 33554432 | bytes 4194304 | tf_op jit(solution)/shard_map/positive_hits/pallas_call | solution.py:295
  115.6 3.4 %copy-done.2 = f32[8,512,512]{2,1,0:T(8,128)S(1)} copy-done((f32[8,512,512]{2,1,0:T(8,128)S(1)}, f32[8,512,512]{2,1,0:T(8,128)}, u32[]{:S(2)}) %copy-start.2) | copy-done | bytes 8388632
  119.0 8.9 %second_pass.1 = (bf16[8,512,512]{2,1,0:T(8,128)(2,1)}, bf16[512,768]{1,0:T(8,128)(2,1)}) custom-call(bf16[4,136,768]{2,1,0:T(8,128)(2,1)S(1)} %bitcast.124, bf16[4,136,768]{2,1,0:T(8,128)(2,1)S(1)} %bitcast.122, bf16[4,136,768]{2,1,0:T(8,128)(2,1)S(1)} %bitcast.120, bf16[2,136,768]{2,1,0:T(8,128)(2,1)} %bitcast.8.refs_3_, ...), custom_call_target="tpu_custom_call" | custom-call | flops 3221225472 | bytes 20971520 | tf_op jit(solution)/shard_map/second_pass/pallas_call | solution.py:314
  127.8 6.6 %all-to-all-start.3 = ((bf16[8,64,768]{2,1,0:T(8,128)(2,1)}), bf16[8,64,768]{2,1,0:T(8,128)(2,1)S(1)}, u32[]{:S(2)}, u32[]{:S(2)}) async-start(bf16[8,64,768]{2,1,0:T(8,128)(2,1)} %bitcast.136), calls=%async_computation.3 | async-start | bytes 1572864 | tf_op jit(solution)/shard_map/all_to_all | solution.py:351
  136.1 4.7 %convolution_convert_fusion = bf16[2048,768]{1,0:T(8,128)(2,1)} fusion(bf16[2048,512]{1,0:T(8,128)(2,1)S(1)} %bitcast.132, bf16[512,768]{1,0:T(8,128)(2,1)} %bitcast.16.refs_10_), kind=kOutput, calls=%fused_computation.1 | convolution fusion | flops 1612185600 | bytes 6029312 | tf_op jit(solution)/shard_map/dot_general | solution.py:431
  140.8 16.4 %all-to-all-done.3 = bf16[8,64,768]{2,1,0:T(8,128)(2,1)S(1)} async-done(((bf16[8,64,768]{2,1,0:T(8,128)(2,1)}), bf16[8,64,768]{2,1,0:T(8,128)(2,1)S(1)}, u32[]{:S(2)}, u32[]{:S(2)}) %all-to-all-start.3) | async-done | bytes 786464 | tf_op jit(solution)/shard_map/all_to_all | solution.py:351
  158.4 3.5 %all-to-all-start.4 = ((bf16[8,64,768]{2,1,0:T(8,128)(2,1)}), bf16[8,64,768]{2,1,0:T(8,128)(2,1)S(1)}, u32[]{:S(2)}, u32[]{:S(2)}) async-start(bf16[8,64,768]{2,1,0:T(8,128)(2,1)} %broadcast_in_dim.11), calls=%async_computation.4 | async-start | bytes 1572864 | tf_op jit(solution)/shard_map/all_to_all | solution.py:351
  164.7 20.7 %all-to-all-done.4 = bf16[8,64,768]{2,1,0:T(8,128)(2,1)S(1)} async-done(((bf16[8,64,768]{2,1,0:T(8,128)(2,1)}), bf16[8,64,768]{2,1,0:T(8,128)(2,1)S(1)}, u32[]{:S(2)}, u32[]{:S(2)}) %all-to-all-start.4) | async-done | bytes 786464 | tf_op jit(solution)/shard_map/all_to_all | solution.py:351
  196.2 3.3 %add_convert_fusion = bf16[1536,768]{1,0:T(8,128)(2,1)S(1)} fusion(bf16[2048,768]{1,0:T(8,128)(2,1)} %collective-permute-done.15, bf16[1536,512]{1,0:T(8,128)(2,1)S(1)} %bitcast.133, bf16[512,768]{1,0:T(8,128)(2,1)} %bitcast.16.refs_10_), kind=kOutput, calls=%fused_computation | convolution fusion | flops 1211498496 | bytes 7077888 | tf_op jit(solution)/shard_map/dot_general | solution.py:436
  201.7 4.5 %collective-permute-done.20 = bf16[256,768]{1,0:T(8,128)(2,1)S(1)} collective-permute-done((bf16[256,768]{1,0:T(8,128)(2,1)S(1)}, bf16[256,768]{1,0:T(8,128)(2,1)S(1)}, u32[]{:S(2)}, u32[]{:S(2)}) %collective-permute-start.20) | collective-permute-done | bytes 393248 | tf_op jit(solution)/shard_map/ppermute | solution.py:30
  209.3 5.3 %collective-permute-done.19 = bf16[256,768]{1,0:T(8,128)(2,1)S(1)} collective-permute-done((bf16[256,768]{1,0:T(8,128)(2,1)S(1)}, bf16[256,768]{1,0:T(8,128)(2,1)S(1)}, u32[]{:S(2)}, u32[]{:S(2)}) %collective-permute-start.19) | collective-permute-done | bytes 393248 | tf_op jit(solution)/shard_map/ppermute | solution.py:30
  214.9 7.2 %collective-permute-done.21 = bf16[256,768]{1,0:T(8,128)(2,1)S(1)} collective-permute-done((bf16[256,768]{1,0:T(8,128)(2,1)S(1)}, bf16[256,768]{1,0:T(8,128)(2,1)S(1)}, u32[]{:S(2)}, u32[]{:S(2)}) %collective-permute-start.21) | collective-permute-done | bytes 393248 | tf_op jit(solution)/shard_map/ppermute | solution.py:30
  230.6 5.3 %all-to-all-start.5 = ((bf16[16,48,384]{2,1,0:T(8,128)(2,1)}), bf16[16,48,384]{2,1,0:T(8,128)(2,1)S(1)}, u32[]{:S(2)}, u32[]{:S(2)}) async-start(bf16[16,48,384]{2,1,0:T(8,128)(2,1)} %bitcast.43), calls=%async_computation.5 | async-start | bytes 1179648 | tf_op jit(solution)/shard_map/all_to_all | solution.py:466
  237.5 12.1 %collective-permute-done.23 = bf16[128,768]{1,0:T(8,128)(2,1)S(1)} collective-permute-done((bf16[128,768]{1,0:T(8,128)(2,1)S(1)}, bf16[128,768]{1,0:T(8,128)(2,1)S(1)}, u32[]{:S(2)}, u32[]{:S(2)}) %collective-permute-start.23) | collective-permute-done | bytes 196640 | tf_op jit(solution)/shard_map/ppermute | solution.py:30
  (132 shorter events, 67.9 us)
Async XLA Ops:
  13.2 17.3 %collective-permute-start.1 = (bf16[136,768]{1,0:T(8,128)(2,1)}, bf16[136,768]{1,0:T(8,128)(2,1)S(1)}, u32[]{:S(2)}, u32[]{:S(2)}) collective-permute-start(bf16[136,768]{1,0:T(8,128)(2,1)} %pad_maximum_fusion.5), channel_id=1, source_target_pairs={{0,129},{1,0},{128,1},{129,128},{2,131},{3,2},{130,3},{131,130},{4... | collective-permute-start | bytes 626696 | tf_op jit(solution)/shard_map/ppermute | solution.py:30
  16.3 17.6 %collective-permute-start = (bf16[136,768]{1,0:T(8,128)(2,1)}, bf16[136,768]{1,0:T(8,128)(2,1)}, u32[]{:S(2)}, u32[]{:S(2)}) collective-permute-start(bf16[136,768]{1,0:T(8,128)(2,1)} %pad_maximum_fusion.5), channel_id=1, source_target_pairs={{0,1},{1,128},{128,129},{129,0},{2,3},{3,130},{130,131},{131,2},{4... | collective-permute-start | bytes 626696 | tf_op jit(solution)/shard_map/ppermute | solution.py:30
  22.0 38.9 %all-to-all-start = ((bf16[8,64,768]{2,1,0:T(8,128)(2,1)}), bf16[8,64,768]{2,1,0:T(8,128)(2,1)S(1)}, u32[]{:S(2)}, u32[]{:S(2)}) async-start(bf16[8,64,768]{2,1,0:T(8,128)(2,1)} %bitcast.5), calls=%async_computation | async-start | bytes 1572864 | tf_op jit(solution)/shard_map/all_to_all | solution.py:351
  30.5 10.0 %collective-permute-start.3 = (bf16[72,768]{1,0:T(8,128)(2,1)S(1)}, bf16[72,768]{1,0:T(8,128)(2,1)S(1)}, u32[]{:S(2)}, u32[]{:S(2)}) collective-permute-start(bf16[72,768]{1,0:T(8,128)(2,1)S(1)} %slice.303), channel_id=1, source_target_pairs={{0,129},{1,0},{128,1},{129,128},{2,131},{3,2},{130,3},{131,130},{4... | collective-permute-start | bytes 331784 | tf_op jit(solution)/shard_map/ppermute | solution.py:30
  40.6 19.1 %collective-permute-start.7 = (bf16[544,768]{1,0:T(8,128)(2,1)S(1)}, bf16[544,768]{1,0:T(8,128)(2,1)S(1)}, u32[]{:S(2)}, u32[]{:S(2)}) collective-permute-start(bf16[544,768]{1,0:T(8,128)(2,1)S(1)} %constant_dynamic-update-slice_fusion), channel_id=1, source_target_pairs={{0,96},{32,0},{64,32},{96,64},{1,97},{33,1},{65,33},{97,65},{2,98}... | collective-permute-start | bytes 2506760 | tf_op jit(solution)/shard_map/ppermute | solution.py:30
  41.2 19.8 %collective-permute-start.6 = (bf16[544,768]{1,0:T(8,128)(2,1)S(1)}, bf16[544,768]{1,0:T(8,128)(2,1)S(1)}, u32[]{:S(2)}, u32[]{:S(2)}) collective-permute-start(bf16[544,768]{1,0:T(8,128)(2,1)S(1)} %constant_dynamic-update-slice_fusion), channel_id=1, source_target_pairs={{0,32},{32,64},{64,96},{96,0},{1,33},{33,65},{65,97},{97,1},{2,34}... | collective-permute-start | bytes 2506760 | tf_op jit(solution)/shard_map/ppermute | solution.py:30
  63.0 27.7 %all-to-all-start.1 = ((bf16[8,64,768]{2,1,0:T(8,128)(2,1)}), bf16[8,64,768]{2,1,0:T(8,128)(2,1)}, u32[]{:S(2)}, u32[]{:S(2)}) async-start(bf16[8,64,768]{2,1,0:T(8,128)(2,1)} %broadcast_in_dim.8), calls=%async_computation.1 | async-start | bytes 1572864 | tf_op jit(solution)/shard_map/all_to_all | solution.py:351
  69.9 15.7 %collective-permute-start.10 = (bf16[544,768]{1,0:T(8,128)(2,1)S(1)}, bf16[544,768]{1,0:T(8,128)(2,1)S(1)}, u32[]{:S(2)}, u32[]{:S(2)}) collective-permute-start(bf16[544,768]{1,0:T(8,128)(2,1)S(1)} %constant_dynamic-update-slice_fusion), channel_id=1, source_target_pairs={{0,16},{16,0},{1,17},{17,1},{2,18},{18,2},{3,19},{19,3},{4,20},{20... | collective-permute-start | bytes 2506760 | tf_op jit(solution)/shard_map/ppermute | solution.py:30
  70.0 12.6 %collective-permute-start.9 = (bf16[272,768]{1,0:T(8,128)(2,1)S(1)}, bf16[272,768]{1,0:T(8,128)(2,1)}, u32[]{:S(2)}, u32[]{:S(2)}) collective-permute-start(bf16[272,768]{1,0:T(8,128)(2,1)S(1)} %slice.229), channel_id=1, source_target_pairs={{0,96},{32,0},{64,32},{96,64},{1,97},{33,1},{65,33},{97,65},{2,98}... | collective-permute-start | bytes 1253384 | tf_op jit(solution)/shard_map/ppermute | solution.py:30
  73.0 11.9 %collective-permute-start.8 = (bf16[272,768]{1,0:T(8,128)(2,1)S(1)}, bf16[272,768]{1,0:T(8,128)(2,1)}, u32[]{:S(2)}, u32[]{:S(2)}) collective-permute-start(bf16[272,768]{1,0:T(8,128)(2,1)S(1)} %slice.228), channel_id=1, source_target_pairs={{0,32},{32,64},{64,96},{96,0},{1,33},{33,65},{65,97},{97,1},{2,34}... | collective-permute-start | bytes 1253384 | tf_op jit(solution)/shard_map/ppermute | solution.py:30
  73.1 14.0 %collective-permute-start.11 = (bf16[544,768]{1,0:T(8,128)(2,1)S(1)}, bf16[544,768]{1,0:T(8,128)(2,1)}, u32[]{:S(2)}, u32[]{:S(2)}) collective-permute-start(bf16[544,768]{1,0:T(8,128)(2,1)S(1)} %collective-permute-done.6), channel_id=1, source_target_pairs={{0,16},{16,0},{1,17},{17,1},{2,18},{18,2},{3,19},{19,3},{4,20},{20... | collective-permute-start | bytes 2506760 | tf_op jit(solution)/shard_map/ppermute | solution.py:30
  73.4 13.7 %collective-permute-start.12 = (bf16[544,768]{1,0:T(8,128)(2,1)S(1)}, bf16[544,768]{1,0:T(8,128)(2,1)}, u32[]{:S(2)}, u32[]{:S(2)}) collective-permute-start(bf16[544,768]{1,0:T(8,128)(2,1)S(1)} %collective-permute-done.7), channel_id=1, source_target_pairs={{0,16},{16,0},{1,17},{17,1},{2,18},{18,2},{3,19},{19,3},{4,20},{20... | collective-permute-start | bytes 2506760 | tf_op jit(solution)/shard_map/ppermute | solution.py:30
  101.7 11.6 %all-to-all-start.2 = ((f32[8,8,128]{2,1,0:T(8,128)}), f32[8,8,128]{2,1,0:T(8,128)S(1)}, u32[]{:S(2)}, u32[]{:S(2)}) async-start(f32[8,8,128]{2,1,0:T(8,128)} %broadcast_in_dim.9), calls=%async_computation.2 | async-start | bytes 65536 | tf_op jit(solution)/shard_map/all_to_all | solution.py:351
  127.8 29.4 %all-to-all-start.3 = ((bf16[8,64,768]{2,1,0:T(8,128)(2,1)}), bf16[8,64,768]{2,1,0:T(8,128)(2,1)S(1)}, u32[]{:S(2)}, u32[]{:S(2)}) async-start(bf16[8,64,768]{2,1,0:T(8,128)(2,1)} %bitcast.136), calls=%async_computation.3 | async-start | bytes 1572864 | tf_op jit(solution)/shard_map/all_to_all | solution.py:351
  140.8 51.1 %collective-permute-start.15 = (bf16[2048,768]{1,0:T(8,128)(2,1)}, bf16[2048,768]{1,0:T(8,128)(2,1)}, u32[]{:S(2)}, u32[]{:S(2)}) collective-permute-start(bf16[2048,768]{1,0:T(8,128)(2,1)} %convolution_convert_fusion), channel_id=1, source_target_pairs={{0,16},{16,0},{1,17},{17,1},{2,18},{18,2},{3,19},{19,3},{4,20},{20... | collective-permute-start | bytes 9437192 | tf_op jit(solution)/shard_map/ppermute | solution.py:30
  158.4 27.0 %all-to-all-start.4 = ((bf16[8,64,768]{2,1,0:T(8,128)(2,1)}), bf16[8,64,768]{2,1,0:T(8,128)(2,1)S(1)}, u32[]{:S(2)}, u32[]{:S(2)}) async-start(bf16[8,64,768]{2,1,0:T(8,128)(2,1)} %broadcast_in_dim.11), calls=%async_computation.4 | async-start | bytes 1572864 | tf_op jit(solution)/shard_map/all_to_all | solution.py:351
  194.1 12.1 %collective-permute-start.20 = (bf16[256,768]{1,0:T(8,128)(2,1)S(1)}, bf16[256,768]{1,0:T(8,128)(2,1)S(1)}, u32[]{:S(2)}, u32[]{:S(2)}) collective-permute-start(bf16[256,768]{1,0:T(8,128)(2,1)S(1)} %get-tuple-element.43), channel_id=1, source_target_pairs={{0,96},{32,0},{64,32},{96,64},{1,97},{33,1},{65,33},{97,65},{2,98}... | collective-permute-start | bytes 1179656 | tf_op jit(solution)/shard_map/ppermute | solution.py:30
  194.2 12.3 %collective-permute-start.16 = (bf16[256,768]{1,0:T(8,128)(2,1)S(1)}, bf16[256,768]{1,0:T(8,128)(2,1)S(1)}, u32[]{:S(2)}, u32[]{:S(2)}) collective-permute-start(bf16[256,768]{1,0:T(8,128)(2,1)S(1)} %get-tuple-element.44), channel_id=1, source_target_pairs={{0,32},{32,64},{64,96},{96,0},{1,33},{33,65},{65,97},{97,1},{2,34}... | collective-permute-start | bytes 1179656 | tf_op jit(solution)/shard_map/ppermute | solution.py:30
  199.6 15.0 %collective-permute-start.19 = (bf16[256,768]{1,0:T(8,128)(2,1)S(1)}, bf16[256,768]{1,0:T(8,128)(2,1)S(1)}, u32[]{:S(2)}, u32[]{:S(2)}) collective-permute-start(bf16[256,768]{1,0:T(8,128)(2,1)S(1)} %get-tuple-element.37), channel_id=1, source_target_pairs={{0,96},{32,0},{64,32},{96,64},{1,97},{33,1},{65,33},{97,65},{2,98}... | collective-permute-start | bytes 1179656 | tf_op jit(solution)/shard_map/ppermute | solution.py:30
  200.0 14.9 %collective-permute-start.18 = (bf16[256,768]{1,0:T(8,128)(2,1)S(1)}, bf16[256,768]{1,0:T(8,128)(2,1)S(1)}, u32[]{:S(2)}, u32[]{:S(2)}) collective-permute-start(bf16[256,768]{1,0:T(8,128)(2,1)S(1)} %get-tuple-element.38), channel_id=1, source_target_pairs={{0,32},{32,64},{64,96},{96,0},{1,33},{33,65},{65,97},{97,1},{2,34}... | collective-permute-start | bytes 1179656 | tf_op jit(solution)/shard_map/ppermute | solution.py:30
  206.7 15.4 %collective-permute-start.21 = (bf16[256,768]{1,0:T(8,128)(2,1)S(1)}, bf16[256,768]{1,0:T(8,128)(2,1)S(1)}, u32[]{:S(2)}, u32[]{:S(2)}) collective-permute-start(bf16[256,768]{1,0:T(8,128)(2,1)S(1)} %get-tuple-element.35), channel_id=1, source_target_pairs={{0,96},{32,0},{64,32},{96,64},{1,97},{33,1},{65,33},{97,65},{2,98}... | collective-permute-start | bytes 1179656 | tf_op jit(solution)/shard_map/ppermute | solution.py:30
  208.7 13.8 %collective-permute-start.17 = (bf16[256,768]{1,0:T(8,128)(2,1)S(1)}, bf16[256,768]{1,0:T(8,128)(2,1)S(1)}, u32[]{:S(2)}, u32[]{:S(2)}) collective-permute-start(bf16[256,768]{1,0:T(8,128)(2,1)S(1)} %get-tuple-element.36), channel_id=1, source_target_pairs={{0,32},{32,64},{64,96},{96,0},{1,33},{33,65},{65,97},{97,1},{2,34}... | collective-permute-start | bytes 1179656 | tf_op jit(solution)/shard_map/ppermute | solution.py:30
  230.6 19.7 %all-to-all-start.5 = ((bf16[16,48,384]{2,1,0:T(8,128)(2,1)}), bf16[16,48,384]{2,1,0:T(8,128)(2,1)S(1)}, u32[]{:S(2)}, u32[]{:S(2)}) async-start(bf16[16,48,384]{2,1,0:T(8,128)(2,1)} %bitcast.43), calls=%async_computation.5 | async-start | bytes 1179648 | tf_op jit(solution)/shard_map/all_to_all | solution.py:466
  235.9 13.6 %collective-permute-start.23 = (bf16[128,768]{1,0:T(8,128)(2,1)S(1)}, bf16[128,768]{1,0:T(8,128)(2,1)S(1)}, u32[]{:S(2)}, u32[]{:S(2)}) collective-permute-start(bf16[128,768]{1,0:T(8,128)(2,1)S(1)} %pad_maximum_fusion.6), channel_id=1, source_target_pairs={{0,1},{1,128},{128,129},{129,0},{2,3},{3,130},{130,131},{131,2},{4... | collective-permute-start | bytes 589832 | tf_op jit(solution)/shard_map/ppermute | solution.py:30
  (24 other events, 249.4 us)

commit v2 on v1

--- a/solution.py
+++ b/solution.py
@@ -199,19 +199,20 @@
 
 def second_kernel(*refs):
     label_refs = refs[:10]
-    exp_ref, top_ref, total_ref, hits_ref, grad_hbm, out_ref = refs[10:16]
-    rows, sems, grad_a, grad_b, grad_sem, acc = refs[16:]
+    exp_ref, top_ref, total_ref, hits_ref, near_hbm, near_end, far_hbm, far_end, out_ref = refs[10:19]
+    rows, sems, grad_a, grad_b, grad_sem, acc = refs[19:]
+    side = STEPS // 2
     step = pl.program_id(0)
     start_and_wait(fetch_labels(label_refs, rows, None, sems))
     before = jnp.maximum(step - 1, 0)
 
-    def put(grad, slot, which):
-        return pltpu.make_async_copy(grad, grad_hbm.at[which], grad_sem.at[slot])
+    def put(grad, slot, home, which):
+        return pltpu.make_async_copy(grad, home.at[which], grad_sem.at[slot])
 
     def body(slot, grad_out, grad_in):
         @pl.when(step >= 2)
         def _():
-            put(grad_out, slot, step - 2).wait()
+            put(grad_out, slot, near_hbm, 0).wait()
 
         scale = jnp.exp(top_ref[0] - total_ref[...])
         for j in range(GRP):
@@ -221,13 +222,27 @@
             grad_in[...], rows[before].reshape(TILE, D), TN, preferred_element_type=F32
         )
 
-        @pl.when(step < STEPS)
-        def _():
-            put(grad_out, slot, step).start()
+        @pl.when(step < side - 1)
+        def _():
+            put(grad_out, slot, near_hbm, step).start()
+
+        @pl.when((step >= side) & (step < STEPS - 1))
+        def _():
+            put(grad_out, slot, far_hbm, step - side).start()
+
+        if slot == 1:
+
+            @pl.when(step == side - 1)
+            def _():
+                put(grad_out, slot, near_end, 0).start()
+
+            @pl.when(step == STEPS - 1)
+            def _():
+                put(grad_out, slot, far_end, 0).start()
 
         @pl.when(step == STEPS)
         def _():
-            put(grad_in, 1 - slot, step - 1).wait()
+            put(grad_in, 1 - slot, far_end, 0).wait()
 
     @pl.when(lax.rem(step, 2) == 0)
     def _():
@@ -244,6 +259,10 @@
     @pl.when(step == STEPS)
     def _():
         out_ref[...] = acc[...].astype(BF16)
+
+
+def in_hbm(array):
+    return pltpu.with_memory_space_constraint(array, pltpu.HBM)
 
 
 def label_specs():
@@ -314,7 +333,10 @@
     return pl.pallas_call(
         second_kernel,
         out_shape=(
-            pltpu.HBM((STEPS, TILE, DOCS), BF16),
+            pltpu.HBM((STEPS // 2 - 1, TILE, DOCS), BF16),
+            pltpu.HBM((1, TILE, DOCS), BF16),
+            pltpu.HBM((STEPS // 2 - 1, TILE, DOCS), BF16),
+            pltpu.HBM((1, TILE, DOCS), BF16),
             pltpu.HBM((DOCS, D), BF16),
         ),
         grid=(STEPS + 1,),
@@ -327,6 +349,9 @@
         ],
         out_specs=(
             pl.BlockSpec(memory_space=pl.ANY),
+            pl.BlockSpec(memory_space=pl.ANY),
+            pl.BlockSpec(memory_space=pl.ANY),
+            pl.BlockSpec(memory_space=pl.ANY),
             pl.BlockSpec((DOCS, D), lambda s: (0, 0)),
         ),
         scratch_shapes=[
@@ -344,7 +369,7 @@
             flops=2 * NB * LAB * DOCS * D, bytes_accessed=20 << 20, transcendentals=0
         ),
         name="second_pass",
-    )(*labels, exps, tops, log_total, hits)
+    )(*labels, in_hbm(exps), tops, log_total, in_hbm(hits))
 
 
 def spread(chunks):
@@ -393,7 +418,6 @@
     hidden = jax.nn.gelu(pre_act, approximate=False).astype(BF16)
     partial_out = jnp.dot(hidden, down_all, preferred_element_type=F32).astype(BF16)
     parts = spread(partial_out.reshape(8, DOCS // 8, D))
-    parts, x_low, x_high = lax.optimization_barrier((parts, x_low, x_high))
     own_docs = lax.dynamic_slice_in_dim(docs, z * (DOCS // 8), DOCS // 8, 0)
     own_emb = (own_docs.astype(F32) + total(parts)).astype(BF16)
     x_far_a = move(x_low[: 2 * BLK], "x", 4, 1)
@@ -405,7 +429,7 @@
     embedding = everywhere(own_emb).reshape(DOCS, D)
     near = [column, x_low, x_high, x_far_a, x_far_b]
     far = [c_column, c_low, c_high, c_far_a, c_far_b]
-    labels = [part.reshape(-1, BLK, D) for part in near + far]
+    labels = [in_hbm(part.reshape(-1, BLK, D)) for part in near + far]
 
     which = jnp.arange(NB, dtype=I32)
     rel = jnp.array(REL, I32)
@@ -414,7 +438,7 @@
     b_y = (yh * 2 + yl + rel[which & 3]) % 4
     bases = (((((b_y >> 1) * 4 + b_x) * 2 + b_core) * 16) + z * 2 + (b_y & 1)) * LAB
 
-    exps, tops, stats = first_pass(labels, embedding)
+    exps, tops, stats = first_pass(labels, in_hbm(embedding))
     all_stats = everywhere(stats)
     maxes, sums = all_stats[:, :4], all_stats[:, 4:]
     row_top = jnp.max(maxes, axis=0)
@@ -422,19 +446,20 @@
     log_total = (row_top + jnp.log(row_total)).reshape(1, DOCS)
     positives = lax.dynamic_slice_in_dim(positive_cols, yl * DOCS, DOCS, 0).T
     hits = positive_hits(bases, positives)
-    grads, embed_part = second_pass(labels, exps, tops, log_total, hits)
+    near_grads, near_end, far_grads, far_end, embed_part = second_pass(labels, exps, tops, log_total, hits)
 
     back = spread(embed_part.reshape(8, DOCS // 8, D))
     own_grad = total(back).astype(BF16)
     embed_grad = everywhere(own_grad).reshape(DOCS, D)
 
-    far_all = jnp.dot(grads[4:].reshape(-1, DOCS), embedding, preferred_element_type=F32).astype(BF16)
-    far_all = move(far_all, "core", 2, 1)
-    far_all = far_all.reshape(4, TILE, D)
-    near_term = jnp.dot(grads[3], embedding, preferred_element_type=F32)
-    last_sum = (near_term + far_all[3].astype(F32)).astype(BF16)
-    near_term = jnp.dot(grads[:3].reshape(-1, DOCS), embedding, preferred_element_type=F32)
-    rest = (near_term + far_all[:3].reshape(-1, D).astype(F32)).astype(BF16).reshape(3, TILE, D)
+    far_last = jnp.dot(far_end[0], embedding, preferred_element_type=F32).astype(BF16)
+    far_last = move(far_last, "core", 2, 1)
+    far_rest = jnp.dot(far_grads.reshape(-1, DOCS), embedding, preferred_element_type=F32).astype(BF16)
+    far_rest = move(far_rest, "core", 2, 1)
+    near_term = jnp.dot(near_end[0], embedding, preferred_element_type=F32)
+    last_sum = (near_term + far_last.astype(F32)).astype(BF16)
+    near_term = jnp.dot(near_grads.reshape(-1, DOCS), embedding, preferred_element_type=F32)
+    rest = (near_term + far_rest.astype(F32)).astype(BF16).reshape(3, TILE, D)
     sums = [rest[0], rest[1], rest[2], last_sum]
     half = TILE // 2
     low_a = move(sums[3][:half], "x", 4, 1)
@@ -459,12 +484,12 @@
     terms = jnp.stack(pieces).reshape(2, 8, 2, rows, 2 * units)
     keep = jnp.where(core == 0, terms[:, :, 0], terms[:, :, 1])
     give = jnp.where(core == 0, terms[:, :, 1], terms[:, :, 0])
-    give, up_lo, up_hi, down_lo, down_hi = lax.optimization_barrier((give, up_lo, up_hi, down_lo, down_hi))
     given = move(give, "core", 2, 1)
     both = add(keep, given).astype(BF16)
     both = jnp.swapaxes(both, 0, 1).reshape(16, rows, 2 * units)
     mlp = total(lax.all_to_all(both, ("yh", "x", "yl"), 0, 0))
 
+    half = TILE // 2
     lo = (add(sums[0][:half], up_lo) + down_lo.astype(F32)).astype(BF16)
     hi = (add(sums[0][half:], up_hi) + down_hi.astype(F32)).astype(BF16)
     y_sums = [lo[:LAB], lo[LAB:], hi[:LAB], hi[LAB:]]

time: 252 us -> 234 us (0.929)
  waiting for transfers between devices: 117 us -> 90.5 us
  local copies, waits for them, and re-layouts: 19.9 us -> 12.5 us
  Pallas kernels: 26.1 us -> 32.9 us
  matrix products: 19.2 us -> 23.1 us
  starting transfers between devices: 59.4 us -> 62.3 us
    ppermute x27 -> x28, waiting for transfers between devices: 75.5 us -> 57.1 us  [move(): lax.ppermute(block, axes, [(i, (i + distance) % size) for i in range(size)])]
    all_to_all x5, waiting for transfers between devices: 41.5 us -> 33.4 us  [spread(): return lax.all_to_all(chunks, 'z', 0, 0)]
    unnamed x34 -> x48, local copies, waits for them, and re-layouts: 8.85 us -> 1.83 us
    ppermute x27 -> x28, starting transfers between devices: 25.1 us -> 30.4 us  [move(): lax.ppermute(block, axes, [(i, (i + distance) % size) for i in range(size)])]
    pallas_call x1, Pallas kernels: 8.87 us -> 13.7 us  [second_pass(): pl.pallas_call(second_kernel, out_shape=(pltpu.HBM((STEPS // 2 - 1, TILE,...]
    slice x3 -> x1, local copies, waits for them, and re-layouts: 4.52 us -> 0.8 us  [step_of(): low_a = move(sums[3][:half], 'x', 4, 1)]
    another operation x2, local copies, waits for them, and re-layouts: 0.34 us -> 3.82 us
    all_to_all x5, starting transfers between devices: 29.1 us -> 26.1 us  [spread(): return lax.all_to_all(chunks, 'z', 0, 0)]
  transfers between devices with their start and end apart: 33 -> 34, of which waited for: 20 -> 20; matrix products, arithmetic and copies ran while one was open for 13% -> 13% of each run, Pallas kernels for 3% -> 3%
where the time goes in v2:
time: 234 us; the launch traced here: 232 us
  waiting for transfers between devices  90.5 us (39%)
  starting transfers between devices  62.3 us (27%)
  Pallas kernels  32.9 us (14%)
  matrix products  23.1 us (10%)
  local copies, waits for them, and re-layouts  12.5 us (5%)
  other arithmetic  10 us (4%)
    ppermute x28, waiting for transfers between devices, move(): lax.ppermute(block, axes, [(i, (i + distance) % size) for i in range(size)])  57.1 us
    all_to_all x5, waiting for transfers between devices, spread(): return lax.all_to_all(chunks, 'z', 0, 0)  33.4 us
    ppermute x28, starting transfers between devices, move(): lax.ppermute(block, axes, [(i, (i + distance) % size) for i in range(size)])  30.4 us
    all_to_all x5, starting transfers between devices, spread(): return lax.all_to_all(chunks, 'z', 0, 0)  26.1 us
    pallas_call x1, Pallas kernels, second_pass(): pl.pallas_call(second_kernel, out_shape=(pltpu.HBM((STEPS // 2 - 1, TILE,...  13.7 us
    pallas_call x1, Pallas kernels, first_pass(): pl.pallas_call(first_kernel, out_shape=(pltpu.HBM((STEPS, TILE, DOCS), F3...  12.4 us
    pallas_call x1, Pallas kernels, positive_hits(): pl.pallas_call(hits_kernel, out_shape=pltpu.HBM((STEPS, TILE, DOCS), BF16...  6.78 us
    all_to_all x1, starting transfers between devices, step_of(): mlp = total(lax.all_to_all(both, ('yh', 'x', 'yl'), 0, 0))  5.8 us
  transfers between devices with their start and end apart: 34, of which 20 were waited for; matrix products, arithmetic and copies ran while one was open for 13% of the time, Pallas kernels for 3%

profile of v2, /device:TPU:2, one launch (start us, length us, event | category | flops | bytes accessed | tf_op | source)
XLA Modules:
  0.0 232.4 jit_solution(5877883997684552001)
XLA Ops:
  3.3 7.3 %collective-permute-done.13 = bf16[192,768]{1,0:T(8,128)(2,1)S(1)} collective-permute-done((bf16[192,768]{1,0:T(8,128)(2,1)S(1)}, bf16[192,768]{1,0:T(8,128)(2,1)S(1)}, u32[]{:S(2)}, u32[]{:S(2)}) %collective-permute-start.13) | collective-permute-done | bytes 294944 | tf_op jit(solution)/shard_map/ppermute | solution.py:30
  18.7 8.5 %all-to-all-start = ((bf16[8,64,768]{2,1,0:T(8,128)(2,1)}), bf16[8,64,768]{2,1,0:T(8,128)(2,1)S(1)}, u32[]{:S(2)}, u32[]{:S(2)}) async-start(bf16[8,64,768]{2,1,0:T(8,128)(2,1)} %bitcast.14), calls=%async_computation | async-start | bytes 1572864 | tf_op jit(solution)/shard_map/all_to_all | solution.py:376
  30.4 4.4 %collective-permute-done.1 = bf16[136,768]{1,0:T(8,128)(2,1)S(1)} collective-permute-done((bf16[136,768]{1,0:T(8,128)(2,1)S(1)}, bf16[136,768]{1,0:T(8,128)(2,1)S(1)}, u32[]{:S(2)}, u32[]{:S(2)}) %collective-permute-start.1) | collective-permute-done | bytes 208928 | tf_op jit(solution)/shard_map/ppermute | solution.py:30
  34.9 3.8 %collective-permute-start.3 = (bf16[72,768]{1,0:T(8,128)(2,1)S(1)}, bf16[72,768]{1,0:T(8,128)(2,1)S(1)}, u32[]{:S(2)}, u32[]{:S(2)}) collective-permute-start(bf16[72,768]{1,0:T(8,128)(2,1)S(1)} %slice.281), channel_id=1, source_target_pairs={{0,129},{1,0},{128,1},{129,128},{2,131},{3,2},{130,3},{131,130},{4... | collective-permute-start | bytes 331784 | tf_op jit(solution)/shard_map/ppermute | solution.py:30
  38.8 5.8 %collective-permute-done.2 = bf16[64,768]{1,0:T(8,128)(2,1)S(1)} collective-permute-done((bf16[64,768]{1,0:T(8,128)(2,1)S(1)}, bf16[64,768]{1,0:T(8,128)(2,1)S(1)}, u32[]{:S(2)}, u32[]{:S(2)}) %collective-permute-start.2) | collective-permute-done | bytes 98336 | tf_op jit(solution)/shard_map/ppermute | solution.py:30
  46.7 3.9 %all-to-all-done = bf16[8,64,768]{2,1,0:T(8,128)(2,1)S(1)} async-done(((bf16[8,64,768]{2,1,0:T(8,128)(2,1)}), bf16[8,64,768]{2,1,0:T(8,128)(2,1)S(1)}, u32[]{:S(2)}, u32[]{:S(2)}) %all-to-all-start) | async-done | bytes 786464 | tf_op jit(solution)/shard_map/all_to_all | solution.py:376
  52.6 4.2 %all-to-all-start.1 = ((bf16[8,64,768]{2,1,0:T(8,128)(2,1)}), bf16[8,64,768]{2,1,0:T(8,128)(2,1)}, u32[]{:S(2)}, u32[]{:S(2)}) async-start(bf16[8,64,768]{2,1,0:T(8,128)(2,1)} %broadcast_in_dim.8), calls=%async_computation.1 | async-start | bytes 1572864 | tf_op jit(solution)/shard_map/all_to_all | solution.py:376
  57.0 6.4 %collective-permute-done.5 = bf16[544,768]{1,0:T(8,128)(2,1)S(1)} collective-permute-done((bf16[544,768]{1,0:T(8,128)(2,1)S(1)}, bf16[544,768]{1,0:T(8,128)(2,1)S(1)}, u32[]{:S(2)}, u32[]{:S(2)}) %collective-permute-start.5) | collective-permute-done | bytes 835616 | tf_op jit(solution)/shard_map/ppermute | solution.py:30
  66.1 6.0 %collective-permute-done.7 = bf16[272,768]{1,0:T(8,128)(2,1)} collective-permute-done((bf16[272,768]{1,0:T(8,128)(2,1)S(1)}, bf16[272,768]{1,0:T(8,128)(2,1)}, u32[]{:S(2)}, u32[]{:S(2)}) %collective-permute-start.7) | collective-permute-done | bytes 417824 | tf_op jit(solution)/shard_map/ppermute | solution.py:30
  76.5 3.9 %all-to-all-done.1 = bf16[8,64,768]{2,1,0:T(8,128)(2,1)} async-done(((bf16[8,64,768]{2,1,0:T(8,128)(2,1)}), bf16[8,64,768]{2,1,0:T(8,128)(2,1)}, u32[]{:S(2)}, u32[]{:S(2)}) %all-to-all-start.1) | async-done | bytes 786464 | tf_op jit(solution)/shard_map/all_to_all | solution.py:376
  80.4 12.4 %first_pass.1 = (f32[8,512,512]{2,1,0:T(8,128)}, f32[8,1,512]{2,1,0:T(1,128)S(1)}, f32[8,128]{1,0:T(8,128)S(1)}) custom-call(bf16[4,136,768]{2,1,0:T(8,128)(2,1)} %bitcast.128, bf16[4,136,768]{2,1,0:T(8,128)(2,1)} %bitcast.124, bf16[4,136,768]{2,1,0:T(8,128)(2,1)} %bitcast.122, bf16[2,136,768]{2,1,0:T(8,128)(2,1)} %bitcast.6.refs_3_, ...), custom_call_target="tpu_custom_call" | custom-call | flops 3221225472 | bytes 16777216 | tf_op jit(solution)/shard_map/first_pass/pallas_call | solution.py:273
  93.4 3.3 %all-to-all-start.2 = ((f32[8,8,128]{2,1,0:T(8,128)}), f32[8,8,128]{2,1,0:T(8,128)S(1)}, u32[]{:S(2)}, u32[]{:S(2)}) async-start(f32[8,8,128]{2,1,0:T(8,128)} %broadcast_in_dim.9), calls=%async_computation.2 | async-start | bytes 65536 | tf_op jit(solution)/shard_map/all_to_all | solution.py:376
  97.3 6.8 %positive_hits.1.refs_13_ = bf16[8,512,512]{2,1,0:T(8,128)(2,1)} custom-call(s32[32]{0:T(128)} %add_multiply_fusion.base_ref, s32[4,512]{1,0:T(4,128)} %dynamic-slice_bitcast_fusion.pos_ref), custom_call_target="tpu_custom_call" | custom-call | flops 33554432 | bytes 4194304 | tf_op jit(solution)/shard_map/positive_hits/pallas_call | solution.py:314
  104.8 13.7 %second_pass.1 = (bf16[3,512,512]{2,1,0:T(8,128)(2,1)}, bf16[1,512,512]{2,1,0:T(8,128)(2,1)}, bf16[3,512,512]{2,1,0:T(8,128)(2,1)}, bf16[1,512,512]{2,1,0:T(8,128)(2,1)}, bf16[512,768]{1,0:T(8,128)(2,1)}) custom-call(bf16[4,136,768]{2,1,0:T(8,128)(2,1)} %bitcast.129, bf16[4,136,768]{2,1,0:T(8,128)(2,1)} %bitcast.125, bf16[4,136,768]{2,1,0:T(8,128)(2,1)} %bitcast.123, ...), custom_call_target="tpu_custom_call" | custom-call | flops 3221225472 | bytes 20971520 | tf_op jit(solution)/shard_map/second_pass/pallas_call | solution.py:333
  118.5 4.4 %convolution_convert_fusion = bf16[1536,768]{1,0:T(8,128)(2,1)} fusion(bf16[1536,512]{1,0:T(8,128)(2,1)} %bitcast.133, bf16[512,768]{1,0:T(8,128)(2,1)} %bitcast.16.refs_10_), kind=kOutput, calls=%fused_computation.1 | convolution fusion | flops 1209139200 | bytes 4718592 | tf_op jit(solution)/shard_map/dot_general | solution.py:457
  122.9 6.5 %all-to-all-start.3 = ((bf16[8,64,768]{2,1,0:T(8,128)(2,1)}), bf16[8,64,768]{2,1,0:T(8,128)(2,1)S(1)}, u32[]{:S(2)}, u32[]{:S(2)}) async-start(bf16[8,64,768]{2,1,0:T(8,128)(2,1)} %bitcast.25), calls=%async_computation.3 | async-start | bytes 1572864 | tf_op jit(solution)/shard_map/all_to_all | solution.py:376
  132.4 20.8 %all-to-all-done.3 = bf16[8,64,768]{2,1,0:T(8,128)(2,1)S(1)} async-done(((bf16[8,64,768]{2,1,0:T(8,128)(2,1)}), bf16[8,64,768]{2,1,0:T(8,128)(2,1)S(1)}, u32[]{:S(2)}, u32[]{:S(2)}) %all-to-all-start.3) | async-done | bytes 786464 | tf_op jit(solution)/shard_map/all_to_all | solution.py:376
  154.3 3.5 %all-to-all-start.4 = ((bf16[8,64,768]{2,1,0:T(8,128)(2,1)}), bf16[8,64,768]{2,1,0:T(8,128)(2,1)S(1)}, u32[]{:S(2)}, u32[]{:S(2)}) async-start(bf16[8,64,768]{2,1,0:T(8,128)(2,1)} %broadcast_in_dim.11), calls=%async_computation.4 | async-start | bytes 1572864 | tf_op jit(solution)/shard_map/all_to_all | solution.py:376
  165.7 6.8 %collective-permute-done.17 = bf16[256,768]{1,0:T(8,128)(2,1)S(1)} collective-permute-done((bf16[256,768]{1,0:T(8,128)(2,1)S(1)}, bf16[256,768]{1,0:T(8,128)(2,1)S(1)}, u32[]{:S(2)}, u32[]{:S(2)}) %collective-permute-start.17) | collective-permute-done | bytes 393248 | tf_op jit(solution)/shard_map/ppermute | solution.py:30
  177.4 4.1 %all-to-all-done.4 = bf16[8,64,768]{2,1,0:T(8,128)(2,1)S(1)} async-done(((bf16[8,64,768]{2,1,0:T(8,128)(2,1)}), bf16[8,64,768]{2,1,0:T(8,128)(2,1)S(1)}, u32[]{:S(2)}, u32[]{:S(2)}) %all-to-all-start.4) | async-done | bytes 786464 | tf_op jit(solution)/shard_map/all_to_all | solution.py:376
  188.8 3.2 %collective-permute-start.22 = (bf16[256,768]{1,0:T(8,128)(2,1)}, bf16[256,768]{1,0:T(8,128)(2,1)}, u32[]{:S(2)}, u32[]{:S(2)}) collective-permute-start(bf16[256,768]{1,0:T(8,128)(2,1)} %get-tuple-element.24), channel_id=1, source_target_pairs={{0,96},{32,0},{64,32},{96,64},{1,97},{33,1},{65,33},{97,65},{2,98}... | collective-permute-start | bytes 1179656 | tf_op jit(solution)/shard_map/ppermute | solution.py:30
  206.1 3.7 %collective-permute-start.26 = (bf16[128,768]{1,0:T(8,128)(2,1)S(1)}, bf16[128,768]{1,0:T(8,128)(2,1)S(1)}, u32[]{:S(2)}, u32[]{:S(2)}) collective-permute-start(bf16[128,768]{1,0:T(8,128)(2,1)S(1)} %pad_maximum_fusion.7), channel_id=1, source_target_pairs={{0,129},{1,0},{128,1},{129,128},{2,131},{3,2},{130,3},{131,130},{4... | collective-permute-start | bytes 589832 | tf_op jit(solution)/shard_map/ppermute | solution.py:30
  211.7 5.8 %all-to-all-start.5 = ((bf16[16,48,384]{2,1,0:T(8,128)(2,1)}), bf16[16,48,384]{2,1,0:T(8,128)(2,1)S(1)}, u32[]{:S(2)}, u32[]{:S(2)}) async-start(bf16[16,48,384]{2,1,0:T(8,128)(2,1)} %bitcast.44), calls=%async_computation.5 | async-start | bytes 1179648 | tf_op jit(solution)/shard_map/all_to_all | solution.py:490
  219.1 11.8 %collective-permute-done.24 = bf16[128,768]{1,0:T(8,128)(2,1)S(1)} collective-permute-done((bf16[128,768]{1,0:T(8,128)(2,1)S(1)}, bf16[128,768]{1,0:T(8,128)(2,1)S(1)}, u32[]{:S(2)}, u32[]{:S(2)}) %collective-permute-start.24) | collective-permute-done | bytes 196640 | tf_op jit(solution)/shard_map/ppermute | solution.py:30
  (148 shorter events, 70.3 us)
Async XLA Ops:
  1.7 8.9 %collective-permute-start.13 = (bf16[192,768]{1,0:T(8,128)(2,1)S(1)}, bf16[192,768]{1,0:T(8,128)(2,1)S(1)}, u32[]{:S(2)}, u32[]{:S(2)}) collective-permute-start(bf16[192,768]{1,0:T(8,128)(2,1)S(1)} %bitcast_select_fusion.4), channel_id=1, source_target_pairs={{0,1},{1,0},{2,3},{3,2},{4,5},{5,4},{6,7},{7,6},{8,9},{9,8},{10,11... | collective-permute-start | bytes 884744 | tf_op jit(solution)/shard_map/ppermute | solution.py:30
  18.7 31.9 %all-to-all-start = ((bf16[8,64,768]{2,1,0:T(8,128)(2,1)}), bf16[8,64,768]{2,1,0:T(8,128)(2,1)S(1)}, u32[]{:S(2)}, u32[]{:S(2)}) async-start(bf16[8,64,768]{2,1,0:T(8,128)(2,1)} %bitcast.14), calls=%async_computation | async-start | bytes 1572864 | tf_op jit(solution)/shard_map/all_to_all | solution.py:376
  34.9 9.7 %collective-permute-start.3 = (bf16[72,768]{1,0:T(8,128)(2,1)S(1)}, bf16[72,768]{1,0:T(8,128)(2,1)S(1)}, u32[]{:S(2)}, u32[]{:S(2)}) collective-permute-start(bf16[72,768]{1,0:T(8,128)(2,1)S(1)} %slice.281), channel_id=1, source_target_pairs={{0,129},{1,0},{128,1},{129,128},{2,131},{3,2},{130,3},{131,130},{4... | collective-permute-start | bytes 331784 | tf_op jit(solution)/shard_map/ppermute | solution.py:30
  44.6 18.7 %collective-permute-start.5 = (bf16[544,768]{1,0:T(8,128)(2,1)S(1)}, bf16[544,768]{1,0:T(8,128)(2,1)S(1)}, u32[]{:S(2)}, u32[]{:S(2)}) collective-permute-start(bf16[544,768]{1,0:T(8,128)(2,1)S(1)} %constant_dynamic-update-slice_fusion), channel_id=1, source_target_pairs={{0,96},{32,0},{64,32},{96,64},{1,97},{33,1},{65,33},{97,65},{2,98}... | collective-permute-start | bytes 2506760 | tf_op jit(solution)/shard_map/ppermute | solution.py:30
  45.2 19.1 %collective-permute-start.4 = (bf16[544,768]{1,0:T(8,128)(2,1)S(1)}, bf16[544,768]{1,0:T(8,128)(2,1)S(1)}, u32[]{:S(2)}, u32[]{:S(2)}) collective-permute-start(bf16[544,768]{1,0:T(8,128)(2,1)S(1)} %constant_dynamic-update-slice_fusion), channel_id=1, source_target_pairs={{0,32},{32,64},{64,96},{96,0},{1,33},{33,65},{65,97},{97,1},{2,34}... | collective-permute-start | bytes 2506760 | tf_op jit(solution)/shard_map/ppermute | solution.py:30
  52.6 27.8 %all-to-all-start.1 = ((bf16[8,64,768]{2,1,0:T(8,128)(2,1)}), bf16[8,64,768]{2,1,0:T(8,128)(2,1)}, u32[]{:S(2)}, u32[]{:S(2)}) async-start(bf16[8,64,768]{2,1,0:T(8,128)(2,1)} %broadcast_in_dim.8), calls=%async_computation.1 | async-start | bytes 1572864 | tf_op jit(solution)/shard_map/all_to_all | solution.py:376
  56.9 18.2 %collective-permute-start.8 = (bf16[544,768]{1,0:T(8,128)(2,1)S(1)}, bf16[544,768]{1,0:T(8,128)(2,1)S(1)}, u32[]{:S(2)}, u32[]{:S(2)}) collective-permute-start(bf16[544,768]{1,0:T(8,128)(2,1)S(1)} %constant_dynamic-update-slice_fusion), channel_id=1, source_target_pairs={{0,16},{16,0},{1,17},{17,1},{2,18},{18,2},{3,19},{19,3},{4,20},{20... | collective-permute-start | bytes 2506760 | tf_op jit(solution)/shard_map/ppermute | solution.py:30
  64.3 10.1 %collective-permute-start.6 = (bf16[272,768]{1,0:T(8,128)(2,1)S(1)}, bf16[272,768]{1,0:T(8,128)(2,1)}, u32[]{:S(2)}, u32[]{:S(2)}) collective-permute-start(bf16[272,768]{1,0:T(8,128)(2,1)S(1)} %slice.282), channel_id=1, source_target_pairs={{0,32},{32,64},{64,96},{96,0},{1,33},{33,65},{65,97},{97,1},{2,34}... | collective-permute-start | bytes 1253384 | tf_op jit(solution)/shard_map/ppermute | solution.py:30
  65.6 9.5 %collective-permute-start.10 = (bf16[544,768]{1,0:T(8,128)(2,1)S(1)}, bf16[544,768]{1,0:T(8,128)(2,1)}, u32[]{:S(2)}, u32[]{:S(2)}) collective-permute-start(bf16[544,768]{1,0:T(8,128)(2,1)S(1)} %collective-permute-done.5), channel_id=1, source_target_pairs={{0,16},{16,0},{1,17},{17,1},{2,18},{18,2},{3,19},{19,3},{4,20},{20... | collective-permute-start | bytes 2506760 | tf_op jit(solution)/shard_map/ppermute | solution.py:30
  65.6 10.9 %collective-permute-start.9 = (bf16[544,768]{1,0:T(8,128)(2,1)S(1)}, bf16[544,768]{1,0:T(8,128)(2,1)}, u32[]{:S(2)}, u32[]{:S(2)}) collective-permute-start(bf16[544,768]{1,0:T(8,128)(2,1)S(1)} %collective-permute-done.4), channel_id=1, source_target_pairs={{0,16},{16,0},{1,17},{17,1},{2,18},{18,2},{3,19},{19,3},{4,20},{20... | collective-permute-start | bytes 2506760 | tf_op jit(solution)/shard_map/ppermute | solution.py:30
  93.4 11.3 %all-to-all-start.2 = ((f32[8,8,128]{2,1,0:T(8,128)}), f32[8,8,128]{2,1,0:T(8,128)S(1)}, u32[]{:S(2)}, u32[]{:S(2)}) async-start(f32[8,8,128]{2,1,0:T(8,128)} %broadcast_in_dim.9), calls=%async_computation.2 | async-start | bytes 65536 | tf_op jit(solution)/shard_map/all_to_all | solution.py:376
  122.9 40.2 %collective-permute-start.15 = (bf16[1536,768]{1,0:T(8,128)(2,1)}, bf16[1536,768]{1,0:T(8,128)(2,1)S(1)}, u32[]{:S(2)}, u32[]{:S(2)}) collective-permute-start(bf16[1536,768]{1,0:T(8,128)(2,1)} %convolution_convert_fusion), channel_id=1, source_target_pairs={{0,16},{16,0},{1,17},{17,1},{2,18},{18,2},{3,19},{19,3},{4,20},{20... | collective-permute-start | bytes 7077896 | tf_op jit(solution)/shard_map/ppermute | solution.py:30
  122.9 30.3 %all-to-all-start.3 = ((bf16[8,64,768]{2,1,0:T(8,128)(2,1)}), bf16[8,64,768]{2,1,0:T(8,128)(2,1)S(1)}, u32[]{:S(2)}, u32[]{:S(2)}) async-start(bf16[8,64,768]{2,1,0:T(8,128)(2,1)} %bitcast.25), calls=%async_computation.3 | async-start | bytes 1572864 | tf_op jit(solution)/shard_map/all_to_all | solution.py:376
  132.2 25.7 %collective-permute-start.16 = (bf16[512,768]{1,0:T(8,128)(2,1)}, bf16[512,768]{1,0:T(8,128)(2,1)}, u32[]{:S(2)}, u32[]{:S(2)}) collective-permute-start(bf16[512,768]{1,0:T(8,128)(2,1)} %convolution_convert_fusion.1), channel_id=1, source_target_pairs={{0,16},{16,0},{1,17},{17,1},{2,18},{18,2},{3,19},{19,3},{4,20},{20... | collective-permute-start | bytes 2359304 | tf_op jit(solution)/shard_map/ppermute | solution.py:30
  154.3 27.1 %all-to-all-start.4 = ((bf16[8,64,768]{2,1,0:T(8,128)(2,1)}), bf16[8,64,768]{2,1,0:T(8,128)(2,1)S(1)}, u32[]{:S(2)}, u32[]{:S(2)}) async-start(bf16[8,64,768]{2,1,0:T(8,128)(2,1)} %broadcast_in_dim.11), calls=%async_computation.4 | async-start | bytes 1572864 | tf_op jit(solution)/shard_map/all_to_all | solution.py:376
  160.9 11.5 %collective-permute-start.17 = (bf16[256,768]{1,0:T(8,128)(2,1)S(1)}, bf16[256,768]{1,0:T(8,128)(2,1)S(1)}, u32[]{:S(2)}, u32[]{:S(2)}) collective-permute-start(bf16[256,768]{1,0:T(8,128)(2,1)S(1)} %get-tuple-element.31), channel_id=1, source_target_pairs={{0,32},{32,64},{64,96},{96,0},{1,33},{33,65},{65,97},{97,1},{2,34}... | collective-permute-start | bytes 1179656 | tf_op jit(solution)/shard_map/ppermute | solution.py:30
  162.4 23.4 %collective-permute-start.21 = (bf16[256,768]{1,0:T(8,128)(2,1)}, bf16[256,768]{1,0:T(8,128)(2,1)}, u32[]{:S(2)}, u32[]{:S(2)}) collective-permute-start(bf16[256,768]{1,0:T(8,128)(2,1)} %get-tuple-element.32), channel_id=1, source_target_pairs={{0,96},{32,0},{64,32},{96,64},{1,97},{33,1},{65,33},{97,65},{2,98}... | collective-permute-start | bytes 1179656 | tf_op jit(solution)/shard_map/ppermute | solution.py:30
  173.4 13.2 %collective-permute-start.18 = (bf16[256,768]{1,0:T(8,128)(2,1)}, bf16[256,768]{1,0:T(8,128)(2,1)}, u32[]{:S(2)}, u32[]{:S(2)}) collective-permute-start(bf16[256,768]{1,0:T(8,128)(2,1)} %add_convert_fusion.6), channel_id=1, source_target_pairs={{0,32},{32,64},{64,96},{96,0},{1,33},{33,65},{65,97},{97,1},{2,34}... | collective-permute-start | bytes 1179656 | tf_op jit(solution)/shard_map/ppermute | solution.py:30
  175.3 11.3 %collective-permute-start.19 = (bf16[256,768]{1,0:T(8,128)(2,1)}, bf16[256,768]{1,0:T(8,128)(2,1)}, u32[]{:S(2)}, u32[]{:S(2)}) collective-permute-start(bf16[256,768]{1,0:T(8,128)(2,1)} %get-tuple-element.25), channel_id=1, source_target_pairs={{0,96},{32,0},{64,32},{96,64},{1,97},{33,1},{65,33},{97,65},{2,98}... | collective-permute-start | bytes 1179656 | tf_op jit(solution)/shard_map/ppermute | solution.py:30
  177.3 21.7 %collective-permute-start.20 = (bf16[256,768]{1,0:T(8,128)(2,1)}, bf16[256,768]{1,0:T(8,128)(2,1)}, u32[]{:S(2)}, u32[]{:S(2)}) collective-permute-start(bf16[256,768]{1,0:T(8,128)(2,1)} %get-tuple-element.26), channel_id=1, source_target_pairs={{0,32},{32,64},{64,96},{96,0},{1,33},{33,65},{65,97},{97,1},{2,34}... | collective-permute-start | bytes 1179656 | tf_op jit(solution)/shard_map/ppermute | solution.py:30
  188.8 10.7 %collective-permute-start.22 = (bf16[256,768]{1,0:T(8,128)(2,1)}, bf16[256,768]{1,0:T(8,128)(2,1)}, u32[]{:S(2)}, u32[]{:S(2)}) collective-permute-start(bf16[256,768]{1,0:T(8,128)(2,1)} %get-tuple-element.24), channel_id=1, source_target_pairs={{0,96},{32,0},{64,32},{96,64},{1,97},{33,1},{65,33},{97,65},{2,98}... | collective-permute-start | bytes 1179656 | tf_op jit(solution)/shard_map/ppermute | solution.py:30
  206.1 12.9 %collective-permute-start.26 = (bf16[128,768]{1,0:T(8,128)(2,1)S(1)}, bf16[128,768]{1,0:T(8,128)(2,1)S(1)}, u32[]{:S(2)}, u32[]{:S(2)}) collective-permute-start(bf16[128,768]{1,0:T(8,128)(2,1)S(1)} %pad_maximum_fusion.7), channel_id=1, source_target_pairs={{0,129},{1,0},{128,1},{129,128},{2,131},{3,2},{130,3},{131,130},{4... | collective-permute-start | bytes 589832 | tf_op jit(solution)/shard_map/ppermute | solution.py:30
  211.7 19.9 %all-to-all-start.5 = ((bf16[16,48,384]{2,1,0:T(8,128)(2,1)}), bf16[16,48,384]{2,1,0:T(8,128)(2,1)S(1)}, u32[]{:S(2)}, u32[]{:S(2)}) async-start(bf16[16,48,384]{2,1,0:T(8,128)(2,1)} %bitcast.44), calls=%async_computation.5 | async-start | bytes 1179648 | tf_op jit(solution)/shard_map/all_to_all | solution.py:490
  217.5 13.3 %collective-permute-start.24 = (bf16[128,768]{1,0:T(8,128)(2,1)S(1)}, bf16[128,768]{1,0:T(8,128)(2,1)S(1)}, u32[]{:S(2)}, u32[]{:S(2)}) collective-permute-start(bf16[128,768]{1,0:T(8,128)(2,1)S(1)} %pad_maximum_fusion.6), channel_id=1, source_target_pairs={{0,1},{1,128},{128,129},{129,0},{2,3},{3,130},{130,131},{131,2},{4... | collective-permute-start | bytes 589832 | tf_op jit(solution)/shard_map/ppermute | solution.py:30
  (32 other events, 276.2 us)

commit v3 on v2

--- a/solution.py
+++ b/solution.py
@@ -21,6 +21,8 @@
 TILE = GRP * LAB
 STEPS = NB // GRP
 DOCS = 512
+DOWN = 384
+ROWS = D // 16
 REL = (0, -1, 1, 2)
 NT = (((1,), (1,)), ((), ()))
 TN = (((0,), (0,)), ((), ()))
@@ -175,8 +177,13 @@
             stat_ref[4 + j : 5 + j, :] = run_sum[:, j * 128 : (j + 1) * 128]
 
 
-def hits_kernel(base_ref, pos_ref, hits_ref):
+def hits_kernel(base_ref, pos_ref, docs_ref, hits_ref, turned_ref):
     step = pl.program_id(0)
+
+    @pl.when(step == 0)
+    def _():
+        turned_ref[...] = docs_ref[...].T
+
     pos = [pos_ref[k : k + 1, :] for k in range(4)]
     weights = []
     for k in range(4):
@@ -273,7 +280,7 @@
     return pl.pallas_call(
         first_kernel,
         out_shape=(
-            pltpu.HBM((STEPS, TILE, DOCS), F32),
+            jax.ShapeDtypeStruct((STEPS, TILE, DOCS), F32),
             jax.ShapeDtypeStruct((STEPS, 1, DOCS), F32),
             jax.ShapeDtypeStruct((8, 128), F32),
         ),
@@ -301,7 +308,7 @@
             pltpu.VMEM((1, DOCS), F32),
         ],
         compiler_params=pltpu.CompilerParams(
-            dimension_semantics=("arbitrary",), vmem_limit_bytes=32 << 20
+            dimension_semantics=("arbitrary",), vmem_limit_bytes=18 << 20
         ),
         cost_estimate=pl.CostEstimate(
             flops=2 * NB * LAB * DOCS * D, bytes_accessed=16 << 20, transcendentals=NB * LAB * DOCS
@@ -310,22 +317,66 @@
     )(*labels, embedding)
 
 
-def positive_hits(bases, positives):
+def positive_hits(bases, positives, documents):
     return pl.pallas_call(
         hits_kernel,
-        out_shape=pltpu.HBM((STEPS, TILE, DOCS), BF16),
+        out_shape=(
+            jax.ShapeDtypeStruct((STEPS, TILE, DOCS), BF16),
+            jax.ShapeDtypeStruct((D, DOCS), BF16),
+        ),
         grid_spec=pltpu.PrefetchScalarGridSpec(
             num_scalar_prefetch=1,
             grid=(STEPS,),
-            in_specs=[pl.BlockSpec((4, DOCS), lambda s, b: (0, 0))],
-            out_specs=pl.BlockSpec((1, TILE, DOCS), lambda s, b: (s, 0, 0)),
+            in_specs=[
+                pl.BlockSpec((4, DOCS), lambda s, b: (0, 0)),
+                pl.BlockSpec((DOCS, D), lambda s, b: (b[NB], 0)),
+            ],
+            out_specs=(
+                pl.BlockSpec((1, TILE, DOCS), lambda s, b: (s, 0, 0)),
+                pl.BlockSpec((D, DOCS), lambda s, b: (0, 0)),
+            ),
         ),
         compiler_params=pltpu.CompilerParams(dimension_semantics=("arbitrary",)),
         cost_estimate=pl.CostEstimate(
             flops=16 * NB * LAB * DOCS, bytes_accessed=4 << 20, transcendentals=0
         ),
         name="positive_hits",
-    )(bases, positives)
+    )(bases, positives, documents)
+
+
+def mlp_kernel(core_ref, grad_ref, down_ref, slope_ref, hidden_ref, turned_ref, keep_ref, give_ref, both):
+    units = DOWN // 2
+    act_grad = lax.dot_general(grad_ref[...], down_ref[...], NT, preferred_element_type=F32)
+    pre_grad = (act_grad * slope_ref[...]).astype(BF16)
+    down_term = lax.dot_general(grad_ref[...], hidden_ref[...], TN, preferred_element_type=F32)
+    up_term = jnp.dot(turned_ref[...], pre_grad, preferred_element_type=F32)
+    for j in range(2):
+        cols = slice(j * units, (j + 1) * units)
+        both[j] = jnp.concatenate([up_term[:, cols], down_term[:, cols]], axis=1).astype(BF16)
+    core = core_ref[0]
+    for q in range(8):
+        for j in range(2):
+            mine = pl.multiple_of((2 * q + core) * ROWS, ROWS)
+            other = pl.multiple_of((2 * q + 1 - core) * ROWS, ROWS)
+            keep_ref[2 * q + j] = both[j, pl.ds(mine, ROWS), :]
+            give_ref[2 * q + j] = both[j, pl.ds(other, ROWS), :]
+
+
+def mlp_back(core, embed_grad, down_all, slope, hidden, turned):
+    shape = jax.ShapeDtypeStruct((16, ROWS, DOWN), BF16)
+    vmem = pl.BlockSpec(memory_space=pltpu.VMEM)
+    return pl.pallas_call(
+        mlp_kernel,
+        out_shape=(shape, shape),
+        in_specs=[pl.BlockSpec(memory_space=pltpu.SMEM)] + [vmem] * 5,
+        out_specs=(vmem, vmem),
+        scratch_shapes=[pltpu.VMEM((2, D, DOWN), BF16)],
+        compiler_params=pltpu.CompilerParams(vmem_limit_bytes=24 << 20),
+        cost_estimate=pl.CostEstimate(
+            flops=6 * DOCS * D * DOWN, bytes_accessed=6 << 20, transcendentals=0
+        ),
+        name="mlp_back",
+    )(core, embed_grad, down_all, slope, hidden, turned)
 
 
 def second_pass(labels, exps, tops, log_total, hits):
@@ -363,13 +414,13 @@
             pltpu.VMEM((DOCS, D), F32),
         ],
         compiler_params=pltpu.CompilerParams(
-            dimension_semantics=("arbitrary",), vmem_limit_bytes=32 << 20
+            dimension_semantics=("arbitrary",), vmem_limit_bytes=18 << 20
         ),
         cost_estimate=pl.CostEstimate(
             flops=2 * NB * LAB * DOCS * D, bytes_accessed=20 << 20, transcendentals=0
         ),
         name="second_pass",
-    )(*labels, in_hbm(exps), tops, log_total, in_hbm(hits))
+    )(*labels, exps, tops, log_total, hits)
 
 
 def spread(chunks):
@@ -415,7 +466,9 @@
 
     docs = lax.dynamic_slice_in_dim(documents, yl * DOCS, DOCS, 0)
     pre_act = lax.dot_general(docs, up_all, NT, preferred_element_type=F32)
-    hidden = jax.nn.gelu(pre_act, approximate=False).astype(BF16)
+    hidden, gelu_pull = jax.vjp(partial(jax.nn.gelu, approximate=False), pre_act)
+    hidden = hidden.astype(BF16)
+    slope = gelu_pull(jnp.ones_like(pre_act))[0]
     partial_out = jnp.dot(hidden, down_all, preferred_element_type=F32).astype(BF16)
     parts = spread(partial_out.reshape(8, DOCS // 8, D))
     own_docs = lax.dynamic_slice_in_dim(docs, z * (DOCS // 8), DOCS // 8, 0)
@@ -445,7 +498,8 @@
     row_total = jnp.sum(sums * jnp.exp(maxes - row_top[None]), axis=0)
     log_total = (row_top + jnp.log(row_total)).reshape(1, DOCS)
     positives = lax.dynamic_slice_in_dim(positive_cols, yl * DOCS, DOCS, 0).T
-    hits = positive_hits(bases, positives)
+    scalars = jnp.concatenate([bases, yl.reshape(1).astype(I32)])
+    hits, turned = positive_hits(scalars, positives, documents)
     near_grads, near_end, far_grads, far_end, embed_part = second_pass(labels, exps, tops, log_total, hits)
 
     back = spread(embed_part.reshape(8, DOCS // 8, D))
@@ -471,22 +525,9 @@
     up_lo = move(up_lo, "x", 4, 1)
     down_hi = move(down_hi, "x", 4, -1)
 
-    act_grad = lax.dot_general(embed_grad, down_all, NT, preferred_element_type=F32)
-    _, gelu_pull = jax.vjp(partial(jax.nn.gelu, approximate=False), pre_act)
-    pre_grad = gelu_pull(act_grad)[0].astype(BF16)
-    pieces = []
-    for j in range(2):
-        cols = slice(j * units, (j + 1) * units)
-        up_term = lax.dot_general(docs, pre_grad[:, cols], TN, preferred_element_type=F32)
-        down_term = lax.dot_general(embed_grad, hidden[:, cols], TN, preferred_element_type=F32)
-        pieces.append(jnp.concatenate([up_term, down_term], axis=1).astype(BF16))
-    rows = D // 16
-    terms = jnp.stack(pieces).reshape(2, 8, 2, rows, 2 * units)
-    keep = jnp.where(core == 0, terms[:, :, 0], terms[:, :, 1])
-    give = jnp.where(core == 0, terms[:, :, 1], terms[:, :, 0])
+    keep, give = mlp_back(core.reshape(1).astype(I32), embed_grad, down_all, slope, hidden, turned)
     given = move(give, "core", 2, 1)
     both = add(keep, given).astype(BF16)
-    both = jnp.swapaxes(both, 0, 1).reshape(16, rows, 2 * units)
     mlp = total(lax.all_to_all(both, ("yh", "x", "yl"), 0, 0))
 
     half = TILE // 2

time: 234 us -> 223 us (0.953)
  waiting for transfers between devices: 90.5 us -> 78.5 us
  matrix products: 23.1 us -> 15.1 us
  local copies, waits for them, and re-layouts: 12.5 us -> 19 us
  starting transfers between devices: 62.3 us -> 65.4 us
    all_to_all x5, waiting for transfers between devices: 33.4 us -> 14.9 us  [spread(): return lax.all_to_all(chunks, 'z', 0, 0)]
    unnamed x48 -> x46, local copies, waits for them, and re-layouts: 1.83 us -> 12.6 us
    dot_general x5 -> x0, matrix products: 6.57 us -> none  [the longest x2 2.54 us: step_of(): lax.dot_general(embed_grad, hidden[:, cols], TN, preferred_element_type=F32)]
    ppermute x28, waiting for transfers between devices: 57.1 us -> 63.6 us  [move(): lax.ppermute(block, axes, [(i, (i + distance) % size) for i in range(size)])]
    all_to_all x5, starting transfers between devices: 26.1 us -> 30.2 us  [spread(): return lax.all_to_all(chunks, 'z', 0, 0)]
    pallas_call x1, Pallas kernels: 13.7 us -> 9.9 us  [second_pass(): pl.pallas_call(second_kernel, out_shape=(pltpu.HBM((STEPS // 2 - 1, TILE,...]
    another operation x2 -> x0, local copies, waits for them, and re-layouts: 3.82 us -> none
    pallas_call x2 -> x3, Pallas kernels: 19.1 us -> 20.7 us  [the longest x1 11.3 us: first_pass(): pl.pallas_call(first_kernel, out_shape=(jax.ShapeDtypeStruct((STEPS, TILE...]
  transfers between devices with their start and end apart: 34 -> 34, of which waited for: 20 -> 17; matrix products, arithmetic and copies ran while one was open for 13% -> 12% of each run, Pallas kernels for 3% -> 4%
where the time goes in v3:
time: 223 us; the launch traced here: 222 us
  waiting for transfers between devices  78.5 us (35%)
  starting transfers between devices  65.4 us (29%)
  Pallas kernels  30.6 us (14%)
  local copies, waits for them, and re-layouts  19 us (9%)
  matrix products  15.1 us (7%)
  other arithmetic  12.2 us (5%)
    ppermute x28, waiting for transfers between devices, move(): lax.ppermute(block, axes, [(i, (i + distance) % size) for i in range(size)])  63.6 us
    all_to_all x5, starting transfers between devices, spread(): return lax.all_to_all(chunks, 'z', 0, 0)  30.2 us
    ppermute x28, starting transfers between devices, move(): lax.ppermute(block, axes, [(i, (i + distance) % size) for i in range(size)])  28.9 us
    all_to_all x5, waiting for transfers between devices, spread(): return lax.all_to_all(chunks, 'z', 0, 0)  14.9 us
    unnamed x46, local copies, waits for them, and re-layouts  12.6 us
    pallas_call x1, Pallas kernels, first_pass(): pl.pallas_call(first_kernel, out_shape=(jax.ShapeDtypeStruct((STEPS, TILE...  11.3 us
    pallas_call x1, Pallas kernels, second_pass(): pl.pallas_call(second_kernel, out_shape=(pltpu.HBM((STEPS // 2 - 1, TILE,...  9.9 us
    pallas_call x1, Pallas kernels, positive_hits(): pl.pallas_call(hits_kernel, out_shape=(jax.ShapeDtypeStruct((STEPS, TILE,...  7.76 us
  transfers between devices with their start and end apart: 34, of which 17 were waited for; matrix products, arithmetic and copies ran while one was open for 12% of the time, Pallas kernels for 4%

profile of v3, /device:TPU:2, one launch (start us, length us, event | category | flops | bytes accessed | tf_op | source)
XLA Modules:
  0.0 221.9 jit_solution(14059816343331195084)
XLA Ops:
  3.3 7.3 %collective-permute-done.13 = bf16[192,768]{1,0:T(8,128)(2,1)S(1)} collective-permute-done((bf16[192,768]{1,0:T(8,128)(2,1)S(1)}, bf16[192,768]{1,0:T(8,128)(2,1)S(1)}, u32[]{:S(2)}, u32[]{:S(2)}) %collective-permute-start.13) | collective-permute-done | bytes 294944 | tf_op jit(solution)/shard_map/ppermute | solution.py:32
  17.2 8.5 %all-to-all-start = ((bf16[8,64,768]{2,1,0:T(8,128)(2,1)}), bf16[8,64,768]{2,1,0:T(8,128)(2,1)S(1)}, u32[]{:S(2)}, u32[]{:S(2)}) async-start(bf16[8,64,768]{2,1,0:T(8,128)(2,1)} %bitcast.14), calls=%async_computation | async-start | bytes 1572864 | tf_op jit(solution)/shard_map/all_to_all | solution.py:427
  29.4 4.8 %collective-permute-done.1 = bf16[136,768]{1,0:T(8,128)(2,1)S(1)} collective-permute-done((bf16[136,768]{1,0:T(8,128)(2,1)S(1)}, bf16[136,768]{1,0:T(8,128)(2,1)S(1)}, u32[]{:S(2)}, u32[]{:S(2)}) %collective-permute-start.1) | collective-permute-done | bytes 208928 | tf_op jit(solution)/shard_map/ppermute | solution.py:32
  34.2 3.8 %collective-permute-start.3 = (bf16[72,768]{1,0:T(8,128)(2,1)S(1)}, bf16[72,768]{1,0:T(8,128)(2,1)S(1)}, u32[]{:S(2)}, u32[]{:S(2)}) collective-permute-start(bf16[72,768]{1,0:T(8,128)(2,1)S(1)} %slice.255), channel_id=1, source_target_pairs={{0,129},{1,0},{128,1},{129,128},{2,131},{3,2},{130,3},{131,130},{4... | collective-permute-start | bytes 331784 | tf_op jit(solution)/shard_map/ppermute | solution.py:32
  39.5 4.4 %collective-permute-done.2 = bf16[64,768]{1,0:T(8,128)(2,1)S(1)} collective-permute-done((bf16[64,768]{1,0:T(8,128)(2,1)S(1)}, bf16[64,768]{1,0:T(8,128)(2,1)S(1)}, u32[]{:S(2)}, u32[]{:S(2)}) %collective-permute-start.2) | collective-permute-done | bytes 98336 | tf_op jit(solution)/shard_map/ppermute | solution.py:32
  51.4 4.7 %all-to-all-start.1 = ((bf16[8,64,768]{2,1,0:T(8,128)(2,1)}), bf16[8,64,768]{2,1,0:T(8,128)(2,1)}, u32[]{:S(2)}, u32[]{:S(2)}) async-start(bf16[8,64,768]{2,1,0:T(8,128)(2,1)} %broadcast_in_dim.8), calls=%async_computation.1 | async-start | bytes 1572864 | tf_op jit(solution)/shard_map/all_to_all | solution.py:427
  56.1 8.0 %collective-permute-done.5 = bf16[544,768]{1,0:T(8,128)(2,1)S(1)} collective-permute-done((bf16[544,768]{1,0:T(8,128)(2,1)}, bf16[544,768]{1,0:T(8,128)(2,1)S(1)}, u32[]{:S(2)}, u32[]{:S(2)}) %collective-permute-start.5) | collective-permute-done | bytes 835616 | tf_op jit(solution)/shard_map/ppermute | solution.py:32
  67.9 5.4 %collective-permute-done.7 = bf16[272,768]{1,0:T(8,128)(2,1)S(1)} collective-permute-done((bf16[272,768]{1,0:T(8,128)(2,1)S(1)}, bf16[272,768]{1,0:T(8,128)(2,1)S(1)}, u32[]{:S(2)}, u32[]{:S(2)}) %collective-permute-start.7) | collective-permute-done | bytes 417824 | tf_op jit(solution)/shard_map/ppermute | solution.py:32
  73.3 3.6 %collective-permute-done.6 = bf16[272,768]{1,0:T(8,128)(2,1)} collective-permute-done((bf16[272,768]{1,0:T(8,128)(2,1)S(1)}, bf16[272,768]{1,0:T(8,128)(2,1)}, u32[]{:S(2)}, u32[]{:S(2)}) %collective-permute-start.6) | collective-permute-done | bytes 417824 | tf_op jit(solution)/shard_map/ppermute | solution.py:32
  79.3 11.3 %first_pass.1 = (f32[8,512,512]{2,1,0:T(8,128)S(1)}, f32[8,1,512]{2,1,0:T(1,128)S(1)}, f32[8,128]{1,0:T(8,128)S(1)}) custom-call(bf16[4,136,768]{2,1,0:T(8,128)(2,1)} %bitcast.3.refs_0_, bf16[4,136,768]{2,1,0:T(8,128)(2,1)} %bitcast.4.refs_1_, bf16[4,136,768]{2,1,0:T(8,128)(2,1)} %bitcast.75, bf16[2,136,768]{2,1,0:T(8,128)(2,1)} %bitcast.6.refs_3_, ...), custom_call_target="tpu_custom_call" | custom-call | flops 3221225472 | bytes 16777216 | tf_op jit(solution)/shard_map/first_pass/pallas_call | solution.py:280
  94.5 6.3 %all-to-all-start.2 = ((f32[8,8,128]{2,1,0:T(8,128)}), f32[8,8,128]{2,1,0:T(8,128)S(1)}, u32[]{:S(2)}, u32[]{:S(2)}) async-start(f32[8,8,128]{2,1,0:T(8,128)} %broadcast_in_dim.9), calls=%async_computation.2 | async-start | bytes 65536 | tf_op jit(solution)/shard_map/all_to_all | solution.py:427
  101.4 7.8 %positive_hits.1 = (bf16[8,512,512]{2,1,0:T(8,128)(2,1)}, bf16[768,512]{1,0:T(8,128)(2,1)}) custom-call(s32[33]{0:T(128)} %pad_add_fusion.base_ref, s32[4,512]{1,0:T(4,128)} %dynamic-slice_bitcast_fusion.pos_ref, bf16[1024,768]{1,0:T(8,128)(2,1)} %docs_ref.1), custom_call_target="tpu_custom_call" | custom-call | flops 33554432 | bytes 4194304 | tf_op jit(solution)/shard_map/positive_hits/pallas_call | solution.py:321
  109.3 3.4 %copy-done.2 = f32[8,512,512]{2,1,0:T(8,128)S(1)} copy-done((f32[8,512,512]{2,1,0:T(8,128)S(1)}, f32[8,512,512]{2,1,0:T(8,128)}, u32[]{:S(2)}) %copy-start.2) | copy-done | bytes 8388632
  114.8 9.9 %second_pass.1 = (bf16[3,512,512]{2,1,0:T(8,128)(2,1)}, bf16[1,512,512]{2,1,0:T(8,128)(2,1)}, bf16[3,512,512]{2,1,0:T(8,128)(2,1)}, bf16[1,512,512]{2,1,0:T(8,128)(2,1)}, bf16[512,768]{1,0:T(8,128)(2,1)}) custom-call(bf16[4,136,768]{2,1,0:T(8,128)(2,1)} %bitcast.3.refs_0_, bf16[4,136,768]{2,1,0:T(8,128)(2,1)} %bitcast.4.refs_1_, ...), custom_call_target="tpu_custom_call" | custom-call | flops 3221225472 | bytes 20971520 | tf_op jit(solution)/shard_map/second_pass/pallas_call | solution.py:384
  124.8 4.5 %convolution_convert_fusion = bf16[1536,768]{1,0:T(8,128)(2,1)} fusion(bf16[1536,512]{1,0:T(8,128)(2,1)} %bitcast.82, bf16[512,768]{1,0:T(8,128)(2,1)} %bitcast.16.refs_10_), kind=kOutput, calls=%fused_computation.1 | convolution fusion | flops 1209139200 | bytes 4718592 | tf_op jit(solution)/shard_map/dot_general | solution.py:511
  131.6 7.2 %all-to-all-start.3 = ((bf16[8,64,768]{2,1,0:T(8,128)(2,1)}), bf16[8,64,768]{2,1,0:T(8,128)(2,1)S(1)}, u32[]{:S(2)}, u32[]{:S(2)}) async-start(bf16[8,64,768]{2,1,0:T(8,128)(2,1)} %bitcast.27), calls=%async_computation.3 | async-start | bytes 1572864 | tf_op jit(solution)/shard_map/all_to_all | solution.py:427
  144.0 3.3 %add_convert_fusion = bf16[1536,768]{1,0:T(8,128)(2,1)S(1)} fusion(bf16[1536,768]{1,0:T(8,128)(2,1)} %collective-permute-done.15, bf16[1536,512]{1,0:T(8,128)(2,1)S(1)} %bitcast.81, bf16[512,768]{1,0:T(8,128)(2,1)} %bitcast.16.refs_10_), kind=kOutput, calls=%fused_computation | convolution fusion | flops 1211498496 | bytes 7077888 | tf_op jit(solution)/shard_map/dot_general | solution.py:515
  147.3 5.5 %collective-permute-done.17 = bf16[256,768]{1,0:T(8,128)(2,1)S(1)} collective-permute-done((bf16[256,768]{1,0:T(8,128)(2,1)S(1)}, bf16[256,768]{1,0:T(8,128)(2,1)S(1)}, u32[]{:S(2)}, u32[]{:S(2)}) %collective-permute-start.17) | collective-permute-done | bytes 393248 | tf_op jit(solution)/shard_map/ppermute | solution.py:32
  156.3 5.7 %all-to-all-done.3 = bf16[8,64,768]{2,1,0:T(8,128)(2,1)S(1)} async-done(((bf16[8,64,768]{2,1,0:T(8,128)(2,1)}), bf16[8,64,768]{2,1,0:T(8,128)(2,1)S(1)}, u32[]{:S(2)}, u32[]{:S(2)}) %all-to-all-start.3) | async-done | bytes 786464 | tf_op jit(solution)/shard_map/all_to_all | solution.py:427
  163.1 3.5 %all-to-all-start.4 = ((bf16[8,64,768]{2,1,0:T(8,128)(2,1)}), bf16[8,64,768]{2,1,0:T(8,128)(2,1)S(1)}, u32[]{:S(2)}, u32[]{:S(2)}) async-start(bf16[8,64,768]{2,1,0:T(8,128)(2,1)} %broadcast_in_dim.11), calls=%async_computation.4 | async-start | bytes 1572864 | tf_op jit(solution)/shard_map/all_to_all | solution.py:427
  172.3 6.7 %collective-permute-done.20 = bf16[256,768]{1,0:T(8,128)(2,1)S(1)} collective-permute-done((bf16[256,768]{1,0:T(8,128)(2,1)S(1)}, bf16[256,768]{1,0:T(8,128)(2,1)S(1)}, u32[]{:S(2)}, u32[]{:S(2)}) %collective-permute-start.20) | collective-permute-done | bytes 393248 | tf_op jit(solution)/shard_map/ppermute | solution.py:32
  183.5 6.7 %all-to-all-done.4 = bf16[8,64,768]{2,1,0:T(8,128)(2,1)S(1)} async-done(((bf16[8,64,768]{2,1,0:T(8,128)(2,1)}), bf16[8,64,768]{2,1,0:T(8,128)(2,1)S(1)}, u32[]{:S(2)}, u32[]{:S(2)}) %all-to-all-start.4) | async-done | bytes 786464 | tf_op jit(solution)/shard_map/all_to_all | solution.py:427
  200.3 6.3 %all-to-all-start.5 = ((bf16[16,48,384]{2,1,0:T(8,128)(2,1)}), bf16[16,48,384]{2,1,0:T(8,128)(2,1)S(1)}, u32[]{:S(2)}, u32[]{:S(2)}) async-start(bf16[16,48,384]{2,1,0:T(8,128)(2,1)} %add_convert_fusion.2), calls=%async_computation.5 | async-start | bytes 1179648 | tf_op jit(solution)/shard_map/all_to_all | solution.py:531
  208.2 12.1 %collective-permute-done.24 = bf16[128,768]{1,0:T(8,128)(2,1)S(1)} collective-permute-done((bf16[128,768]{1,0:T(8,128)(2,1)S(1)}, bf16[128,768]{1,0:T(8,128)(2,1)S(1)}, u32[]{:S(2)}, u32[]{:S(2)}) %collective-permute-start.24) | collective-permute-done | bytes 196640 | tf_op jit(solution)/shard_map/ppermute | solution.py:32
  (139 shorter events, 70.1 us)
Async XLA Ops:
  17.2 32.3 %all-to-all-start = ((bf16[8,64,768]{2,1,0:T(8,128)(2,1)}), bf16[8,64,768]{2,1,0:T(8,128)(2,1)S(1)}, u32[]{:S(2)}, u32[]{:S(2)}) async-start(bf16[8,64,768]{2,1,0:T(8,128)(2,1)} %bitcast.14), calls=%async_computation | async-start | bytes 1572864 | tf_op jit(solution)/shard_map/all_to_all | solution.py:427
  34.2 10.3 %collective-permute-start.3 = (bf16[72,768]{1,0:T(8,128)(2,1)S(1)}, bf16[72,768]{1,0:T(8,128)(2,1)S(1)}, u32[]{:S(2)}, u32[]{:S(2)}) collective-permute-start(bf16[72,768]{1,0:T(8,128)(2,1)S(1)} %slice.255), channel_id=1, source_target_pairs={{0,129},{1,0},{128,1},{129,128},{2,131},{3,2},{130,3},{131,130},{4... | collective-permute-start | bytes 331784 | tf_op jit(solution)/shard_map/ppermute | solution.py:32
  45.2 18.9 %collective-permute-start.5 = (bf16[544,768]{1,0:T(8,128)(2,1)}, bf16[544,768]{1,0:T(8,128)(2,1)S(1)}, u32[]{:S(2)}, u32[]{:S(2)}) collective-permute-start(bf16[544,768]{1,0:T(8,128)(2,1)} %constant_dynamic-update-slice_fusion), channel_id=1, source_target_pairs={{0,96},{32,0},{64,32},{96,64},{1,97},{33,1},{65,33},{97,65},{2,98}... | collective-permute-start | bytes 2506760 | tf_op jit(solution)/shard_map/ppermute | solution.py:32
  45.8 19.8 %collective-permute-start.4 = (bf16[544,768]{1,0:T(8,128)(2,1)}, bf16[544,768]{1,0:T(8,128)(2,1)}, u32[]{:S(2)}, u32[]{:S(2)}) collective-permute-start(bf16[544,768]{1,0:T(8,128)(2,1)} %constant_dynamic-update-slice_fusion), channel_id=1, source_target_pairs={{0,32},{32,64},{64,96},{96,0},{1,33},{33,65},{65,97},{97,1},{2,34}... | collective-permute-start | bytes 2506760 | tf_op jit(solution)/shard_map/ppermute | solution.py:32
  51.4 27.8 %all-to-all-start.1 = ((bf16[8,64,768]{2,1,0:T(8,128)(2,1)}), bf16[8,64,768]{2,1,0:T(8,128)(2,1)}, u32[]{:S(2)}, u32[]{:S(2)}) async-start(bf16[8,64,768]{2,1,0:T(8,128)(2,1)} %broadcast_in_dim.8), calls=%async_computation.1 | async-start | bytes 1572864 | tf_op jit(solution)/shard_map/all_to_all | solution.py:427
  56.1 21.4 %collective-permute-start.8 = (bf16[544,768]{1,0:T(8,128)(2,1)}, bf16[544,768]{1,0:T(8,128)(2,1)S(1)}, u32[]{:S(2)}, u32[]{:S(2)}) collective-permute-start(bf16[544,768]{1,0:T(8,128)(2,1)} %constant_dynamic-update-slice_fusion), channel_id=1, source_target_pairs={{0,16},{16,0},{1,17},{17,1},{2,18},{18,2},{3,19},{19,3},{4,20},{20... | collective-permute-start | bytes 2506760 | tf_op jit(solution)/shard_map/ppermute | solution.py:32
  64.2 9.1 %collective-permute-start.7 = (bf16[272,768]{1,0:T(8,128)(2,1)S(1)}, bf16[272,768]{1,0:T(8,128)(2,1)S(1)}, u32[]{:S(2)}, u32[]{:S(2)}) collective-permute-start(bf16[272,768]{1,0:T(8,128)(2,1)S(1)} %slice.257), channel_id=1, source_target_pairs={{0,96},{32,0},{64,32},{96,64},{1,97},{33,1},{65,33},{97,65},{2,98}... | collective-permute-start | bytes 1253384 | tf_op jit(solution)/shard_map/ppermute | solution.py:32
  66.6 10.3 %collective-permute-start.6 = (bf16[272,768]{1,0:T(8,128)(2,1)S(1)}, bf16[272,768]{1,0:T(8,128)(2,1)}, u32[]{:S(2)}, u32[]{:S(2)}) collective-permute-start(bf16[272,768]{1,0:T(8,128)(2,1)S(1)} %slice.256), channel_id=1, source_target_pairs={{0,32},{32,64},{64,96},{96,0},{1,33},{33,65},{65,97},{97,1},{2,34}... | collective-permute-start | bytes 1253384 | tf_op jit(solution)/shard_map/ppermute | solution.py:32
  67.4 10.2 %collective-permute-start.10 = (bf16[544,768]{1,0:T(8,128)(2,1)S(1)}, bf16[544,768]{1,0:T(8,128)(2,1)}, u32[]{:S(2)}, u32[]{:S(2)}) collective-permute-start(bf16[544,768]{1,0:T(8,128)(2,1)S(1)} %collective-permute-done.5), channel_id=1, source_target_pairs={{0,16},{16,0},{1,17},{17,1},{2,18},{18,2},{3,19},{19,3},{4,20},{20... | collective-permute-start | bytes 2506760 | tf_op jit(solution)/shard_map/ppermute | solution.py:32
  67.4 11.6 %collective-permute-start.9 = (bf16[544,768]{1,0:T(8,128)(2,1)}, bf16[544,768]{1,0:T(8,128)(2,1)}, u32[]{:S(2)}, u32[]{:S(2)}) collective-permute-start(bf16[544,768]{1,0:T(8,128)(2,1)} %collective-permute-done.4), channel_id=1, source_target_pairs={{0,16},{16,0},{1,17},{17,1},{2,18},{18,2},{3,19},{19,3},{4,20},{20... | collective-permute-start | bytes 2506760 | tf_op jit(solution)/shard_map/ppermute | solution.py:32
  94.5 14.7 %all-to-all-start.2 = ((f32[8,8,128]{2,1,0:T(8,128)}), f32[8,8,128]{2,1,0:T(8,128)S(1)}, u32[]{:S(2)}, u32[]{:S(2)}) async-start(f32[8,8,128]{2,1,0:T(8,128)} %broadcast_in_dim.9), calls=%async_computation.2 | async-start | bytes 65536 | tf_op jit(solution)/shard_map/all_to_all | solution.py:427
  129.3 14.7 %collective-permute-start.15 = (bf16[1536,768]{1,0:T(8,128)(2,1)}, bf16[1536,768]{1,0:T(8,128)(2,1)}, u32[]{:S(2)}, u32[]{:S(2)}) collective-permute-start(bf16[1536,768]{1,0:T(8,128)(2,1)} %convolution_convert_fusion), channel_id=1, source_target_pairs={{0,16},{16,0},{1,17},{17,1},{2,18},{18,2},{3,19},{19,3},{4,20},{20... | collective-permute-start | bytes 7077896 | tf_op jit(solution)/shard_map/ppermute | solution.py:32
  131.6 30.5 %all-to-all-start.3 = ((bf16[8,64,768]{2,1,0:T(8,128)(2,1)}), bf16[8,64,768]{2,1,0:T(8,128)(2,1)S(1)}, u32[]{:S(2)}, u32[]{:S(2)}) async-start(bf16[8,64,768]{2,1,0:T(8,128)(2,1)} %bitcast.27), calls=%async_computation.3 | async-start | bytes 1572864 | tf_op jit(solution)/shard_map/all_to_all | solution.py:427
  140.8 12.0 %collective-permute-start.17 = (bf16[256,768]{1,0:T(8,128)(2,1)S(1)}, bf16[256,768]{1,0:T(8,128)(2,1)S(1)}, u32[]{:S(2)}, u32[]{:S(2)}) collective-permute-start(bf16[256,768]{1,0:T(8,128)(2,1)S(1)} %get-tuple-element.39), channel_id=1, source_target_pairs={{0,32},{32,64},{64,96},{96,0},{1,33},{33,65},{65,97},{97,1},{2,34}... | collective-permute-start | bytes 1179656 | tf_op jit(solution)/shard_map/ppermute | solution.py:32
  140.9 25.8 %collective-permute-start.21 = (bf16[256,768]{1,0:T(8,128)(2,1)S(1)}, bf16[256,768]{1,0:T(8,128)(2,1)}, u32[]{:S(2)}, u32[]{:S(2)}) collective-permute-start(bf16[256,768]{1,0:T(8,128)(2,1)S(1)} %get-tuple-element.40), channel_id=1, source_target_pairs={{0,96},{32,0},{64,32},{96,64},{1,97},{33,1},{65,33},{97,65},{2,98}... | collective-permute-start | bytes 1179656 | tf_op jit(solution)/shard_map/ppermute | solution.py:32
  153.0 13.8 %collective-permute-start.18 = (bf16[256,768]{1,0:T(8,128)(2,1)S(1)}, bf16[256,768]{1,0:T(8,128)(2,1)}, u32[]{:S(2)}, u32[]{:S(2)}) collective-permute-start(bf16[256,768]{1,0:T(8,128)(2,1)S(1)} %add_convert_fusion.6), channel_id=1, source_target_pairs={{0,32},{32,64},{64,96},{96,0},{1,33},{33,65},{65,97},{97,1},{2,34}... | collective-permute-start | bytes 1179656 | tf_op jit(solution)/shard_map/ppermute | solution.py:32
  153.3 13.5 %collective-permute-start.19 = (bf16[256,768]{1,0:T(8,128)(2,1)S(1)}, bf16[256,768]{1,0:T(8,128)(2,1)}, u32[]{:S(2)}, u32[]{:S(2)}) collective-permute-start(bf16[256,768]{1,0:T(8,128)(2,1)S(1)} %get-tuple-element.33), channel_id=1, source_target_pairs={{0,96},{32,0},{64,32},{96,64},{1,97},{33,1},{65,33},{97,65},{2,98}... | collective-permute-start | bytes 1179656 | tf_op jit(solution)/shard_map/ppermute | solution.py:32
  163.1 27.0 %all-to-all-start.4 = ((bf16[8,64,768]{2,1,0:T(8,128)(2,1)}), bf16[8,64,768]{2,1,0:T(8,128)(2,1)S(1)}, u32[]{:S(2)}, u32[]{:S(2)}) async-start(bf16[8,64,768]{2,1,0:T(8,128)(2,1)} %broadcast_in_dim.11), calls=%async_computation.4 | async-start | bytes 1572864 | tf_op jit(solution)/shard_map/all_to_all | solution.py:427
  166.7 12.3 %collective-permute-start.20 = (bf16[256,768]{1,0:T(8,128)(2,1)S(1)}, bf16[256,768]{1,0:T(8,128)(2,1)S(1)}, u32[]{:S(2)}, u32[]{:S(2)}) collective-permute-start(bf16[256,768]{1,0:T(8,128)(2,1)S(1)} %get-tuple-element.34), channel_id=1, source_target_pairs={{0,32},{32,64},{64,96},{96,0},{1,33},{33,65},{65,97},{97,1},{2,34}... | collective-permute-start | bytes 1179656 | tf_op jit(solution)/shard_map/ppermute | solution.py:32
  169.3 11.6 %collective-permute-start.22 = (bf16[256,768]{1,0:T(8,128)(2,1)S(1)}, bf16[256,768]{1,0:T(8,128)(2,1)S(1)}, u32[]{:S(2)}, u32[]{:S(2)}) collective-permute-start(bf16[256,768]{1,0:T(8,128)(2,1)S(1)} %get-tuple-element.32), channel_id=1, source_target_pairs={{0,96},{32,0},{64,32},{96,64},{1,97},{33,1},{65,33},{97,65},{2,98}... | collective-permute-start | bytes 1179656 | tf_op jit(solution)/shard_map/ppermute | solution.py:32
  182.7 9.3 %collective-permute-start.25 = (bf16[64,768]{1,0:T(8,128)(2,1)}, bf16[64,768]{1,0:T(8,128)(2,1)}, u32[]{:S(2)}, u32[]{:S(2)}) collective-permute-start(bf16[64,768]{1,0:T(8,128)(2,1)} %get-tuple-element.44), channel_id=1, source_target_pairs={{0,129},{1,0},{128,1},{129,128},{2,131},{3,2},{130,3},{131,130},{4... | collective-permute-start | bytes 294920 | tf_op jit(solution)/shard_map/ppermute | solution.py:32
  192.9 15.2 %collective-permute-start.26 = (bf16[128,768]{1,0:T(8,128)(2,1)S(1)}, bf16[128,768]{1,0:T(8,128)(2,1)S(1)}, u32[]{:S(2)}, u32[]{:S(2)}) collective-permute-start(bf16[128,768]{1,0:T(8,128)(2,1)S(1)} %pad_maximum_fusion.3), channel_id=1, source_target_pairs={{0,129},{1,0},{128,1},{129,128},{2,131},{3,2},{130,3},{131,130},{4... | collective-permute-start | bytes 589832 | tf_op jit(solution)/shard_map/ppermute | solution.py:32
  200.3 20.8 %all-to-all-start.5 = ((bf16[16,48,384]{2,1,0:T(8,128)(2,1)}), bf16[16,48,384]{2,1,0:T(8,128)(2,1)S(1)}, u32[]{:S(2)}, u32[]{:S(2)}) async-start(bf16[16,48,384]{2,1,0:T(8,128)(2,1)} %add_convert_fusion.2), calls=%async_computation.5 | async-start | bytes 1179648 | tf_op jit(solution)/shard_map/all_to_all | solution.py:531
  206.6 13.7 %collective-permute-start.24 = (bf16[128,768]{1,0:T(8,128)(2,1)S(1)}, bf16[128,768]{1,0:T(8,128)(2,1)S(1)}, u32[]{:S(2)}, u32[]{:S(2)}) collective-permute-start(bf16[128,768]{1,0:T(8,128)(2,1)S(1)} %pad_maximum_fusion.2), channel_id=1, source_target_pairs={{0,1},{1,128},{128,129},{129,0},{2,3},{3,130},{130,131},{131,2},{4... | collective-permute-start | bytes 589832 | tf_op jit(solution)/shard_map/ppermute | solution.py:32
  (31 other events, 295.1 us)

commit v4 on v3

--- a/solution.py
+++ b/solution.py
@@ -68,7 +68,7 @@
         for n, (ref, at, size) in enumerate(sources):
             span = pl.ds(at, size)
             copies.append(
-                (g, pltpu.make_async_copy(ref.at[:, pl.ds(0, LAB), :], rows.at[g, span], sems.at[g, 2 * n]))
+                (g, pltpu.make_async_copy(ref.at[:, pl.ds(0, LAB), :], rows[g % 2].at[span], sems.at[g, 2 * n]))
             )
             if extras is not None:
                 copies.append(
@@ -76,7 +76,7 @@
                         g,
                         pltpu.make_async_copy(
                             ref.at[:, pl.ds(LAB, EXTRA), pl.ds(0, LAB)],
-                            extras.at[g, span],
+                            extras[g % 2].at[span],
                             sems.at[g, 2 * n + 1],
                         ),
                     )
@@ -84,17 +84,19 @@
     return copies
 
 
-def start_and_wait(copies):
+def start_and_wait(copies, late):
     step = pl.program_id(0)
-
-    @pl.when(step == 0)
-    def _():
-        for _, copy in copies:
-            copy.start()
-
     for g in range(STEPS):
 
-        @pl.when(step == g)
+        @pl.when(step == max(g - 1 + late, 0))
+        def _():
+            for at, copy in copies:
+                if at == g:
+                    copy.start()
+
+    for g in range(STEPS):
+
+        @pl.when(step == g + late)
         def _():
             for at, copy in copies:
                 if at == g:
@@ -103,8 +105,9 @@
 
 def first_kernel(*refs):
     label_refs = refs[:10]
-    (emb_hbm, exp_hbm, top_ref, stat_ref, rows, extras, sems, emb, emb_sem) = refs[10:19]
-    (raw_a, raw_b, bias_a, bias_b, exp_a, exp_b, exp_sem, run_max, run_sum) = refs[19:]
+    emb_hbm, exp_hbm, top_ref, stat_ref = refs[10:14]
+    rows_a, rows_b, extras_a, extras_b, sems, emb, emb_sem = refs[14:21]
+    (raw_a, raw_b, bias_a, bias_b, exp_a, exp_b, exp_sem, run_max, run_sum) = refs[21:]
     step = pl.program_id(0)
     fetch_emb = pltpu.make_async_copy(emb_hbm, emb, emb_sem)
 
@@ -112,27 +115,25 @@
     def _():
         fetch_emb.start()
 
-    start_and_wait(fetch_labels(label_refs, rows, extras, sems))
+    start_and_wait(fetch_labels(label_refs, (rows_a, rows_b), (extras_a, extras_b), sems), 0)
 
     @pl.when(step == 0)
     def _():
         fetch_emb.wait()
-
-    group = jnp.minimum(step, STEPS - 1)
 
     def put(exp_out, slot, which):
         return pltpu.make_async_copy(exp_out, exp_hbm.at[which], exp_sem.at[slot])
 
-    def body(slot, raw_out, bias_out, raw_in, bias_in, exp_out):
+    def body(slot, rows, extras, raw_out, bias_out, raw_in, bias_in, exp_out):
         @pl.when(step >= 3)
         def _():
             put(exp_out, slot, step - 3).wait()
 
         for j in range(GRP):
-            pieces = extras[group, j].astype(F32)
+            pieces = extras[j].astype(F32)
             row = pieces[0:1] + pieces[1:2] + pieces[2:3]
             bias_out[j * LAB : (j + 1) * LAB, :] = jnp.broadcast_to(row, (LAB, LAB)).T
-        lhs = rows[group].reshape(TILE, D)
+        lhs = rows[...].reshape(TILE, D)
         for half in range(2):
             wide = slice(half * 256, (half + 1) * 256)
             raw_out[:, wide] = lax.dot_general(lhs, emb[wide, :], NT, preferred_element_type=F32)
@@ -157,11 +158,11 @@
 
     @pl.when(lax.rem(step, 2) == 0)
     def _():
-        body(0, raw_a, bias_a, raw_b, bias_b, exp_a)
+        body(0, rows_a, extras_a, raw_a, bias_a, raw_b, bias_b, exp_a)
 
     @pl.when(lax.rem(step, 2) == 1)
     def _():
-        body(1, raw_b, bias_b, raw_a, bias_a, exp_b)
+        body(1, rows_b, extras_b, raw_b, bias_b, raw_a, bias_a, exp_b)
 
     @pl.when(step == 0)
     def _():
@@ -207,16 +208,15 @@
 def second_kernel(*refs):
     label_refs = refs[:10]
     exp_ref, top_ref, total_ref, hits_ref, near_hbm, near_end, far_hbm, far_end, out_ref = refs[10:19]
-    rows, sems, grad_a, grad_b, grad_sem, acc = refs[19:]
+    rows_a, rows_b, sems, grad_a, grad_b, grad_sem, acc = refs[19:]
     side = STEPS // 2
     step = pl.program_id(0)
-    start_and_wait(fetch_labels(label_refs, rows, None, sems))
-    before = jnp.maximum(step - 1, 0)
+    start_and_wait(fetch_labels(label_refs, (rows_a, rows_b), None, sems), 1)
 
     def put(grad, slot, home, which):
         return pltpu.make_async_copy(grad, home.at[which], grad_sem.at[slot])
 
-    def body(slot, grad_out, grad_in):
+    def body(slot, rows, grad_out, grad_in):
         @pl.when(step >= 2)
         def _():
             put(grad_out, slot, near_hbm, 0).wait()
@@ -226,7 +226,7 @@
             span = slice(j * LAB, (j + 1) * LAB)
             grad_out[span, :] = (exp_ref[0, span, :] * scale - hits_ref[0, span, :].astype(F32)).astype(BF16)
         acc[...] += lax.dot_general(
-            grad_in[...], rows[before].reshape(TILE, D), TN, preferred_element_type=F32
+            grad_in[...], rows[...].reshape(TILE, D), TN, preferred_element_type=F32
         )
 
         @pl.when(step < side - 1)
@@ -253,11 +253,11 @@
 
     @pl.when(lax.rem(step, 2) == 0)
     def _():
-        body(0, grad_a, grad_b)
+        body(0, rows_b, grad_a, grad_b)
 
     @pl.when(lax.rem(step, 2) == 1)
     def _():
-        body(1, grad_b, grad_a)
+        body(1, rows_a, grad_b, grad_a)
 
     @pl.when(step == 0)
     def _():
@@ -292,8 +292,10 @@
             pl.BlockSpec((8, 128), lambda s: (0, 0)),
         ),
         scratch_shapes=[
-            pltpu.VMEM((STEPS, GRP, LAB, D), BF16),
-            pltpu.VMEM((STEPS, GRP, EXTRA, LAB), BF16),
+            pltpu.VMEM((GRP, LAB, D), BF16),
+            pltpu.VMEM((GRP, LAB, D), BF16),
+            pltpu.VMEM((GRP, EXTRA, LAB), BF16),
+            pltpu.VMEM((GRP, EXTRA, LAB), BF16),
             pltpu.SemaphoreType.DMA((STEPS, 4)),
             pltpu.VMEM((DOCS, D), BF16),
             pltpu.SemaphoreType.DMA,
@@ -406,7 +408,8 @@
             pl.BlockSpec((DOCS, D), lambda s: (0, 0)),
         ),
         scratch_shapes=[
-            pltpu.VMEM((STEPS, GRP, LAB, D), BF16),
+            pltpu.VMEM((GRP, LAB, D), BF16),
+            pltpu.VMEM((GRP, LAB, D), BF16),
             pltpu.SemaphoreType.DMA((STEPS, 4)),
             pltpu.VMEM((TILE, DOCS), BF16),
             pltpu.VMEM((TILE, DOCS), BF16),

time: 223 us -> 224 us (level)
  no operation moved by 1% of the time
where the time goes in v4:
time: 224 us; the launch traced here: 222 us
  waiting for transfers between devices  78.5 us (35%)
  starting transfers between devices  65.4 us (29%)
  Pallas kernels  30.6 us (14%)
  local copies, waits for them, and re-layouts  19 us (8%)
  matrix products  15.1 us (7%)
  other arithmetic  12.2 us (5%)
    ppermute x28, waiting for transfers between devices, move(): lax.ppermute(block, axes, [(i, (i + distance) % size) for i in range(size)])  63.6 us
    all_to_all x5, starting transfers between devices, spread(): return lax.all_to_all(chunks, 'z', 0, 0)  30.2 us
    ppermute x28, starting transfers between devices, move(): lax.ppermute(block, axes, [(i, (i + distance) % size) for i in range(size)])  28.9 us
    all_to_all x5, waiting for transfers between devices, spread(): return lax.all_to_all(chunks, 'z', 0, 0)  14.9 us
    unnamed x46, local copies, waits for them, and re-layouts  12.6 us
    pallas_call x1, Pallas kernels, second_pass(): pl.pallas_call(second_kernel, out_shape=(pltpu.HBM((STEPS // 2 - 1, TILE,...  10.7 us
    pallas_call x1, Pallas kernels, first_pass(): pl.pallas_call(first_kernel, out_shape=(jax.ShapeDtypeStruct((STEPS, TILE...  10.6 us
    pallas_call x1, Pallas kernels, positive_hits(): pl.pallas_call(hits_kernel, out_shape=(jax.ShapeDtypeStruct((STEPS, TILE,...  7.76 us
  transfers between devices with their start and end apart: 34, of which 17 were waited for; matrix products, arithmetic and copies ran while one was open for 12% of the time, Pallas kernels for 4%

profile of v4, /device:TPU:2, one launch (start us, length us, event | category | flops | bytes accessed | tf_op | source)
XLA Modules:
  0.0 222.0 jit_solution(6140012783540271825)
XLA Ops:
  3.3 7.3 %collective-permute-done.13 = bf16[192,768]{1,0:T(8,128)(2,1)S(1)} collective-permute-done((bf16[192,768]{1,0:T(8,128)(2,1)S(1)}, bf16[192,768]{1,0:T(8,128)(2,1)S(1)}, u32[]{:S(2)}, u32[]{:S(2)}) %collective-permute-start.13) | collective-permute-done | bytes 294944 | tf_op jit(solution)/shard_map/ppermute | solution.py:32
  17.2 8.5 %all-to-all-start = ((bf16[8,64,768]{2,1,0:T(8,128)(2,1)}), bf16[8,64,768]{2,1,0:T(8,128)(2,1)S(1)}, u32[]{:S(2)}, u32[]{:S(2)}) async-start(bf16[8,64,768]{2,1,0:T(8,128)(2,1)} %bitcast.14), calls=%async_computation | async-start | bytes 1572864 | tf_op jit(solution)/shard_map/all_to_all | solution.py:430
  29.4 4.8 %collective-permute-done.1 = bf16[136,768]{1,0:T(8,128)(2,1)S(1)} collective-permute-done((bf16[136,768]{1,0:T(8,128)(2,1)S(1)}, bf16[136,768]{1,0:T(8,128)(2,1)S(1)}, u32[]{:S(2)}, u32[]{:S(2)}) %collective-permute-start.1) | collective-permute-done | bytes 208928 | tf_op jit(solution)/shard_map/ppermute | solution.py:32
  34.2 3.8 %collective-permute-start.3 = (bf16[72,768]{1,0:T(8,128)(2,1)S(1)}, bf16[72,768]{1,0:T(8,128)(2,1)S(1)}, u32[]{:S(2)}, u32[]{:S(2)}) collective-permute-start(bf16[72,768]{1,0:T(8,128)(2,1)S(1)} %slice.255), channel_id=1, source_target_pairs={{0,129},{1,0},{128,1},{129,128},{2,131},{3,2},{130,3},{131,130},{4... | collective-permute-start | bytes 331784 | tf_op jit(solution)/shard_map/ppermute | solution.py:32
  39.5 4.4 %collective-permute-done.2 = bf16[64,768]{1,0:T(8,128)(2,1)S(1)} collective-permute-done((bf16[64,768]{1,0:T(8,128)(2,1)S(1)}, bf16[64,768]{1,0:T(8,128)(2,1)S(1)}, u32[]{:S(2)}, u32[]{:S(2)}) %collective-permute-start.2) | collective-permute-done | bytes 98336 | tf_op jit(solution)/shard_map/ppermute | solution.py:32
  51.4 4.7 %all-to-all-start.1 = ((bf16[8,64,768]{2,1,0:T(8,128)(2,1)}), bf16[8,64,768]{2,1,0:T(8,128)(2,1)}, u32[]{:S(2)}, u32[]{:S(2)}) async-start(bf16[8,64,768]{2,1,0:T(8,128)(2,1)} %broadcast_in_dim.8), calls=%async_computation.1 | async-start | bytes 1572864 | tf_op jit(solution)/shard_map/all_to_all | solution.py:430
  56.1 8.0 %collective-permute-done.5 = bf16[544,768]{1,0:T(8,128)(2,1)S(1)} collective-permute-done((bf16[544,768]{1,0:T(8,128)(2,1)}, bf16[544,768]{1,0:T(8,128)(2,1)S(1)}, u32[]{:S(2)}, u32[]{:S(2)}) %collective-permute-start.5) | collective-permute-done | bytes 835616 | tf_op jit(solution)/shard_map/ppermute | solution.py:32
  67.9 5.4 %collective-permute-done.7 = bf16[272,768]{1,0:T(8,128)(2,1)S(1)} collective-permute-done((bf16[272,768]{1,0:T(8,128)(2,1)S(1)}, bf16[272,768]{1,0:T(8,128)(2,1)S(1)}, u32[]{:S(2)}, u32[]{:S(2)}) %collective-permute-start.7) | collective-permute-done | bytes 417824 | tf_op jit(solution)/shard_map/ppermute | solution.py:32
  73.3 3.6 %collective-permute-done.6 = bf16[272,768]{1,0:T(8,128)(2,1)} collective-permute-done((bf16[272,768]{1,0:T(8,128)(2,1)S(1)}, bf16[272,768]{1,0:T(8,128)(2,1)}, u32[]{:S(2)}, u32[]{:S(2)}) %collective-permute-start.6) | collective-permute-done | bytes 417824 | tf_op jit(solution)/shard_map/ppermute | solution.py:32
  79.3 10.6 %first_pass.1 = (f32[8,512,512]{2,1,0:T(8,128)S(1)}, f32[8,1,512]{2,1,0:T(1,128)S(1)}, f32[8,128]{1,0:T(8,128)S(1)}) custom-call(bf16[4,136,768]{2,1,0:T(8,128)(2,1)} %bitcast.3.refs_0_, bf16[4,136,768]{2,1,0:T(8,128)(2,1)} %bitcast.4.refs_1_, bf16[4,136,768]{2,1,0:T(8,128)(2,1)} %bitcast.75, bf16[2,136,768]{2,1,0:T(8,128)(2,1)} %bitcast.6.refs_3_, ...), custom_call_target="tpu_custom_call" | custom-call | flops 3221225472 | bytes 16777216 | tf_op jit(solution)/shard_map/first_pass/pallas_call | solution.py:280
  93.8 6.3 %all-to-all-start.2 = ((f32[8,8,128]{2,1,0:T(8,128)}), f32[8,8,128]{2,1,0:T(8,128)S(1)}, u32[]{:S(2)}, u32[]{:S(2)}) async-start(f32[8,8,128]{2,1,0:T(8,128)} %broadcast_in_dim.9), calls=%async_computation.2 | async-start | bytes 65536 | tf_op jit(solution)/shard_map/all_to_all | solution.py:430
  100.7 7.8 %positive_hits.1 = (bf16[8,512,512]{2,1,0:T(8,128)(2,1)}, bf16[768,512]{1,0:T(8,128)(2,1)}) custom-call(s32[33]{0:T(128)} %pad_add_fusion.base_ref, s32[4,512]{1,0:T(4,128)} %dynamic-slice_bitcast_fusion.pos_ref, bf16[1024,768]{1,0:T(8,128)(2,1)} %docs_ref.1), custom_call_target="tpu_custom_call" | custom-call | flops 33554432 | bytes 4194304 | tf_op jit(solution)/shard_map/positive_hits/pallas_call | solution.py:323
  108.6 3.4 %copy-done.2 = f32[8,512,512]{2,1,0:T(8,128)S(1)} copy-done((f32[8,512,512]{2,1,0:T(8,128)S(1)}, f32[8,512,512]{2,1,0:T(8,128)}, u32[]{:S(2)}) %copy-start.2) | copy-done | bytes 8388632
  114.1 10.7 %second_pass.1 = (bf16[3,512,512]{2,1,0:T(8,128)(2,1)}, bf16[1,512,512]{2,1,0:T(8,128)(2,1)}, bf16[3,512,512]{2,1,0:T(8,128)(2,1)}, bf16[1,512,512]{2,1,0:T(8,128)(2,1)}, bf16[512,768]{1,0:T(8,128)(2,1)}) custom-call(bf16[4,136,768]{2,1,0:T(8,128)(2,1)} %bitcast.3.refs_0_, bf16[4,136,768]{2,1,0:T(8,128)(2,1)} %bitcast.4.refs_1_, ...), custom_call_target="tpu_custom_call" | custom-call | flops 3221225472 | bytes 20971520 | tf_op jit(solution)/shard_map/second_pass/pallas_call | solution.py:386
  124.8 4.5 %convolution_convert_fusion = bf16[1536,768]{1,0:T(8,128)(2,1)} fusion(bf16[1536,512]{1,0:T(8,128)(2,1)} %bitcast.82, bf16[512,768]{1,0:T(8,128)(2,1)} %bitcast.16.refs_10_), kind=kOutput, calls=%fused_computation.1 | convolution fusion | flops 1209139200 | bytes 4718592 | tf_op jit(solution)/shard_map/dot_general | solution.py:514
  131.6 7.2 %all-to-all-start.3 = ((bf16[8,64,768]{2,1,0:T(8,128)(2,1)}), bf16[8,64,768]{2,1,0:T(8,128)(2,1)S(1)}, u32[]{:S(2)}, u32[]{:S(2)}) async-start(bf16[8,64,768]{2,1,0:T(8,128)(2,1)} %bitcast.27), calls=%async_computation.3 | async-start | bytes 1572864 | tf_op jit(solution)/shard_map/all_to_all | solution.py:430
  144.0 3.3 %add_convert_fusion = bf16[1536,768]{1,0:T(8,128)(2,1)S(1)} fusion(bf16[1536,768]{1,0:T(8,128)(2,1)} %collective-permute-done.15, bf16[1536,512]{1,0:T(8,128)(2,1)S(1)} %bitcast.81, bf16[512,768]{1,0:T(8,128)(2,1)} %bitcast.16.refs_10_), kind=kOutput, calls=%fused_computation | convolution fusion | flops 1211498496 | bytes 7077888 | tf_op jit(solution)/shard_map/dot_general | solution.py:518
  147.4 5.5 %collective-permute-done.17 = bf16[256,768]{1,0:T(8,128)(2,1)S(1)} collective-permute-done((bf16[256,768]{1,0:T(8,128)(2,1)S(1)}, bf16[256,768]{1,0:T(8,128)(2,1)S(1)}, u32[]{:S(2)}, u32[]{:S(2)}) %collective-permute-start.17) | collective-permute-done | bytes 393248 | tf_op jit(solution)/shard_map/ppermute | solution.py:32
  156.4 5.7 %all-to-all-done.3 = bf16[8,64,768]{2,1,0:T(8,128)(2,1)S(1)} async-done(((bf16[8,64,768]{2,1,0:T(8,128)(2,1)}), bf16[8,64,768]{2,1,0:T(8,128)(2,1)S(1)}, u32[]{:S(2)}, u32[]{:S(2)}) %all-to-all-start.3) | async-done | bytes 786464 | tf_op jit(solution)/shard_map/all_to_all | solution.py:430
  163.2 3.5 %all-to-all-start.4 = ((bf16[8,64,768]{2,1,0:T(8,128)(2,1)}), bf16[8,64,768]{2,1,0:T(8,128)(2,1)S(1)}, u32[]{:S(2)}, u32[]{:S(2)}) async-start(bf16[8,64,768]{2,1,0:T(8,128)(2,1)} %broadcast_in_dim.11), calls=%async_computation.4 | async-start | bytes 1572864 | tf_op jit(solution)/shard_map/all_to_all | solution.py:430
  172.4 6.7 %collective-permute-done.20 = bf16[256,768]{1,0:T(8,128)(2,1)S(1)} collective-permute-done((bf16[256,768]{1,0:T(8,128)(2,1)S(1)}, bf16[256,768]{1,0:T(8,128)(2,1)S(1)}, u32[]{:S(2)}, u32[]{:S(2)}) %collective-permute-start.20) | collective-permute-done | bytes 393248 | tf_op jit(solution)/shard_map/ppermute | solution.py:32
  183.5 6.7 %all-to-all-done.4 = bf16[8,64,768]{2,1,0:T(8,128)(2,1)S(1)} async-done(((bf16[8,64,768]{2,1,0:T(8,128)(2,1)}), bf16[8,64,768]{2,1,0:T(8,128)(2,1)S(1)}, u32[]{:S(2)}, u32[]{:S(2)}) %all-to-all-start.4) | async-done | bytes 786464 | tf_op jit(solution)/shard_map/all_to_all | solution.py:430
  200.3 6.3 %all-to-all-start.5 = ((bf16[16,48,384]{2,1,0:T(8,128)(2,1)}), bf16[16,48,384]{2,1,0:T(8,128)(2,1)S(1)}, u32[]{:S(2)}, u32[]{:S(2)}) async-start(bf16[16,48,384]{2,1,0:T(8,128)(2,1)} %add_convert_fusion.2), calls=%async_computation.5 | async-start | bytes 1179648 | tf_op jit(solution)/shard_map/all_to_all | solution.py:534
  208.2 12.1 %collective-permute-done.24 = bf16[128,768]{1,0:T(8,128)(2,1)S(1)} collective-permute-done((bf16[128,768]{1,0:T(8,128)(2,1)S(1)}, bf16[128,768]{1,0:T(8,128)(2,1)S(1)}, u32[]{:S(2)}, u32[]{:S(2)}) %collective-permute-start.24) | collective-permute-done | bytes 196640 | tf_op jit(solution)/shard_map/ppermute | solution.py:32
  (139 shorter events, 70.1 us)
Async XLA Ops:
  17.2 32.3 %all-to-all-start = ((bf16[8,64,768]{2,1,0:T(8,128)(2,1)}), bf16[8,64,768]{2,1,0:T(8,128)(2,1)S(1)}, u32[]{:S(2)}, u32[]{:S(2)}) async-start(bf16[8,64,768]{2,1,0:T(8,128)(2,1)} %bitcast.14), calls=%async_computation | async-start | bytes 1572864 | tf_op jit(solution)/shard_map/all_to_all | solution.py:430
  34.2 10.3 %collective-permute-start.3 = (bf16[72,768]{1,0:T(8,128)(2,1)S(1)}, bf16[72,768]{1,0:T(8,128)(2,1)S(1)}, u32[]{:S(2)}, u32[]{:S(2)}) collective-permute-start(bf16[72,768]{1,0:T(8,128)(2,1)S(1)} %slice.255), channel_id=1, source_target_pairs={{0,129},{1,0},{128,1},{129,128},{2,131},{3,2},{130,3},{131,130},{4... | collective-permute-start | bytes 331784 | tf_op jit(solution)/shard_map/ppermute | solution.py:32
  45.2 18.9 %collective-permute-start.5 = (bf16[544,768]{1,0:T(8,128)(2,1)}, bf16[544,768]{1,0:T(8,128)(2,1)S(1)}, u32[]{:S(2)}, u32[]{:S(2)}) collective-permute-start(bf16[544,768]{1,0:T(8,128)(2,1)} %constant_dynamic-update-slice_fusion), channel_id=1, source_target_pairs={{0,96},{32,0},{64,32},{96,64},{1,97},{33,1},{65,33},{97,65},{2,98}... | collective-permute-start | bytes 2506760 | tf_op jit(solution)/shard_map/ppermute | solution.py:32
  45.8 19.8 %collective-permute-start.4 = (bf16[544,768]{1,0:T(8,128)(2,1)}, bf16[544,768]{1,0:T(8,128)(2,1)}, u32[]{:S(2)}, u32[]{:S(2)}) collective-permute-start(bf16[544,768]{1,0:T(8,128)(2,1)} %constant_dynamic-update-slice_fusion), channel_id=1, source_target_pairs={{0,32},{32,64},{64,96},{96,0},{1,33},{33,65},{65,97},{97,1},{2,34}... | collective-permute-start | bytes 2506760 | tf_op jit(solution)/shard_map/ppermute | solution.py:32
  51.4 27.8 %all-to-all-start.1 = ((bf16[8,64,768]{2,1,0:T(8,128)(2,1)}), bf16[8,64,768]{2,1,0:T(8,128)(2,1)}, u32[]{:S(2)}, u32[]{:S(2)}) async-start(bf16[8,64,768]{2,1,0:T(8,128)(2,1)} %broadcast_in_dim.8), calls=%async_computation.1 | async-start | bytes 1572864 | tf_op jit(solution)/shard_map/all_to_all | solution.py:430
  56.1 21.4 %collective-permute-start.8 = (bf16[544,768]{1,0:T(8,128)(2,1)}, bf16[544,768]{1,0:T(8,128)(2,1)S(1)}, u32[]{:S(2)}, u32[]{:S(2)}) collective-permute-start(bf16[544,768]{1,0:T(8,128)(2,1)} %constant_dynamic-update-slice_fusion), channel_id=1, source_target_pairs={{0,16},{16,0},{1,17},{17,1},{2,18},{18,2},{3,19},{19,3},{4,20},{20... | collective-permute-start | bytes 2506760 | tf_op jit(solution)/shard_map/ppermute | solution.py:32
  64.2 9.1 %collective-permute-start.7 = (bf16[272,768]{1,0:T(8,128)(2,1)S(1)}, bf16[272,768]{1,0:T(8,128)(2,1)S(1)}, u32[]{:S(2)}, u32[]{:S(2)}) collective-permute-start(bf16[272,768]{1,0:T(8,128)(2,1)S(1)} %slice.257), channel_id=1, source_target_pairs={{0,96},{32,0},{64,32},{96,64},{1,97},{33,1},{65,33},{97,65},{2,98}... | collective-permute-start | bytes 1253384 | tf_op jit(solution)/shard_map/ppermute | solution.py:32
  66.6 10.3 %collective-permute-start.6 = (bf16[272,768]{1,0:T(8,128)(2,1)S(1)}, bf16[272,768]{1,0:T(8,128)(2,1)}, u32[]{:S(2)}, u32[]{:S(2)}) collective-permute-start(bf16[272,768]{1,0:T(8,128)(2,1)S(1)} %slice.256), channel_id=1, source_target_pairs={{0,32},{32,64},{64,96},{96,0},{1,33},{33,65},{65,97},{97,1},{2,34}... | collective-permute-start | bytes 1253384 | tf_op jit(solution)/shard_map/ppermute | solution.py:32
  67.4 10.2 %collective-permute-start.10 = (bf16[544,768]{1,0:T(8,128)(2,1)S(1)}, bf16[544,768]{1,0:T(8,128)(2,1)}, u32[]{:S(2)}, u32[]{:S(2)}) collective-permute-start(bf16[544,768]{1,0:T(8,128)(2,1)S(1)} %collective-permute-done.5), channel_id=1, source_target_pairs={{0,16},{16,0},{1,17},{17,1},{2,18},{18,2},{3,19},{19,3},{4,20},{20... | collective-permute-start | bytes 2506760 | tf_op jit(solution)/shard_map/ppermute | solution.py:32
  67.4 11.6 %collective-permute-start.9 = (bf16[544,768]{1,0:T(8,128)(2,1)}, bf16[544,768]{1,0:T(8,128)(2,1)}, u32[]{:S(2)}, u32[]{:S(2)}) collective-permute-start(bf16[544,768]{1,0:T(8,128)(2,1)} %collective-permute-done.4), channel_id=1, source_target_pairs={{0,16},{16,0},{1,17},{17,1},{2,18},{18,2},{3,19},{19,3},{4,20},{20... | collective-permute-start | bytes 2506760 | tf_op jit(solution)/shard_map/ppermute | solution.py:32
  93.8 14.7 %all-to-all-start.2 = ((f32[8,8,128]{2,1,0:T(8,128)}), f32[8,8,128]{2,1,0:T(8,128)S(1)}, u32[]{:S(2)}, u32[]{:S(2)}) async-start(f32[8,8,128]{2,1,0:T(8,128)} %broadcast_in_dim.9), calls=%async_computation.2 | async-start | bytes 65536 | tf_op jit(solution)/shard_map/all_to_all | solution.py:430
  129.3 14.7 %collective-permute-start.15 = (bf16[1536,768]{1,0:T(8,128)(2,1)}, bf16[1536,768]{1,0:T(8,128)(2,1)}, u32[]{:S(2)}, u32[]{:S(2)}) collective-permute-start(bf16[1536,768]{1,0:T(8,128)(2,1)} %convolution_convert_fusion), channel_id=1, source_target_pairs={{0,16},{16,0},{1,17},{17,1},{2,18},{18,2},{3,19},{19,3},{4,20},{20... | collective-permute-start | bytes 7077896 | tf_op jit(solution)/shard_map/ppermute | solution.py:32
  131.6 30.5 %all-to-all-start.3 = ((bf16[8,64,768]{2,1,0:T(8,128)(2,1)}), bf16[8,64,768]{2,1,0:T(8,128)(2,1)S(1)}, u32[]{:S(2)}, u32[]{:S(2)}) async-start(bf16[8,64,768]{2,1,0:T(8,128)(2,1)} %bitcast.27), calls=%async_computation.3 | async-start | bytes 1572864 | tf_op jit(solution)/shard_map/all_to_all | solution.py:430
  140.9 12.1 %collective-permute-start.17 = (bf16[256,768]{1,0:T(8,128)(2,1)S(1)}, bf16[256,768]{1,0:T(8,128)(2,1)S(1)}, u32[]{:S(2)}, u32[]{:S(2)}) collective-permute-start(bf16[256,768]{1,0:T(8,128)(2,1)S(1)} %get-tuple-element.39), channel_id=1, source_target_pairs={{0,32},{32,64},{64,96},{96,0},{1,33},{33,65},{65,97},{97,1},{2,34}... | collective-permute-start | bytes 1179656 | tf_op jit(solution)/shard_map/ppermute | solution.py:32
  141.0 25.8 %collective-permute-start.21 = (bf16[256,768]{1,0:T(8,128)(2,1)S(1)}, bf16[256,768]{1,0:T(8,128)(2,1)}, u32[]{:S(2)}, u32[]{:S(2)}) collective-permute-start(bf16[256,768]{1,0:T(8,128)(2,1)S(1)} %get-tuple-element.40), channel_id=1, source_target_pairs={{0,96},{32,0},{64,32},{96,64},{1,97},{33,1},{65,33},{97,65},{2,98}... | collective-permute-start | bytes 1179656 | tf_op jit(solution)/shard_map/ppermute | solution.py:32
  153.1 13.8 %collective-permute-start.18 = (bf16[256,768]{1,0:T(8,128)(2,1)S(1)}, bf16[256,768]{1,0:T(8,128)(2,1)}, u32[]{:S(2)}, u32[]{:S(2)}) collective-permute-start(bf16[256,768]{1,0:T(8,128)(2,1)S(1)} %add_convert_fusion.6), channel_id=1, source_target_pairs={{0,32},{32,64},{64,96},{96,0},{1,33},{33,65},{65,97},{97,1},{2,34}... | collective-permute-start | bytes 1179656 | tf_op jit(solution)/shard_map/ppermute | solution.py:32
  153.4 13.5 %collective-permute-start.19 = (bf16[256,768]{1,0:T(8,128)(2,1)S(1)}, bf16[256,768]{1,0:T(8,128)(2,1)}, u32[]{:S(2)}, u32[]{:S(2)}) collective-permute-start(bf16[256,768]{1,0:T(8,128)(2,1)S(1)} %get-tuple-element.33), channel_id=1, source_target_pairs={{0,96},{32,0},{64,32},{96,64},{1,97},{33,1},{65,33},{97,65},{2,98}... | collective-permute-start | bytes 1179656 | tf_op jit(solution)/shard_map/ppermute | solution.py:32
  163.2 27.0 %all-to-all-start.4 = ((bf16[8,64,768]{2,1,0:T(8,128)(2,1)}), bf16[8,64,768]{2,1,0:T(8,128)(2,1)S(1)}, u32[]{:S(2)}, u32[]{:S(2)}) async-start(bf16[8,64,768]{2,1,0:T(8,128)(2,1)} %broadcast_in_dim.11), calls=%async_computation.4 | async-start | bytes 1572864 | tf_op jit(solution)/shard_map/all_to_all | solution.py:430
  166.7 12.3 %collective-permute-start.20 = (bf16[256,768]{1,0:T(8,128)(2,1)S(1)}, bf16[256,768]{1,0:T(8,128)(2,1)S(1)}, u32[]{:S(2)}, u32[]{:S(2)}) collective-permute-start(bf16[256,768]{1,0:T(8,128)(2,1)S(1)} %get-tuple-element.34), channel_id=1, source_target_pairs={{0,32},{32,64},{64,96},{96,0},{1,33},{33,65},{65,97},{97,1},{2,34}... | collective-permute-start | bytes 1179656 | tf_op jit(solution)/shard_map/ppermute | solution.py:32
  169.3 11.6 %collective-permute-start.22 = (bf16[256,768]{1,0:T(8,128)(2,1)S(1)}, bf16[256,768]{1,0:T(8,128)(2,1)S(1)}, u32[]{:S(2)}, u32[]{:S(2)}) collective-permute-start(bf16[256,768]{1,0:T(8,128)(2,1)S(1)} %get-tuple-element.32), channel_id=1, source_target_pairs={{0,96},{32,0},{64,32},{96,64},{1,97},{33,1},{65,33},{97,65},{2,98}... | collective-permute-start | bytes 1179656 | tf_op jit(solution)/shard_map/ppermute | solution.py:32
  182.8 9.3 %collective-permute-start.25 = (bf16[64,768]{1,0:T(8,128)(2,1)}, bf16[64,768]{1,0:T(8,128)(2,1)}, u32[]{:S(2)}, u32[]{:S(2)}) collective-permute-start(bf16[64,768]{1,0:T(8,128)(2,1)} %get-tuple-element.44), channel_id=1, source_target_pairs={{0,129},{1,0},{128,1},{129,128},{2,131},{3,2},{130,3},{131,130},{4... | collective-permute-start | bytes 294920 | tf_op jit(solution)/shard_map/ppermute | solution.py:32
  193.0 15.2 %collective-permute-start.26 = (bf16[128,768]{1,0:T(8,128)(2,1)S(1)}, bf16[128,768]{1,0:T(8,128)(2,1)S(1)}, u32[]{:S(2)}, u32[]{:S(2)}) collective-permute-start(bf16[128,768]{1,0:T(8,128)(2,1)S(1)} %pad_maximum_fusion.3), channel_id=1, source_target_pairs={{0,129},{1,0},{128,1},{129,128},{2,131},{3,2},{130,3},{131,130},{4... | collective-permute-start | bytes 589832 | tf_op jit(solution)/shard_map/ppermute | solution.py:32
  200.3 20.8 %all-to-all-start.5 = ((bf16[16,48,384]{2,1,0:T(8,128)(2,1)}), bf16[16,48,384]{2,1,0:T(8,128)(2,1)S(1)}, u32[]{:S(2)}, u32[]{:S(2)}) async-start(bf16[16,48,384]{2,1,0:T(8,128)(2,1)} %add_convert_fusion.2), calls=%async_computation.5 | async-start | bytes 1179648 | tf_op jit(solution)/shard_map/all_to_all | solution.py:534
  206.7 13.7 %collective-permute-start.24 = (bf16[128,768]{1,0:T(8,128)(2,1)S(1)}, bf16[128,768]{1,0:T(8,128)(2,1)S(1)}, u32[]{:S(2)}, u32[]{:S(2)}) collective-permute-start(bf16[128,768]{1,0:T(8,128)(2,1)S(1)} %pad_maximum_fusion.2), channel_id=1, source_target_pairs={{0,1},{1,128},{128,129},{129,0},{2,3},{3,130},{130,131},{131,2},{4... | collective-permute-start | bytes 589832 | tf_op jit(solution)/shard_map/ppermute | solution.py:32
  (31 other events, 295.1 us)

commit v5 on v4

--- a/solution.py
+++ b/solution.py
@@ -208,63 +208,48 @@
 def second_kernel(*refs):
     label_refs = refs[:10]
     exp_ref, top_ref, total_ref, hits_ref, near_hbm, near_end, far_hbm, far_end, out_ref = refs[10:19]
-    rows_a, rows_b, sems, grad_a, grad_b, grad_sem, acc = refs[19:]
+    rows_ref, sems, grads, grad_sem, acc = refs[19:]
     side = STEPS // 2
     step = pl.program_id(0)
-    start_and_wait(fetch_labels(label_refs, (rows_a, rows_b), None, sems), 1)
-
-    def put(grad, slot, home, which):
-        return pltpu.make_async_copy(grad, home.at[which], grad_sem.at[slot])
-
-    def body(slot, rows, grad_out, grad_in):
-        @pl.when(step >= 2)
-        def _():
-            put(grad_out, slot, near_hbm, 0).wait()
-
-        scale = jnp.exp(top_ref[0] - total_ref[...])
-        for j in range(GRP):
-            span = slice(j * LAB, (j + 1) * LAB)
-            grad_out[span, :] = (exp_ref[0, span, :] * scale - hits_ref[0, span, :].astype(F32)).astype(BF16)
-        acc[...] += lax.dot_general(
-            grad_in[...], rows[...].reshape(TILE, D), TN, preferred_element_type=F32
-        )
-
-        @pl.when(step < side - 1)
-        def _():
-            put(grad_out, slot, near_hbm, step).start()
-
-        @pl.when((step >= side) & (step < STEPS - 1))
-        def _():
-            put(grad_out, slot, far_hbm, step - side).start()
-
-        if slot == 1:
-
-            @pl.when(step == side - 1)
-            def _():
-                put(grad_out, slot, near_end, 0).start()
-
-            @pl.when(step == STEPS - 1)
-            def _():
-                put(grad_out, slot, far_end, 0).start()
-
-        @pl.when(step == STEPS)
-        def _():
-            put(grad_in, 1 - slot, far_end, 0).wait()
-
-    @pl.when(lax.rem(step, 2) == 0)
-    def _():
-        body(0, rows_b, grad_a, grad_b)
-
-    @pl.when(lax.rem(step, 2) == 1)
-    def _():
-        body(1, rows_a, grad_b, grad_a)
+    slot = lax.rem(step, 2)
+    start_and_wait(fetch_labels(label_refs, (rows_ref.at[0], rows_ref.at[1]), None, sems), 0)
+
+    def put(at, home, which):
+        return pltpu.make_async_copy(grads.at[at], home.at[which], grad_sem.at[at])
 
     @pl.when(step == 0)
     def _():
         acc[...] = jnp.zeros_like(acc)
 
-    @pl.when(step == STEPS)
-    def _():
+    @pl.when(step >= 2)
+    def _():
+        put(slot, near_hbm, 0).wait()
+
+    scale = jnp.exp(top_ref[0] - total_ref[...])
+    for j in range(GRP):
+        span = slice(j * LAB, (j + 1) * LAB)
+        grads[slot, span, :] = (exp_ref[0, span, :] * scale - hits_ref[0, span, :].astype(F32)).astype(BF16)
+
+    rows = rows_ref[slot].reshape(TILE, D)
+    acc[...] += lax.dot_general(grads[slot], rows, TN, preferred_element_type=F32)
+
+    @pl.when(step < side - 1)
+    def _():
+        put(slot, near_hbm, step).start()
+
+    @pl.when((step >= side) & (step < STEPS - 1))
+    def _():
+        put(slot, far_hbm, step - side).start()
+
+    @pl.when(step == side - 1)
+    def _():
+        put(slot, near_end, 0).start()
+
+    @pl.when(step == STEPS - 1)
+    def _():
+        put(slot, far_end, 0).start()
+        put(1 - slot, far_hbm, 0).wait()
+        put(slot, far_end, 0).wait()
         out_ref[...] = acc[...].astype(BF16)
 
 
@@ -382,7 +367,6 @@
 
 
 def second_pass(labels, exps, tops, log_total, hits):
-    last = STEPS - 1
     return pl.pallas_call(
         second_kernel,
         out_shape=(
@@ -392,13 +376,13 @@
             pltpu.HBM((1, TILE, DOCS), BF16),
             pltpu.HBM((DOCS, D), BF16),
         ),
-        grid=(STEPS + 1,),
+        grid=(STEPS,),
         in_specs=label_specs()
         + [
-            pl.BlockSpec((1, TILE, DOCS), lambda s: (jnp.minimum(s, last), 0, 0)),
-            pl.BlockSpec((1, 1, DOCS), lambda s: (jnp.minimum(s, last), 0, 0)),
+            pl.BlockSpec((1, TILE, DOCS), lambda s: (s, 0, 0)),
+            pl.BlockSpec((1, 1, DOCS), lambda s: (s, 0, 0)),
             pl.BlockSpec((1, DOCS), lambda s: (0, 0)),
-            pl.BlockSpec((1, TILE, DOCS), lambda s: (jnp.minimum(s, last), 0, 0)),
+            pl.BlockSpec((1, TILE, DOCS), lambda s: (s, 0, 0)),
         ],
         out_specs=(
             pl.BlockSpec(memory_space=pl.ANY),
@@ -408,11 +392,9 @@
             pl.BlockSpec((DOCS, D), lambda s: (0, 0)),
         ),
         scratch_shapes=[
-            pltpu.VMEM((GRP, LAB, D), BF16),
-            pltpu.VMEM((GRP, LAB, D), BF16),
+            pltpu.VMEM((2, GRP, LAB, D), BF16),
             pltpu.SemaphoreType.DMA((STEPS, 4)),
-            pltpu.VMEM((TILE, DOCS), BF16),
-            pltpu.VMEM((TILE, DOCS), BF16),
+            pltpu.VMEM((2, TILE, DOCS), BF16),
             pltpu.SemaphoreType.DMA((2,)),
             pltpu.VMEM((DOCS, D), F32),
         ],
@@ -454,7 +436,11 @@
     column = jnp.concatenate([block, y_low, y_high, y_far_a, y_far_b], axis=0)
     x_low = move(column, "x", 4, 1)
     x_high = move(column, "x", 4, -1)
-    c_column = move(column, "core", 2, 1)
+    x_far_a = move(x_low[: 2 * BLK], "x", 4, 1)
+    x_far_b = move(x_high[2 * BLK :], "x", 4, -1)
+    near = [column, x_low, x_high, x_far_a, x_far_b]
+    far = [move(column, "core", 2, 1)]
+    far += [move(part, "core", 2, 1) for part in near[1:]]
 
     up_rows = up_weight.T
     mine = jnp.where(core == 0, up_rows, down_weight)
@@ -476,15 +462,7 @@
     parts = spread(partial_out.reshape(8, DOCS // 8, D))
     own_docs = lax.dynamic_slice_in_dim(docs, z * (DOCS // 8), DOCS // 8, 0)
     own_emb = (own_docs.astype(F32) + total(parts)).astype(BF16)
-    x_far_a = move(x_low[: 2 * BLK], "x", 4, 1)
-    x_far_b = move(x_high[2 * BLK :], "x", 4, -1)
-    c_low = move(x_low, "core", 2, 1)
-    c_high = move(x_high, "core", 2, 1)
-    c_far_a = move(x_far_a, "core", 2, 1)
-    c_far_b = move(x_far_b, "core", 2, 1)
     embedding = everywhere(own_emb).reshape(DOCS, D)
-    near = [column, x_low, x_high, x_far_a, x_far_b]
-    far = [c_column, c_low, c_high, c_far_a, c_far_b]
     labels = [in_hbm(part.reshape(-1, BLK, D)) for part in near + far]
 
     which = jnp.arange(NB, dtype=I32)
@@ -525,6 +503,7 @@
     down_lo = move(sums[1][:half], "x", 4, -1)
     up_lo = add(sums[2][:half], low_a).astype(BF16)
     down_hi = add(sums[1][half:], high_b).astype(BF16)
+    up_lo, down_hi = lax.optimization_barrier((up_lo, down_hi))
     up_lo = move(up_lo, "x", 4, 1)
     down_hi = move(down_hi, "x", 4, -1)
 

time: 224 us -> 226 us (level)
  waiting for transfers between devices: 78.5 us -> 83.8 us
  other arithmetic: 12.2 us -> 9.79 us
    ppermute x28, waiting for transfers between devices: 63.6 us -> 66.4 us  [move(): lax.ppermute(block, axes, [(i, (i + distance) % size) for i in range(size)])]
    all_to_all x5, waiting for transfers between devices: 14.9 us -> 17.4 us  [spread(): return lax.all_to_all(chunks, 'z', 0, 0)]
    unnamed x46 -> x44, local copies, waits for them, and re-layouts: 12.6 us -> 13.2 us
  transfers between devices with their start and end apart: 34 -> 34, of which waited for: 17 -> 18; matrix products, arithmetic and copies ran while one was open for 12% -> 10% of each run, Pallas kernels for 4% -> 4%
where the time goes in v5:
time: 226 us; the launch traced here: 224 us
  waiting for transfers between devices  83.8 us (37%)
  starting transfers between devices  64.7 us (29%)
  Pallas kernels  30 us (13%)
  local copies, waits for them, and re-layouts  19.5 us (9%)
  matrix products  15.3 us (7%)
  other arithmetic  9.79 us (4%)
    ppermute x28, waiting for transfers between devices, move(): lax.ppermute(block, axes, [(i, (i + distance) % size) for i in range(size)])  66.4 us
    all_to_all x5, starting transfers between devices, spread(): return lax.all_to_all(chunks, 'z', 0, 0)  30.3 us
    ppermute x28, starting transfers between devices, move(): lax.ppermute(block, axes, [(i, (i + distance) % size) for i in range(size)])  27.2 us
    all_to_all x5, waiting for transfers between devices, spread(): return lax.all_to_all(chunks, 'z', 0, 0)  17.4 us
    unnamed x44, local copies, waits for them, and re-layouts  13.2 us
    pallas_call x1, Pallas kernels, first_pass(): pl.pallas_call(first_kernel, out_shape=(jax.ShapeDtypeStruct((STEPS, TILE...  10.6 us
    pallas_call x1, Pallas kernels, second_pass(): pl.pallas_call(second_kernel, out_shape=(pltpu.HBM((STEPS // 2 - 1, TILE,...  10.1 us
    pallas_call x1, Pallas kernels, positive_hits(): pl.pallas_call(hits_kernel, out_shape=(jax.ShapeDtypeStruct((STEPS, TILE,...  7.76 us
  transfers between devices with their start and end apart: 34, of which 18 were waited for; matrix products, arithmetic and copies ran while one was open for 10% of the time, Pallas kernels for 4%

profile of v5, /device:TPU:2, one launch (start us, length us, event | category | flops | bytes accessed | tf_op | source)
XLA Modules:
  0.0 224.2 jit_solution(17771243326155883267)
XLA Ops:
  3.3 7.3 %collective-permute-done.13 = bf16[192,768]{1,0:T(8,128)(2,1)S(1)} collective-permute-done((bf16[192,768]{1,0:T(8,128)(2,1)S(1)}, bf16[192,768]{1,0:T(8,128)(2,1)S(1)}, u32[]{:S(2)}, u32[]{:S(2)}) %collective-permute-start.13) | collective-permute-done | bytes 294944 | tf_op jit(solution)/shard_map/ppermute | solution.py:32
  17.2 8.5 %all-to-all-start = ((bf16[8,64,768]{2,1,0:T(8,128)(2,1)}), bf16[8,64,768]{2,1,0:T(8,128)(2,1)S(1)}, u32[]{:S(2)}, u32[]{:S(2)}) async-start(bf16[8,64,768]{2,1,0:T(8,128)(2,1)} %bitcast.14), calls=%async_computation | async-start | bytes 1572864 | tf_op jit(solution)/shard_map/all_to_all | solution.py:412
  29.4 4.8 %collective-permute-done.1 = bf16[136,768]{1,0:T(8,128)(2,1)S(1)} collective-permute-done((bf16[136,768]{1,0:T(8,128)(2,1)S(1)}, bf16[136,768]{1,0:T(8,128)(2,1)S(1)}, u32[]{:S(2)}, u32[]{:S(2)}) %collective-permute-start.1) | collective-permute-done | bytes 208928 | tf_op jit(solution)/shard_map/ppermute | solution.py:32
  34.2 3.8 %collective-permute-start.3 = (bf16[72,768]{1,0:T(8,128)(2,1)S(1)}, bf16[72,768]{1,0:T(8,128)(2,1)S(1)}, u32[]{:S(2)}, u32[]{:S(2)}) collective-permute-start(bf16[72,768]{1,0:T(8,128)(2,1)S(1)} %slice.255), channel_id=1, source_target_pairs={{0,129},{1,0},{128,1},{129,128},{2,131},{3,2},{130,3},{131,130},{4... | collective-permute-start | bytes 331784 | tf_op jit(solution)/shard_map/ppermute | solution.py:32
  39.5 4.4 %collective-permute-done.2 = bf16[64,768]{1,0:T(8,128)(2,1)S(1)} collective-permute-done((bf16[64,768]{1,0:T(8,128)(2,1)S(1)}, bf16[64,768]{1,0:T(8,128)(2,1)S(1)}, u32[]{:S(2)}, u32[]{:S(2)}) %collective-permute-start.2) | collective-permute-done | bytes 98336 | tf_op jit(solution)/shard_map/ppermute | solution.py:32
  51.5 4.7 %all-to-all-start.1 = ((bf16[8,64,768]{2,1,0:T(8,128)(2,1)}), bf16[8,64,768]{2,1,0:T(8,128)(2,1)}, u32[]{:S(2)}, u32[]{:S(2)}) async-start(bf16[8,64,768]{2,1,0:T(8,128)(2,1)} %broadcast_in_dim.8), calls=%async_computation.1 | async-start | bytes 1572864 | tf_op jit(solution)/shard_map/all_to_all | solution.py:412
  56.2 8.0 %collective-permute-done.5 = bf16[544,768]{1,0:T(8,128)(2,1)S(1)} collective-permute-done((bf16[544,768]{1,0:T(8,128)(2,1)}, bf16[544,768]{1,0:T(8,128)(2,1)S(1)}, u32[]{:S(2)}, u32[]{:S(2)}) %collective-permute-start.5) | collective-permute-done | bytes 835616 | tf_op jit(solution)/shard_map/ppermute | solution.py:32
  67.9 5.4 %collective-permute-done.7 = bf16[272,768]{1,0:T(8,128)(2,1)S(1)} collective-permute-done((bf16[272,768]{1,0:T(8,128)(2,1)S(1)}, bf16[272,768]{1,0:T(8,128)(2,1)S(1)}, u32[]{:S(2)}, u32[]{:S(2)}) %collective-permute-start.7) | collective-permute-done | bytes 417824 | tf_op jit(solution)/shard_map/ppermute | solution.py:32
  73.3 3.6 %collective-permute-done.6 = bf16[272,768]{1,0:T(8,128)(2,1)} collective-permute-done((bf16[272,768]{1,0:T(8,128)(2,1)S(1)}, bf16[272,768]{1,0:T(8,128)(2,1)}, u32[]{:S(2)}, u32[]{:S(2)}) %collective-permute-start.6) | collective-permute-done | bytes 417824 | tf_op jit(solution)/shard_map/ppermute | solution.py:32
  79.3 10.6 %first_pass.1 = (f32[8,512,512]{2,1,0:T(8,128)S(1)}, f32[8,1,512]{2,1,0:T(1,128)S(1)}, f32[8,128]{1,0:T(8,128)S(1)}) custom-call(bf16[4,136,768]{2,1,0:T(8,128)(2,1)} %bitcast.3.refs_0_, bf16[4,136,768]{2,1,0:T(8,128)(2,1)} %bitcast.4.refs_1_, bf16[4,136,768]{2,1,0:T(8,128)(2,1)} %bitcast.75, bf16[2,136,768]{2,1,0:T(8,128)(2,1)} %bitcast.6.refs_3_, ...), custom_call_target="tpu_custom_call" | custom-call | flops 3221225472 | bytes 16777216 | tf_op jit(solution)/shard_map/first_pass/pallas_call | solution.py:265
  89.9 3.3 %copy-done.1 = f32[8,512,512]{2,1,0:T(8,128)} copy-done((f32[8,512,512]{2,1,0:T(8,128)}, f32[8,512,512]{2,1,0:T(8,128)S(1)}, u32[]{:S(2)}) %copy-start.1) | copy-done | bytes 8388632
  93.8 6.2 %all-to-all-start.2 = ((f32[8,8,128]{2,1,0:T(8,128)}), f32[8,8,128]{2,1,0:T(8,128)S(1)}, u32[]{:S(2)}, u32[]{:S(2)}) async-start(f32[8,8,128]{2,1,0:T(8,128)} %broadcast_in_dim.9), calls=%async_computation.2 | async-start | bytes 65536 | tf_op jit(solution)/shard_map/all_to_all | solution.py:412
  100.7 7.8 %positive_hits.1 = (bf16[8,512,512]{2,1,0:T(8,128)(2,1)}, bf16[768,512]{1,0:T(8,128)(2,1)}) custom-call(s32[33]{0:T(128)} %pad_add_fusion.base_ref, s32[4,512]{1,0:T(4,128)} %dynamic-slice_bitcast_fusion.pos_ref, bf16[1024,768]{1,0:T(8,128)(2,1)} %docs_ref.1), custom_call_target="tpu_custom_call" | custom-call | flops 33554432 | bytes 4194304 | tf_op jit(solution)/shard_map/positive_hits/pallas_call | solution.py:308
  108.5 3.4 %copy-done.2 = f32[8,512,512]{2,1,0:T(8,128)S(1)} copy-done((f32[8,512,512]{2,1,0:T(8,128)S(1)}, f32[8,512,512]{2,1,0:T(8,128)}, u32[]{:S(2)}) %copy-start.2) | copy-done | bytes 8388632
  114.1 10.1 %second_pass.1 = (bf16[3,512,512]{2,1,0:T(8,128)(2,1)}, bf16[1,512,512]{2,1,0:T(8,128)(2,1)}, bf16[3,512,512]{2,1,0:T(8,128)(2,1)}, bf16[1,512,512]{2,1,0:T(8,128)(2,1)}, bf16[512,768]{1,0:T(8,128)(2,1)}) custom-call(bf16[4,136,768]{2,1,0:T(8,128)(2,1)} %bitcast.3.refs_0_, bf16[4,136,768]{2,1,0:T(8,128)(2,1)} %bitcast.4.refs_1_, ...), custom_call_target="tpu_custom_call" | custom-call | flops 3221225472 | bytes 20971520 | tf_op jit(solution)/shard_map/second_pass/pallas_call | solution.py:370
  124.2 4.4 %convolution_convert_fusion = bf16[1536,768]{1,0:T(8,128)(2,1)} fusion(bf16[1536,512]{1,0:T(8,128)(2,1)} %bitcast.82, bf16[512,768]{1,0:T(8,128)(2,1)} %bitcast.16.refs_10_), kind=kOutput, calls=%fused_computation.1 | convolution fusion | flops 1209139200 | bytes 4718592 | tf_op jit(solution)/shard_map/dot_general | solution.py:492
  128.7 7.3 %all-to-all-start.3 = ((bf16[8,64,768]{2,1,0:T(8,128)(2,1)}), bf16[8,64,768]{2,1,0:T(8,128)(2,1)S(1)}, u32[]{:S(2)}, u32[]{:S(2)}) async-start(bf16[8,64,768]{2,1,0:T(8,128)(2,1)} %bitcast.27), calls=%async_computation.3 | async-start | bytes 1572864 | tf_op jit(solution)/shard_map/all_to_all | solution.py:412
  144.9 14.9 %all-to-all-done.3 = bf16[8,64,768]{2,1,0:T(8,128)(2,1)S(1)} async-done(((bf16[8,64,768]{2,1,0:T(8,128)(2,1)}), bf16[8,64,768]{2,1,0:T(8,128)(2,1)S(1)}, u32[]{:S(2)}, u32[]{:S(2)}) %all-to-all-start.3) | async-done | bytes 786464 | tf_op jit(solution)/shard_map/all_to_all | solution.py:412
  160.9 3.5 %all-to-all-start.4 = ((bf16[8,64,768]{2,1,0:T(8,128)(2,1)}), bf16[8,64,768]{2,1,0:T(8,128)(2,1)S(1)}, u32[]{:S(2)}, u32[]{:S(2)}) async-start(bf16[8,64,768]{2,1,0:T(8,128)(2,1)} %broadcast_in_dim.11), calls=%async_computation.4 | async-start | bytes 1572864 | tf_op jit(solution)/shard_map/all_to_all | solution.py:412
  164.4 3.8 %add_convert_fusion = bf16[1536,768]{1,0:T(8,128)(2,1)S(1)} fusion(bf16[1536,768]{1,0:T(8,128)(2,1)} %collective-permute-done.15, bf16[1536,512]{1,0:T(8,128)(2,1)} %bitcast.81, bf16[512,768]{1,0:T(8,128)(2,1)} %bitcast.16.refs_10_), kind=kOutput, calls=%fused_computation | convolution fusion | flops 1211498496 | bytes 7077888 | tf_op jit(solution)/shard_map/dot_general | solution.py:496
  174.9 6.6 %collective-permute-done.19 = bf16[256,768]{1,0:T(8,128)(2,1)S(1)} collective-permute-done((bf16[256,768]{1,0:T(8,128)(2,1)S(1)}, bf16[256,768]{1,0:T(8,128)(2,1)S(1)}, u32[]{:S(2)}, u32[]{:S(2)}) %collective-permute-start.19) | collective-permute-done | bytes 393248 | tf_op jit(solution)/shard_map/ppermute | solution.py:32
  181.5 7.3 %collective-permute-done.20 = bf16[256,768]{1,0:T(8,128)(2,1)S(1)} collective-permute-done((bf16[256,768]{1,0:T(8,128)(2,1)S(1)}, bf16[256,768]{1,0:T(8,128)(2,1)S(1)}, u32[]{:S(2)}, u32[]{:S(2)}) %collective-permute-start.20) | collective-permute-done | bytes 393248 | tf_op jit(solution)/shard_map/ppermute | solution.py:32
  201.7 7.2 %all-to-all-start.5 = ((bf16[16,48,384]{2,1,0:T(8,128)(2,1)}), bf16[16,48,384]{2,1,0:T(8,128)(2,1)S(1)}, u32[]{:S(2)}, u32[]{:S(2)}) async-start(bf16[16,48,384]{2,1,0:T(8,128)(2,1)} %add_convert_fusion.2), calls=%async_computation.5 | async-start | bytes 1179648 | tf_op jit(solution)/shard_map/all_to_all | solution.py:513
  210.5 12.1 %collective-permute-done.24 = bf16[128,768]{1,0:T(8,128)(2,1)S(1)} collective-permute-done((bf16[128,768]{1,0:T(8,128)(2,1)S(1)}, bf16[128,768]{1,0:T(8,128)(2,1)S(1)}, u32[]{:S(2)}, u32[]{:S(2)}) %collective-permute-start.24) | collective-permute-done | bytes 196640 | tf_op jit(solution)/shard_map/ppermute | solution.py:32
  (136 shorter events, 64.2 us)
Async XLA Ops:
  1.7 8.9 %collective-permute-start.13 = (bf16[192,768]{1,0:T(8,128)(2,1)S(1)}, bf16[192,768]{1,0:T(8,128)(2,1)S(1)}, u32[]{:S(2)}, u32[]{:S(2)}) collective-permute-start(bf16[192,768]{1,0:T(8,128)(2,1)S(1)} %bitcast_select_fusion.2), channel_id=1, source_target_pairs={{0,1},{1,0},{2,3},{3,2},{4,5},{5,4},{6,7},{7,6},{8,9},{9,8},{10,11... | collective-permute-start | bytes 884744 | tf_op jit(solution)/shard_map/ppermute | solution.py:32
  17.2 32.3 %all-to-all-start = ((bf16[8,64,768]{2,1,0:T(8,128)(2,1)}), bf16[8,64,768]{2,1,0:T(8,128)(2,1)S(1)}, u32[]{:S(2)}, u32[]{:S(2)}) async-start(bf16[8,64,768]{2,1,0:T(8,128)(2,1)} %bitcast.14), calls=%async_computation | async-start | bytes 1572864 | tf_op jit(solution)/shard_map/all_to_all | solution.py:412
  34.2 10.3 %collective-permute-start.3 = (bf16[72,768]{1,0:T(8,128)(2,1)S(1)}, bf16[72,768]{1,0:T(8,128)(2,1)S(1)}, u32[]{:S(2)}, u32[]{:S(2)}) collective-permute-start(bf16[72,768]{1,0:T(8,128)(2,1)S(1)} %slice.255), channel_id=1, source_target_pairs={{0,129},{1,0},{128,1},{129,128},{2,131},{3,2},{130,3},{131,130},{4... | collective-permute-start | bytes 331784 | tf_op jit(solution)/shard_map/ppermute | solution.py:32
  45.2 18.9 %collective-permute-start.5 = (bf16[544,768]{1,0:T(8,128)(2,1)}, bf16[544,768]{1,0:T(8,128)(2,1)S(1)}, u32[]{:S(2)}, u32[]{:S(2)}) collective-permute-start(bf16[544,768]{1,0:T(8,128)(2,1)} %constant_dynamic-update-slice_fusion), channel_id=1, source_target_pairs={{0,96},{32,0},{64,32},{96,64},{1,97},{33,1},{65,33},{97,65},{2,98}... | collective-permute-start | bytes 2506760 | tf_op jit(solution)/shard_map/ppermute | solution.py:32
  45.8 19.8 %collective-permute-start.4 = (bf16[544,768]{1,0:T(8,128)(2,1)}, bf16[544,768]{1,0:T(8,128)(2,1)}, u32[]{:S(2)}, u32[]{:S(2)}) collective-permute-start(bf16[544,768]{1,0:T(8,128)(2,1)} %constant_dynamic-update-slice_fusion), channel_id=1, source_target_pairs={{0,32},{32,64},{64,96},{96,0},{1,33},{33,65},{65,97},{97,1},{2,34}... | collective-permute-start | bytes 2506760 | tf_op jit(solution)/shard_map/ppermute | solution.py:32
  51.5 27.8 %all-to-all-start.1 = ((bf16[8,64,768]{2,1,0:T(8,128)(2,1)}), bf16[8,64,768]{2,1,0:T(8,128)(2,1)}, u32[]{:S(2)}, u32[]{:S(2)}) async-start(bf16[8,64,768]{2,1,0:T(8,128)(2,1)} %broadcast_in_dim.8), calls=%async_computation.1 | async-start | bytes 1572864 | tf_op jit(solution)/shard_map/all_to_all | solution.py:412
  56.2 21.4 %collective-permute-start.8 = (bf16[544,768]{1,0:T(8,128)(2,1)}, bf16[544,768]{1,0:T(8,128)(2,1)S(1)}, u32[]{:S(2)}, u32[]{:S(2)}) collective-permute-start(bf16[544,768]{1,0:T(8,128)(2,1)} %constant_dynamic-update-slice_fusion), channel_id=1, source_target_pairs={{0,16},{16,0},{1,17},{17,1},{2,18},{18,2},{3,19},{19,3},{4,20},{20... | collective-permute-start | bytes 2506760 | tf_op jit(solution)/shard_map/ppermute | solution.py:32
  64.2 9.1 %collective-permute-start.7 = (bf16[272,768]{1,0:T(8,128)(2,1)S(1)}, bf16[272,768]{1,0:T(8,128)(2,1)S(1)}, u32[]{:S(2)}, u32[]{:S(2)}) collective-permute-start(bf16[272,768]{1,0:T(8,128)(2,1)S(1)} %slice.257), channel_id=1, source_target_pairs={{0,96},{32,0},{64,32},{96,64},{1,97},{33,1},{65,33},{97,65},{2,98}... | collective-permute-start | bytes 1253384 | tf_op jit(solution)/shard_map/ppermute | solution.py:32
  66.6 10.3 %collective-permute-start.6 = (bf16[272,768]{1,0:T(8,128)(2,1)S(1)}, bf16[272,768]{1,0:T(8,128)(2,1)}, u32[]{:S(2)}, u32[]{:S(2)}) collective-permute-start(bf16[272,768]{1,0:T(8,128)(2,1)S(1)} %slice.256), channel_id=1, source_target_pairs={{0,32},{32,64},{64,96},{96,0},{1,33},{33,65},{65,97},{97,1},{2,34}... | collective-permute-start | bytes 1253384 | tf_op jit(solution)/shard_map/ppermute | solution.py:32
  67.4 10.2 %collective-permute-start.10 = (bf16[544,768]{1,0:T(8,128)(2,1)S(1)}, bf16[544,768]{1,0:T(8,128)(2,1)}, u32[]{:S(2)}, u32[]{:S(2)}) collective-permute-start(bf16[544,768]{1,0:T(8,128)(2,1)S(1)} %collective-permute-done.5), channel_id=1, source_target_pairs={{0,16},{16,0},{1,17},{17,1},{2,18},{18,2},{3,19},{19,3},{4,20},{20... | collective-permute-start | bytes 2506760 | tf_op jit(solution)/shard_map/ppermute | solution.py:32
  67.4 11.6 %collective-permute-start.9 = (bf16[544,768]{1,0:T(8,128)(2,1)}, bf16[544,768]{1,0:T(8,128)(2,1)}, u32[]{:S(2)}, u32[]{:S(2)}) collective-permute-start(bf16[544,768]{1,0:T(8,128)(2,1)} %collective-permute-done.4), channel_id=1, source_target_pairs={{0,16},{16,0},{1,17},{17,1},{2,18},{18,2},{3,19},{19,3},{4,20},{20... | collective-permute-start | bytes 2506760 | tf_op jit(solution)/shard_map/ppermute | solution.py:32
  93.8 14.6 %all-to-all-start.2 = ((f32[8,8,128]{2,1,0:T(8,128)}), f32[8,8,128]{2,1,0:T(8,128)S(1)}, u32[]{:S(2)}, u32[]{:S(2)}) async-start(f32[8,8,128]{2,1,0:T(8,128)} %broadcast_in_dim.9), calls=%async_computation.2 | async-start | bytes 65536 | tf_op jit(solution)/shard_map/all_to_all | solution.py:412
  128.7 35.8 %collective-permute-start.15 = (bf16[1536,768]{1,0:T(8,128)(2,1)}, bf16[1536,768]{1,0:T(8,128)(2,1)}, u32[]{:S(2)}, u32[]{:S(2)}) collective-permute-start(bf16[1536,768]{1,0:T(8,128)(2,1)} %convolution_convert_fusion), channel_id=1, source_target_pairs={{0,16},{16,0},{1,17},{17,1},{2,18},{18,2},{3,19},{19,3},{4,20},{20... | collective-permute-start | bytes 7077896 | tf_op jit(solution)/shard_map/ppermute | solution.py:32
  128.7 31.2 %all-to-all-start.3 = ((bf16[8,64,768]{2,1,0:T(8,128)(2,1)}), bf16[8,64,768]{2,1,0:T(8,128)(2,1)S(1)}, u32[]{:S(2)}, u32[]{:S(2)}) async-start(bf16[8,64,768]{2,1,0:T(8,128)(2,1)} %bitcast.27), calls=%async_computation.3 | async-start | bytes 1572864 | tf_op jit(solution)/shard_map/all_to_all | solution.py:412
  141.9 26.4 %collective-permute-start.18 = (bf16[256,768]{1,0:T(8,128)(2,1)S(1)}, bf16[256,768]{1,0:T(8,128)(2,1)S(1)}, u32[]{:S(2)}, u32[]{:S(2)}) collective-permute-start(bf16[256,768]{1,0:T(8,128)(2,1)S(1)} %get-tuple-element.45), channel_id=1, source_target_pairs={{0,96},{32,0},{64,32},{96,64},{1,97},{33,1},{65,33},{97,65},{2,98}... | collective-permute-start | bytes 1179656 | tf_op jit(solution)/shard_map/ppermute | solution.py:32
  144.9 23.3 %collective-permute-start.17 = (bf16[256,768]{1,0:T(8,128)(2,1)S(1)}, bf16[256,768]{1,0:T(8,128)(2,1)S(1)}, u32[]{:S(2)}, u32[]{:S(2)}) collective-permute-start(bf16[256,768]{1,0:T(8,128)(2,1)S(1)} %get-tuple-element.46), channel_id=1, source_target_pairs={{0,32},{32,64},{64,96},{96,0},{1,33},{33,65},{65,97},{97,1},{2,34}... | collective-permute-start | bytes 1179656 | tf_op jit(solution)/shard_map/ppermute | solution.py:32
  160.9 30.3 %all-to-all-start.4 = ((bf16[8,64,768]{2,1,0:T(8,128)(2,1)}), bf16[8,64,768]{2,1,0:T(8,128)(2,1)S(1)}, u32[]{:S(2)}, u32[]{:S(2)}) async-start(bf16[8,64,768]{2,1,0:T(8,128)(2,1)} %broadcast_in_dim.11), calls=%async_computation.4 | async-start | bytes 1572864 | tf_op jit(solution)/shard_map/all_to_all | solution.py:412
  168.5 13.0 %collective-permute-start.19 = (bf16[256,768]{1,0:T(8,128)(2,1)S(1)}, bf16[256,768]{1,0:T(8,128)(2,1)S(1)}, u32[]{:S(2)}, u32[]{:S(2)}) collective-permute-start(bf16[256,768]{1,0:T(8,128)(2,1)S(1)} %get-tuple-element.25), channel_id=1, source_target_pairs={{0,32},{32,64},{64,96},{96,0},{1,33},{33,65},{65,97},{97,1},{2,34}... | collective-permute-start | bytes 1179656 | tf_op jit(solution)/shard_map/ppermute | solution.py:32
  168.6 12.9 %collective-permute-start.22 = (bf16[256,768]{1,0:T(8,128)(2,1)S(1)}, bf16[256,768]{1,0:T(8,128)(2,1)S(1)}, u32[]{:S(2)}, u32[]{:S(2)}) collective-permute-start(bf16[256,768]{1,0:T(8,128)(2,1)S(1)} %get-tuple-element.26), channel_id=1, source_target_pairs={{0,96},{32,0},{64,32},{96,64},{1,97},{33,1},{65,33},{97,65},{2,98}... | collective-permute-start | bytes 1179656 | tf_op jit(solution)/shard_map/ppermute | solution.py:32
  171.9 16.9 %collective-permute-start.20 = (bf16[256,768]{1,0:T(8,128)(2,1)S(1)}, bf16[256,768]{1,0:T(8,128)(2,1)S(1)}, u32[]{:S(2)}, u32[]{:S(2)}) collective-permute-start(bf16[256,768]{1,0:T(8,128)(2,1)S(1)} %get-tuple-element.37), channel_id=1, source_target_pairs={{0,96},{32,0},{64,32},{96,64},{1,97},{33,1},{65,33},{97,65},{2,98}... | collective-permute-start | bytes 1179656 | tf_op jit(solution)/shard_map/ppermute | solution.py:32
  174.9 14.4 %collective-permute-start.21 = (bf16[256,768]{1,0:T(8,128)(2,1)S(1)}, bf16[256,768]{1,0:T(8,128)(2,1)S(1)}, u32[]{:S(2)}, u32[]{:S(2)}) collective-permute-start(bf16[256,768]{1,0:T(8,128)(2,1)S(1)} %get-tuple-element.38), channel_id=1, source_target_pairs={{0,32},{32,64},{64,96},{96,0},{1,33},{33,65},{65,97},{97,1},{2,34}... | collective-permute-start | bytes 1179656 | tf_op jit(solution)/shard_map/ppermute | solution.py:32
  196.8 13.7 %collective-permute-start.26 = (bf16[128,768]{1,0:T(8,128)(2,1)S(1)}, bf16[128,768]{1,0:T(8,128)(2,1)S(1)}, u32[]{:S(2)}, u32[]{:S(2)}) collective-permute-start(bf16[128,768]{1,0:T(8,128)(2,1)S(1)} %pad_maximum_fusion.3), channel_id=1, source_target_pairs={{0,129},{1,0},{128,1},{129,128},{2,131},{3,2},{130,3},{131,130},{4... | collective-permute-start | bytes 589832 | tf_op jit(solution)/shard_map/ppermute | solution.py:32
  201.7 21.6 %all-to-all-start.5 = ((bf16[16,48,384]{2,1,0:T(8,128)(2,1)}), bf16[16,48,384]{2,1,0:T(8,128)(2,1)S(1)}, u32[]{:S(2)}, u32[]{:S(2)}) async-start(bf16[16,48,384]{2,1,0:T(8,128)(2,1)} %add_convert_fusion.2), calls=%async_computation.5 | async-start | bytes 1179648 | tf_op jit(solution)/shard_map/all_to_all | solution.py:513
  209.0 13.6 %collective-permute-start.24 = (bf16[128,768]{1,0:T(8,128)(2,1)S(1)}, bf16[128,768]{1,0:T(8,128)(2,1)S(1)}, u32[]{:S(2)}, u32[]{:S(2)}) collective-permute-start(bf16[128,768]{1,0:T(8,128)(2,1)S(1)} %pad_maximum_fusion.2), channel_id=1, source_target_pairs={{0,1},{1,128},{128,129},{129,0},{2,3},{3,130},{130,131},{131,2},{4... | collective-permute-start | bytes 589832 | tf_op jit(solution)/shard_map/ppermute | solution.py:32
  (30 other events, 273.6 us)
